TPU v7x, 32 devices: a whole 2x2x4 slice. The times are simulated.
32 devices in a mesh: comp: 2 (over x), row: 4 (over y, core), col: 4 (over z).
Axes of the slice: x: 2, y: 2, z: 4, core: 2. Of those that a mesh axis runs over, the one named last changes fastest.
Arguments:
- model_state: float32 [2, 1280, 32, 512], P('comp', 'row', None, 'col'), may hold values from -6 to 6
- legendre: bfloat16 [32, 1280, 1280], P('row'), may hold values from -0.15625 to 0.15625
- gauss_weight: float32 [1280], P('row'), may hold values from 0.5 to 1.5
- mixing: float32 [32, 32], replicated, may hold values from -1 to 1
- surface: float32 [2, 1280, 512], P('comp', 'row', 'col'), may hold values from -6 to 6
- sea_count: int32 [2, 1280, 4], P('comp', 'row', 'col'), may hold values from 0 to 128, as said below
- remap_source: int32 [2, 1280, 512], P('comp', 'row', 'col'), may hold values from 0 to 40959
Outputs:
- new_state: float32 [2, 1280, 32, 512], P('comp', 'row', None, 'col')
- new_surface: float32 [2, 1280, 512], P('comp', 'row', 'col')
Inputs may be any that keep to these rules, and one draw needn't show every extreme that they name: `sea_count`: the sea cells of a tile row are its first ones, of 128. `remap_source`: an entry counts row-major within a tile of 320 rows and 128 columns.
All inputs are finite; a program needn't handle non-finite values.
Results may differ from a plain program's by a relative error of at most 0.0043.
Values may be sent and summed in bfloat16 or wider, within the bound.
No kernel may reach another device: no remote copies, remote signals or barrier semaphores. Data moves between devices by JAX's collectives and lax.ppermute only.
A program may use at most 128 MiB of HBM per device.

v0:
```python
import jax
import jax.numpy as jnp
from jax import lax
from jax.sharding import PartitionSpec as P

diffusion_rate = 0.2


def padded_2(block, sides, width):
    for axis, dim in sides:
        count = lax.axis_size(axis)
        forward = [(i, i + 1) for i in range(count - 1)]
        backward = [(target, source) for source, target in forward]
        low = lax.ppermute(
            lax.slice_in_dim(block, block.shape[dim] - width, None, axis=dim), axis, forward
        )
        high = lax.ppermute(lax.slice_in_dim(block, 0, width, axis=dim), axis, backward)
        block = jnp.concatenate([low, block, high], axis=dim)
    return block


def swapped(block, axis, stride):
    count = lax.axis_size(axis)
    route = []
    for low in range(count):
        high = low | 1 << stride
        if high != low and high < count:
            route += [(low, high), (high, low)]
    return lax.ppermute(block, axis, route)


def damping_table(row_index, wave_dev, nwave_count):
    global_wave = row_index * wave_dev + jnp.arange(wave_dev, dtype=jnp.int32)
    total_wave = (global_wave[:, None] + jnp.arange(nwave_count, dtype=jnp.int32)[None, :]).astype(
        jnp.float32
    )
    wave_ratio = total_wave * (total_wave + 1.0) / (1279.0 * 1280.0)
    return 1.0 / (1.0 + 20.0 * wave_ratio * wave_ratio)


def laplace_inner(padded):
    centre = padded[1:-1, :, 1:-1]
    return (
        padded[2:, :, 1:-1]
        + padded[:-2, :, 1:-1]
        + padded[1:-1, :, 2:]
        + padded[1:-1, :, :-2]
        - 4.0 * centre
    )


def atmosphere(fields, gauss_weight, legendre):
    weighted = (gauss_weight[None, :, None] * jnp.transpose(fields, (1, 0, 2))).astype(jnp.bfloat16)
    damping = damping_table(lax.axis_index("row"), legendre.shape[0], legendre.shape[2])
    spectral = jnp.einsum(
        "wln,wlc->wnc",
        legendre,
        lax.all_to_all(weighted, "row", split_axis=0, concat_axis=1, tiled=True),
        preferred_element_type=jnp.float32,
    )
    filtered = (damping[:, :, None] * spectral).astype(jnp.bfloat16)
    synthesized = jnp.einsum(
        "wln,wnc->wlc", legendre, filtered, preferred_element_type=jnp.float32
    ).astype(jnp.bfloat16)
    returned = lax.all_to_all(synthesized, "row", split_axis=1, concat_axis=0, tiled=True)
    return jnp.transpose(returned, (1, 0, 2)).astype(jnp.float32)


def advance_ocean(heat_level, mixing, water_mask):
    water_column = water_mask[:, None, :]
    blended_field = heat_level + water_column * jnp.einsum(
        "do,eot->edt", mixing, heat_level, precision=lax.Precision.HIGHEST
    )
    current = blended_field
    for sweep_index in range(2):
        padded = padded_2(water_column * current, (("row", 0), ("col", 2)), 1)
        current = current + diffusion_rate * water_column * laplace_inner(padded)
    return current


def shards(model_state, legendre, gauss_weight, mixing, surface, sea_count, remap_source):
    fields = model_state[0]
    counts = sea_count[0, :, 0]
    water_mask = (jnp.arange(fields.shape[2], dtype=jnp.int32)[None, :] < counts[:, None]).astype(
        jnp.float32
    )
    own_surface = surface[0]
    group_index = lax.axis_index("comp")
    air_result = atmosphere(fields, gauss_weight, legendre)
    sea_result = advance_ocean(fields, mixing, water_mask)
    result = jnp.where(group_index == 0, air_result, sea_result)
    partner = swapped(own_surface, "comp", 0)
    pulled = jnp.take(partner.reshape(-1), remap_source[0].reshape(-1)).reshape(own_surface.shape)
    surface_gap = water_mask * (pulled - own_surface)
    slot_rate = jnp.where(group_index == 0, 0.5, 0.25).astype(jnp.float32)
    ocean_share = jnp.where(group_index == 0, 0.0, 0.3).astype(jnp.float32)
    new_surface = own_surface + slot_rate * surface_gap
    result = result.at[:, 0, :].add(ocean_share * surface_gap)
    return (result[None], new_surface[None])


def solution(mesh):
    in_specs = (
        P("comp", "row", None, "col"),
        P("row", None, None),
        P("row"),
        P(),
        P("comp", "row", "col"),
        P("comp", "row", "col"),
        P("comp", "row", "col"),
    )
    out_specs = (P("comp", "row", None, "col"), P("comp", "row", "col"))
    return jax.shard_map(shards, mesh=mesh, in_specs=in_specs, out_specs=out_specs, check_vma=False)
```

profile of v0, /device:TPU:7, one launch (start us, length us, event | category | flops | bytes accessed | tf_op | source)
XLA Modules:
  0.0 415.6 jit_solution(12864694766231401023)
XLA Ops:
  1.5 11.6 %broadcast_multiply_fusion.1 = (f32[320,32,128]{2,1,0:T(8,128)S(1)}, f32[320,32,128]{2,1,0:T(8,128)}) fusion(f32[320,128]{1,0:T(8,128)S(1)} %fusion.29, f32[32,32]{1,0:T(8,128)S(1)} %copy-done, f32[1,320,32,128]{3,2,1,0:T(8,128)} %param.9), kind=kOutput, calls=%fused_computation.43 | convolution fusion | flops 507248640 | bytes 15896576 | tf_op jit(solution)/shard_map/do,eot->edt/dot_general | solution.py:71
  22.4 4.9 %all-to-all-start = ((bf16[32,320,128]{2,1,0:T(8,128)(2,1)}), bf16[32,320,128]{2,1,0:T(8,128)(2,1)S(1)}, u32[]{:S(2)}, u32[]{:S(2)}) async-start(bf16[32,320,128]{2,1,0:T(8,128)(2,1)} %copy.29), calls=%async_computation | async-start | bytes 5242880 | tf_op jit(solution)/shard_map/all_to_all | solution.py:58
  28.2 3.1 pad_maximum_fusion
  31.3 5.8 %fusion.34 = (f32[322,32,1]{2,1,0:T(8,128)}, f32[322,32,1]{2,1,0:T(8,128)}) fusion(f32[322,32,128]{2,1,0:T(8,128)S(1)} %pad_maximum_fusion), kind=kLoop, calls=%fused_computation.69 | loop fusion | bytes 164864 | tf_op jit(solution)/shard_map/slice | solution.py:17
  37.1 4.3 %copy.35 = f32[322,32,1]{0,1,2:T(8,128)S(1)} copy(f32[322,32,1]{2,1,0:T(8,128)} %get-tuple-element.18) | data formatting | bytes 82432 | tf_op jit(solution)/shard_map/slice | solution.py:17
  42.9 4.3 %copy.37 = f32[322,32,1]{0,1,2:T(8,128)S(1)} copy(f32[322,32,1]{2,1,0:T(8,128)} %get-tuple-element.19) | data formatting | bytes 82432 | tf_op jit(solution)/shard_map/slice | solution.py:15
  47.1 4.1 collective-permute-start.3
  51.2 4.6 %copy.36 = f32[322,32,1]{2,1,0:T(8,128)} copy(f32[322,32,1]{0,1,2:T(8,128)S(1)} %collective-permute-done.2) | data formatting | bytes 82432 | tf_op jit(solution)/shard_map/ppermute | solution.py:17
  55.8 4.5 %copy.38 = f32[322,32,1]{2,1,0:T(8,128)} copy(f32[322,32,1]{0,1,2:T(8,128)S(1)} %collective-permute-done.3) | data formatting | bytes 82432 | tf_op jit(solution)/shard_map/ppermute | solution.py:14
  60.3 20.8 %broadcast_multiply_fusion = (f32[320,32,128]{2,1,0:T(8,128)S(1)}, f32[320,32,128]{2,1,0:T(8,128)}) fusion(f32[320,128]{1,0:T(8,128)S(1)} %fusion.29, f32[320,32,128]{2,1,0:T(8,128)} %get-tuple-element.25, f32[320,32,128]{2,1,0:T(8,128)} %copy-done.2, f32[1,32,128]{2,1,0:T(8,128)S(1)} %collective-permute-done, f32[1,32,128]{2,1,0:T(8,128)S(1)} %collective-permute-done.1, ...), kind=kLoop, calls=%fused_computation.42 | loop fusion | flops 20971520 | bytes 21414400 | tf_op jit(solution)/shard_map/mul | solution.py:76
  81.1 2.9 collective-permute-start.4
  87.1 2.9 pad_maximum_fusion.1
  93.5 22.1 %fusion.16 = bf16[8,1280,128]{1,2,0:T(8,128)(2,1)} fusion(bf16[8,1280,1280]{2,1,0:T(8,128)(2,1)} %param.10, bf16[8,1280,128]{2,1,0:T(8,128)(2,1)S(1)} %bitcast.66, f32[8,1280]{1,0:T(8,128)S(1)} %add_divide_fusion), kind=kOutput, calls=%fused_computation.40 | convolution fusion | flops 6714818560 | bytes 31498240 | tf_op jit(solution)/shard_map/wln,wnc->wlc/dot_general | solution.py:62
  115.6 4.8 %copy.32 = bf16[8,1280,128]{2,0,1:T(8,128)(2,1)} copy(bf16[8,1280,128]{1,2,0:T(8,128)(2,1)} %fusion.16) | data formatting | bytes 5242880 | tf_op jit(solution)/shard_map/convert_element_type | solution.py:64
  120.3 5.3 %all-to-all-start.1 = ((bf16[8,1280,128]{2,0,1:T(8,128)(2,1)}), bf16[8,1280,128]{2,0,1:T(8,128)(2,1)S(1)}, u32[]{:S(2)}, u32[]{:S(2)}) async-start(bf16[8,1280,128]{2,0,1:T(8,128)(2,1)} %copy.32), calls=%async_computation.1 | async-start | bytes 5242880 | tf_op jit(solution)/shard_map/all_to_all | solution.py:65
  125.6 9.5 %fusion.33 = (f32[322,32,1]{2,1,0:T(8,128)}, f32[322,32,1]{2,1,0:T(8,128)}) fusion(f32[322,32,128]{2,1,0:T(8,128)} %pad_maximum_fusion.1), kind=kLoop, calls=%fused_computation.68 | loop fusion | bytes 164864 | tf_op jit(solution)/shard_map/slice | solution.py:17
  135.1 4.3 %copy.39 = f32[322,32,1]{0,1,2:T(8,128)S(1)} copy(f32[322,32,1]{2,1,0:T(8,128)} %get-tuple-element.16) | data formatting | bytes 82432 | tf_op jit(solution)/shard_map/slice | solution.py:17
  140.7 4.9 %copy.41 = f32[322,32,1]{0,1,2:T(8,128)} copy(f32[322,32,1]{2,1,0:T(8,128)} %get-tuple-element.17) | data formatting | bytes 82432 | tf_op jit(solution)/shard_map/slice | solution.py:15
  145.6 4.6 %collective-permute-start.7 = (f32[322,32,1]{0,1,2:T(8,128)}, f32[322,32,1]{0,1,2:T(8,128)}, u32[]{:S(2)}, u32[]{:S(2)}) collective-permute-start(f32[322,32,1]{0,1,2:T(8,128)} %copy.41), channel_id=1, source_target_pairs={{0,1},{1,2},{2,3},{4,5},{5,6},{6,7},{8,9},{9,10},{10,11},{12,13},{... | collective-permute-start | bytes 123656 | tf_op jit(solution)/shard_map/ppermute | solution.py:14
  150.3 5.2 %copy.40 = f32[322,32,1]{2,1,0:T(8,128)} copy(f32[322,32,1]{0,1,2:T(8,128)} %collective-permute-done.6) | data formatting | bytes 82432 | tf_op jit(solution)/shard_map/ppermute | solution.py:17
  155.5 5.3 %copy.42 = f32[322,32,1]{2,1,0:T(8,128)} copy(f32[322,32,1]{0,1,2:T(8,128)} %collective-permute-done.7) | data formatting | bytes 82432 | tf_op jit(solution)/shard_map/ppermute | solution.py:14
  160.7 225.5 %gather_fusion = f32[40960]{0:T(1024)S(1)} fusion(f32[40960]{0:T(1024)S(1)} %bitcast.61, s32[40960]{0:T(1024)S(1)} %broadcast_clamp_fusion), kind=kCustom, calls=%fused_computation | custom fusion | bytes 491520 | tf_op jit(solution)/shard_map/jit(_take)/gather | solution.py:93
  392.1 15.6 %fusion.4 = f32[320,32,128]{2,1,0:T(8,128)} fusion(f32[320,32,128]{2,1,0:T(8,128)} %get-tuple-element.15, f32[322,32,1]{2,1,0:T(8,128)} %copy.42, f32[1,32,128]{2,1,0:T(8,128)S(1)} %collective-permute-done.4, f32[320,32,128]{2,1,0:T(8,128)S(1)} %bitcast.63, f32[1,32,128]{2,1,0:T(8,128)S(1)} %collective-permute-done.5, f32[322,32,1]{2,1,0:T(8,128)S(1)} %copy-done.4, ...), kind=kLoop, calls=%fused_computation.8 | loop fusion | flops 20971520 | bytes 21250560 | tf_op jit(solution)/shard_map/jit(_where)/select_n | solution.py:91
  409.9 5.7 %scatter-add.4 = f32[1,320,32,128]{3,2,1,0:T(8,128)} dynamic-update-slice(f32[1,320,32,128]{3,2,1,0:T(8,128)} %bitcast.69, f32[1,320,1,128]{3,2,1,0:T(1,128)S(1)} %fusion.30, s32[]{:T(128)} %constant.63.clone.1, s32[]{:T(128)} %constant.63.clone.1, s32[]{:T(128)} %constant.63.clone.1, s32[]{:T(128)} %constant.63.clone.1) | dynamic-update-slice | bytes 327684 | tf_op jit(solution)/shard_map/scatter-add | solution.py:98
  (61 shorter events, 28.3 us)
Async XLA Ops:
  0.6 0.8 copy-start
  1.4 17.9 %slice-start.2 = ((s8[5242880]{0:T(1024)(128)(4,1)}), s8[4194304]{0:T(1024)(128)(4,1)S(1)}, s32[]{:S(2)}) async-start(s8[5242880]{0:T(1024)(128)(4,1)} %bitcast.64), calls=%async_computation.4 | async-start | bytes 8388608
  1.5 17.8 %slice-start.3 = ((s8[5242880]{0:T(1024)(128)(4,1)}), s8[1048576]{0:T(1024)(128)(4,1)S(1)}, s32[]{:S(2)}) async-start(s8[5242880]{0:T(1024)(128)(4,1)} %bitcast.64), calls=%async_computation.5 | async-start | bytes 2097152
  1.5 17.8 %copy-start.8 = (f32[320]{0:T(512)S(1)}, f32[320]{0:T(512)}, u32[]{:S(2)}) copy-start(f32[320]{0:T(512)} %param.11) | copy-start | bytes 3844
  13.1 2.3 copy-start.2
  15.4 12.8 %collective-permute-start = (f32[1,32,128]{2,1,0:T(8,128)S(1)}, f32[1,32,128]{2,1,0:T(8,128)S(1)}, u32[]{:S(2)}, u32[]{:S(2)}) collective-permute-start(f32[1,32,128]{2,1,0:T(8,128)S(1)} %get-tuple-element.23), channel_id=1, source_target_pairs={{4,0},{8,4},{12,8},{5,1},{9,5},{13,9},{6,2},{10,6},{14,10},{7,3},{... | collective-permute-start | bytes 49160 | tf_op jit(solution)/shard_map/ppermute | solution.py:17
  18.0 10.2 %collective-permute-start.1 = (f32[1,32,128]{2,1,0:T(8,128)S(1)}, f32[1,32,128]{2,1,0:T(8,128)S(1)}, u32[]{:S(2)}, u32[]{:S(2)}) collective-permute-start(f32[1,32,128]{2,1,0:T(8,128)S(1)} %get-tuple-element.22), channel_id=1, source_target_pairs={{0,4},{4,8},{8,12},{1,5},{5,9},{9,13},{2,6},{6,10},{10,14},{3,7},{... | collective-permute-start | bytes 49160 | tf_op jit(solution)/shard_map/ppermute | solution.py:14
  19.8 7.4 %copy-start.6 = (s32[1,320,128]{2,1,0:T(8,128)S(1)}, s32[1,320,128]{2,1,0:T(8,128)}, u32[]{:S(2)}) copy-start(s32[1,320,128]{2,1,0:T(8,128)} %param.15) | copy-start | bytes 491524
  22.4 67.6 %all-to-all-start = ((bf16[32,320,128]{2,1,0:T(8,128)(2,1)}), bf16[32,320,128]{2,1,0:T(8,128)(2,1)S(1)}, u32[]{:S(2)}, u32[]{:S(2)}) async-start(bf16[32,320,128]{2,1,0:T(8,128)(2,1)} %copy.29), calls=%async_computation | async-start | bytes 5242880 | tf_op jit(solution)/shard_map/all_to_all | solution.py:58
  27.2 133.5 %collective-permute-start.8 = (f32[320,128]{1,0:T(8,128)}, f32[320,128]{1,0:T(8,128)S(1)}, u32[]{:S(2)}, u32[]{:S(2)}) collective-permute-start(f32[320,128]{1,0:T(8,128)} %bitcast.14), channel_id=1, source_target_pairs={{0,16},{16,0},{1,17},{17,1},{2,18},{18,2},{3,19},{19,3},{4,20},{20... | collective-permute-start | bytes 491528 | tf_op jit(solution)/shard_map/ppermute | solution.py:29
  41.4 9.8 %collective-permute-start.2 = (f32[322,32,1]{0,1,2:T(8,128)S(1)}, f32[322,32,1]{0,1,2:T(8,128)S(1)}, u32[]{:S(2)}, u32[]{:S(2)}) collective-permute-start(f32[322,32,1]{0,1,2:T(8,128)S(1)} %copy.35), channel_id=1, source_target_pairs={{1,0},{2,1},{3,2},{5,4},{6,5},{7,6},{9,8},{10,9},{11,10},{13,12},{... | collective-permute-start | bytes 123656 | tf_op jit(solution)/shard_map/ppermute | solution.py:17
  47.1 8.7 %collective-permute-start.3 = (f32[322,32,1]{0,1,2:T(8,128)S(1)}, f32[322,32,1]{0,1,2:T(8,128)S(1)}, u32[]{:S(2)}, u32[]{:S(2)}) collective-permute-start(f32[322,32,1]{0,1,2:T(8,128)S(1)} %copy.37), channel_id=1, source_target_pairs={{0,1},{1,2},{2,3},{4,5},{5,6},{6,7},{8,9},{9,10},{10,11},{12,13},{... | collective-permute-start | bytes 123656 | tf_op jit(solution)/shard_map/ppermute | solution.py:14
  81.1 6.0 %copy-start.3 = (f32[320,32,128]{2,1,0:T(8,128)}, f32[320,32,128]{2,1,0:T(8,128)S(1)}, u32[]{:S(2)}) copy-start(f32[320,32,128]{2,1,0:T(8,128)S(1)} %get-tuple-element.14) | copy-start | bytes 15728644
  81.1 4.3 %collective-permute-start.4 = (f32[1,32,128]{2,1,0:T(8,128)S(1)}, f32[1,32,128]{2,1,0:T(8,128)S(1)}, u32[]{:S(2)}, u32[]{:S(2)}) collective-permute-start(f32[1,32,128]{2,1,0:T(8,128)S(1)} %get-tuple-element.21), channel_id=1, source_target_pairs={{4,0},{8,4},{12,8},{5,1},{9,5},{13,9},{6,2},{10,6},{14,10},{7,3},{... | collective-permute-start | bytes 49160 | tf_op jit(solution)/shard_map/ppermute | solution.py:17
  84.0 3.1 collective-permute-start.5
  90.0 1.5 copy-start.5
  120.3 267.7 %all-to-all-start.1 = ((bf16[8,1280,128]{2,0,1:T(8,128)(2,1)}), bf16[8,1280,128]{2,0,1:T(8,128)(2,1)S(1)}, u32[]{:S(2)}, u32[]{:S(2)}) async-start(bf16[8,1280,128]{2,0,1:T(8,128)(2,1)} %copy.32), calls=%async_computation.1 | async-start | bytes 5242880 | tf_op jit(solution)/shard_map/all_to_all | solution.py:65
  135.1 15.1 %copy-start.7 = (s32[40960,1]{0,1:T(1,128)S(1)}, s32[40960,1]{0,1:T(1,128)}, u32[]{:S(2)}) copy-start(s32[40960,1]{0,1:T(1,128)} %compare_select_fusion) | copy-start | bytes 491524
  139.4 10.8 %collective-permute-start.6 = (f32[322,32,1]{0,1,2:T(8,128)S(1)}, f32[322,32,1]{0,1,2:T(8,128)}, u32[]{:S(2)}, u32[]{:S(2)}) collective-permute-start(f32[322,32,1]{0,1,2:T(8,128)S(1)} %copy.39), channel_id=1, source_target_pairs={{1,0},{2,1},{3,2},{5,4},{6,5},{7,6},{9,8},{10,9},{11,10},{13,12},{... | collective-permute-start | bytes 123656 | tf_op jit(solution)/shard_map/ppermute | solution.py:17
  145.6 9.9 %collective-permute-start.7 = (f32[322,32,1]{0,1,2:T(8,128)}, f32[322,32,1]{0,1,2:T(8,128)}, u32[]{:S(2)}, u32[]{:S(2)}) collective-permute-start(f32[322,32,1]{0,1,2:T(8,128)} %copy.41), channel_id=1, source_target_pairs={{0,1},{1,2},{2,3},{4,5},{5,6},{6,7},{8,9},{9,10},{10,11},{12,13},{... | collective-permute-start | bytes 123656 | tf_op jit(solution)/shard_map/ppermute | solution.py:14
  388.0 2.2 slice-start
  388.3 3.5 copy-start.4
  388.3 3.7 slice-start.1
  392.1 23.5 %copy-start.1 = (f32[32,32]{1,0:T(8,128)S(1)}, f32[32,32]{1,0:T(8,128)}, u32[]{:S(2)}) copy-start(f32[32,32]{1,0:T(8,128)} %param.12) | copy-start | bytes 12292
where the time goes:
time: 419 us; the launch traced here: 416 us
  local copies, waits for them, and re-layouts  300 us (72%)
  other arithmetic  49.3 us (12%)
  matrix products  33.7 us (8%)
  starting transfers between devices  29.6 us (7%)
    gather x1, local copies, waits for them, and re-layouts, shards(): jnp.take(partner.reshape(-1), remap_source[0].reshape(-1))  226 us
    slice x4, local copies, waits for them, and re-layouts, padded_2(): lax.slice_in_dim(block, 0, width, axis=dim)  23.9 us
    dot_general x1, matrix products, atmosphere(): jnp.einsum('wln,wnc->wlc', legendre, filtered, preferred_element_type=jnp...  22.1 us
    mul x1, other arithmetic, advance_ocean(): padded = padded_2(water_column * current, (('row', 0), ('col', 2)), 1)  20.8 us
    select_n x1, other arithmetic, shards(): result = jnp.where(group_index == 0, air_result, sea_result)  15.6 us
    dot_general x1, matrix products, advance_ocean(): jnp.einsum('do,eot->edt', mixing, heat_level, precision=lax.Precision.HIG...  11.6 us
    ppermute x4, starting transfers between devices, padded_2(): lax.ppermute(lax.slice_in_dim(block, block.shape[dim] - width, None, axis...  11.3 us
    ppermute x2, local copies, waits for them, and re-layouts, padded_2(): lax.ppermute(lax.slice_in_dim(block, 0, width, axis=dim), axis, backward)  9.77 us
  transfers between devices with their start and end apart: 11, of which 1 were waited for; matrix products, arithmetic and copies ran while one was open for 82% of the time, Pallas kernels for 0%

commit v1 on v0

v1 whole, which is shorter than its diff:
```python
import functools

import jax
import jax.numpy as jnp
from jax import lax
from jax.experimental import pallas as pl
from jax.experimental.pallas import tpu as pltpu
from jax.sharding import PartitionSpec as P

diffusion_rate = 0.2
lanes = 128


def row_block(rows):
    return 64 if rows % 64 == 0 else rows


def lane_index(shape=(8, lanes)):
    return lax.broadcasted_iota(jnp.int32, shape, len(shape) - 1)


def cost(flops, bytes_accessed):
    return pl.CostEstimate(flops=flops, bytes_accessed=bytes_accessed, transcendentals=0)


def entry_kernel(ids, counts, field, last, gauss, mix, send, mixed, edge, *, n_row, chunks, block, groups):
    levels = field.shape[0] // block
    width = levels // n_row // chunks
    step = pl.program_id(0)
    wide = groups * levels

    @pl.when(ids[0] == 0)
    def _():
        for wave in range(levels):
            dest, local = divmod(wave, levels // n_row)
            chunk, slot = divmod(local, width)
            values = field[pl.ds(wave, block, stride=levels), :] * gauss[...]
            send[chunk][dest, slot] = values.astype(jnp.bfloat16)

    def mixed_rows(ref, start, first_row):
        heat = ref[pl.ds(start, wide), :]
        blend = jnp.dot(mix[...], heat, precision=lax.Precision.HIGHEST, preferred_element_type=jnp.float32)
        out = []
        for s in range(groups):
            sea = lane_index((levels, lanes)) < counts[first_row + s]
            part = slice(levels * s, levels * (s + 1))
            out.append((heat[part] + jnp.where(sea, blend[part], 0.0), sea))
        return out

    @pl.when(ids[0] != 0)
    def _():
        def body(g, packed):
            start = pl.multiple_of(g * wide, wide)
            for s, (value, sea) in enumerate(mixed_rows(field, start, step * block + g * groups)):
                mixed[pl.ds(pl.multiple_of(start + s * levels, levels), levels), :] = value
                packed = pack_edge(packed, jnp.where(sea, value, 0.0), g * groups + s)
            return packed

        packed = lax.fori_loop(0, block // groups, body, jnp.zeros((levels, lanes), jnp.float32))
        for c in range(edge.shape[0]):
            edge[c, 0] = packed.astype(jnp.bfloat16)

        @pl.when(step == 0)
        def _():
            total = pl.num_programs(0) * block
            top, top_sea = mixed_rows(field, 0, 0)[0]
            low, low_sea = mixed_rows(last, 0, total - groups)[-1]
            top = jnp.where(top_sea, top, 0.0).astype(jnp.bfloat16)
            low = jnp.where(low_sea, low, 0.0).astype(jnp.bfloat16)
            for dest in range(n_row):
                send[0][dest, 0, 0:levels, :] = jnp.where(dest > ids[1], low, top)


def pack_edge(packed, sea_value, y):
    lane = lane_index(packed.shape)
    shift = (2 * y + 1) % lanes
    moved = pltpu.roll(sea_value, shift, 1)
    return jnp.where((lane == 2 * y) | (lane == 2 * y + 1), moved, packed)


def sweep_kernel(ids, counts, field, above, below, halo_up, halo_down, east_in, west_in, *rest,
                 block, n_row, n_col, final):
    if final:
        gap, out = rest
    else:
        out, edge, ends = rest
    levels = field.shape[0] // block
    step = pl.program_id(0)
    steps = pl.num_programs(0)
    rows = steps * block

    @pl.when(ids[0] != 0)
    def _():
        shape = (levels, lanes)
        lane = lane_index(shape)
        first = lane == 0
        final_lane = lane == lanes - 1

        def sea_of(y):
            return lane < counts[jnp.clip(y, 0, rows - 1)]

        west = jnp.where(ids[2] > 0, west_in[0, 0].astype(jnp.float32), 0.0)
        east = jnp.where(ids[2] < n_col - 1, east_in[0, 0].astype(jnp.float32), 0.0)
        sides = jnp.where(lane % 2 == 0, pltpu.roll(east, lanes - 1, 1), pltpu.roll(west, 1, 1))
        base = step * block
        up0 = jnp.where(step > 0, jnp.where(sea_of(base - 1), above[...], 0.0),
                        jnp.where(ids[1] > 0, halo_up[0, 0].astype(jnp.float32), 0.0))
        down_end = jnp.where(step < steps - 1, jnp.where(sea_of(base + block), below[...], 0.0),
                             jnp.where(ids[1] < n_row - 1, halo_down[0, 0].astype(jnp.float32), 0.0))

        def one(y, up, here, value, down, packed):
            turned = pltpu.roll(sides, (lanes - 1 - 2 * y) % lanes, 1)
            left = jnp.where(first, turned, pltpu.roll(here, 1, 1))
            right = jnp.where(final_lane, turned, pltpu.roll(here, lanes - 1, 1))
            sea = sea_of(base + y)
            lap = up + down + left + right - 4.0 * here
            new = value + jnp.where(sea, diffusion_rate * lap, 0.0)
            out[pl.ds(pl.multiple_of(y * levels, levels), levels), :] = new
            if final:
                here_row = out[pl.ds(y * levels, 1), :]
                out[pl.ds(y * levels, 1), :] = here_row + 0.3 * gap[pl.ds(y, 1), :]
                return packed, None
            masked = jnp.where(sea, new, 0.0)
            return pack_edge(packed, masked, y), masked

        def masked_row(y):
            value = field[pl.ds(pl.multiple_of(y * levels, levels), levels), :]
            return value, jnp.where(sea_of(base + y), value, 0.0)

        def body(y, carry):
            up, here, value, packed = carry
            down_value, down = masked_row(y + 1)
            packed, _ = one(y, up, here, value, down, packed)
            return here, down, down_value, packed

        value0, here0 = masked_row(0)
        packed0 = jnp.zeros(shape, jnp.float32)
        up, here, value, packed = lax.fori_loop(0, block - 1, body, (up0, here0, value0, packed0), unroll=3)
        packed, _ = one(block - 1, up, here, value, down_end, packed)
        if not final:
            for c in range(edge.shape[0]):
                edge[c, 0] = packed.astype(jnp.bfloat16)

            @pl.when(step == 0)
            def _():
                ends[0] = jnp.where(sea_of(0), out[0:levels, :], 0.0).astype(jnp.bfloat16)

            @pl.when(step == steps - 1)
            def _():
                ends[1] = jnp.where(
                    sea_of(rows - 1), out[pl.ds((block - 1) * levels, levels), :], 0.0
                ).astype(jnp.bfloat16)


def legendre_kernel(ids, legendre, coeffs, *rest, n_row, wave_dev, first_wave, with_ends):
    if with_ends:
        ends, out = rest
    else:
        (out,) = rest
    index = pl.program_id(0)
    lats = coeffs.shape[2]
    count = legendre.shape[2]

    @pl.when(ids[0] == 0)
    def _():
        table = legendre[0]
        fourier = coeffs[:, 0].reshape(n_row * lats, lanes)
        spectral = lax.dot_general(fourier, table, (((0,), (0,)), ((), ())), preferred_element_type=jnp.float32)
        wave = ids[1] * wave_dev + first_wave + index
        total = (wave + lax.broadcasted_iota(jnp.int32, (1, count), 1)).astype(jnp.float32)
        ratio = total * (total + 1.0) / (1279.0 * 1280.0)
        damping = 1.0 / (1.0 + 20.0 * ratio * ratio)
        filtered = (spectral * damping).astype(jnp.bfloat16)
        result = lax.dot_general(table, filtered, (((1,), (1,)), ((), ())), preferred_element_type=jnp.float32)
        out[:, 0] = result.astype(jnp.bfloat16).reshape(n_row, lats, lanes)

    if with_ends:
        @pl.when((ids[0] != 0) & (index == 0))
        def _():
            levels = ends.shape[1]
            for dest in range(n_row):
                out[dest, 0, 0:levels, :] = jnp.where(dest > ids[1], ends[1], ends[0])


def surface_kernel(ids, counts, partner, own, source, new, gap, *, group):
    rows = partner.shape[0]
    half = rows // 2
    width = 2 * lanes
    table = jnp.concatenate(
        [partner[pl.ds(0, half, stride=2), :], partner[pl.ds(1, half, stride=2), :]], axis=1
    )
    coarse = table.astype(jnp.bfloat16)
    fine = (table - coarse.astype(jnp.float32)).astype(jnp.bfloat16)
    low_index = lax.broadcasted_iota(jnp.int32, (width, lanes), 0)
    high_index = lax.broadcasted_iota(jnp.int32, (half, lanes), 0)
    one = jnp.ones((width, lanes), jnp.bfloat16)
    zero = jnp.zeros((width, lanes), jnp.bfloat16)
    sublane = lax.broadcasted_iota(jnp.int32, (8, lanes), 0)
    rate = jnp.where(ids[0] == 0, 0.5, 0.25).astype(jnp.float32)

    def body(g, carry):
        start = pl.multiple_of(g * 8, 8)
        entries = source[pl.ds(start, 8), :]
        low = entries & (width - 1)
        high = entries >> 8
        found = []
        for p in range(0, 8, group):
            pick = jnp.concatenate(
                [jnp.where(low_index == low[s:s + 1, :], one, zero) for s in range(p, p + group)], axis=1
            )
            picked = jnp.dot(coarse, pick, preferred_element_type=jnp.float32)
            picked = picked + jnp.dot(fine, pick, preferred_element_type=jnp.float32)
            for s in range(group):
                part = picked[:, lanes * s:lanes * (s + 1)]
                match = high_index == high[p + s:p + s + 1, :]
                found.append(jnp.sum(jnp.where(match, part, 0.0), axis=0, keepdims=True))
        pulled = jnp.concatenate(found, axis=0)
        limit = jnp.zeros((8, lanes), jnp.int32)
        for s in range(8):
            limit = jnp.where(sublane == s, counts[start + s], limit)
        here = own[pl.ds(start, 8), :]
        difference = jnp.where(lane_index() < limit, pulled - here, 0.0)
        new[pl.ds(start, 8), :] = here + rate * difference
        gap[pl.ds(start, 8), :] = difference
        return carry

    lax.fori_loop(0, rows // 8, body, 0)


def exit_kernel(ids, sea, *rest, n_row, chunks, block):
    back, out = rest[:chunks], rest[chunks]
    levels = out.shape[0] // block
    width = levels // n_row // chunks

    @pl.when(ids[0] == 0)
    def _():
        for wave in range(levels):
            origin, local = divmod(wave, levels // n_row)
            chunk, slot = divmod(local, width)
            out[pl.ds(wave, block, stride=levels), :] = back[chunk][origin, slot].astype(jnp.float32)

    @pl.when(ids[0] != 0)
    def _():
        out[...] = sea[...]


def entry_body(*refs, chunks, **kw):
    ids, counts, field, last, gauss, mix = refs[:6]
    send = refs[6:6 + chunks]
    mixed, edge = refs[6 + chunks:]
    entry_kernel(ids, counts, field, last, gauss, mix, send, mixed, edge, chunks=chunks, **kw)


def shards(model_state, legendre, gauss_weight, mixing, surface, sea_count, remap_source):
    n_row, n_col = lax.axis_size("row"), lax.axis_size("col")
    rows, levels = model_state.shape[1], model_state.shape[2]
    wave_dev = levels // n_row
    chunks = 2 if wave_dev % 2 == 0 else 1
    width = wave_dev // chunks
    block = row_block(rows)
    steps = rows // block
    groups = 8
    f32, bf16 = jnp.float32, jnp.bfloat16
    sds = jax.ShapeDtypeStruct

    fields = model_state.reshape(rows * levels, lanes)
    counts = sea_count.reshape(rows)
    ids = jnp.stack([lax.axis_index("comp"), lax.axis_index("row"), lax.axis_index("col")]).astype(jnp.int32)
    own = surface[0]
    comp_size = lax.axis_size("comp")
    partner = lax.ppermute(own, "comp", [(i, comp_size - 1 - i) for i in range(comp_size)])

    gauss = jnp.broadcast_to(gauss_weight[:, None], (rows, lanes))
    stacked = jnp.kron(jnp.eye(groups, dtype=f32), mixing)

    def on(comp, i, s):
        return jnp.where(s[0] == comp, i, 0)

    *send, mixed, edge = pl.pallas_call(
        functools.partial(entry_body, n_row=n_row, chunks=chunks, block=block, groups=groups),
        out_shape=[sds((n_row, width, rows, lanes), bf16)] * chunks
        + [sds((rows * levels, lanes), f32), sds((n_col, steps, levels, lanes), bf16)],
        grid_spec=pltpu.PrefetchScalarGridSpec(
            num_scalar_prefetch=2, grid=(steps,),
            in_specs=[
                pl.BlockSpec((block * levels, lanes), lambda i, s, c: (i, 0)),
                pl.BlockSpec((groups * levels, lanes), lambda i, s, c: (rows // groups - 1, 0)),
                pl.BlockSpec((block, lanes), lambda i, s, c: (i, 0)),
                pl.BlockSpec((groups * levels, groups * levels), lambda i, s, c: (0, 0)),
            ],
            out_specs=[pl.BlockSpec((n_row, width, block, lanes), lambda i, s, c: (0, 0, i, 0))] * chunks
            + [
                pl.BlockSpec((block * levels, lanes), lambda i, s, c: (on(1, i, s), 0)),
                pl.BlockSpec((n_col, 1, levels, lanes), lambda i, s, c: (0, i, 0, 0)),
            ],
        ),
        name="entry",
        cost_estimate=cost(10**7, 4 * rows * levels * lanes * 2),
    )(ids, counts, fields, fields, gauss, stacked)

    def to_waves(x):
        return lax.all_to_all(x, "row", split_axis=0, concat_axis=0, tiled=True)

    def to_columns(x):
        return lax.all_to_all(x, "col", split_axis=0, concat_axis=0, tiled=True)

    coeffs = [to_waves(x) for x in send]
    sides = to_columns(edge)

    new_surface, gap = pl.pallas_call(
        functools.partial(surface_kernel, group=2),
        out_shape=[sds((rows, lanes), f32)] * 2,
        grid_spec=pltpu.PrefetchScalarGridSpec(
            num_scalar_prefetch=2, grid=(1,),
            in_specs=[pl.BlockSpec((rows, lanes), lambda i, s, c: (0, 0))] * 3,
            out_specs=[pl.BlockSpec((rows, lanes), lambda i, s, c: (0, 0))] * 2,
        ),
        name="surface",
        cost_estimate=cost(10**10, 5 * 4 * rows * lanes),
    )(ids, counts, partner, own, remap_source[0])

    def sweep(field, rows_in, cols_in, final, extra=()):
        out_shape = [sds((rows * levels, lanes), f32)]
        out_specs = [pl.BlockSpec((block * levels, lanes), lambda i, s, c: (on(1, i, s), 0))]
        if not final:
            out_shape += [sds((n_col, steps, levels, lanes), bf16), sds((2, levels, lanes), bf16)]
            out_specs += [
                pl.BlockSpec((n_col, 1, levels, lanes), lambda i, s, c: (0, i, 0, 0)),
                pl.BlockSpec((2, levels, lanes), lambda i, s, c: (0, 0, 0)),
            ]
        return pl.pallas_call(
            functools.partial(sweep_kernel, block=block, n_row=n_row, n_col=n_col, final=final),
            out_shape=out_shape,
            grid_spec=pltpu.PrefetchScalarGridSpec(
                num_scalar_prefetch=2, grid=(steps,),
                in_specs=[
                    pl.BlockSpec((block * levels, lanes), lambda i, s, c: (on(1, i, s), 0)),
                    pl.BlockSpec((levels, lanes), lambda i, s, c: (jnp.maximum(on(1, i, s) * block - 1, 0), 0)),
                    pl.BlockSpec((levels, lanes),
                                 lambda i, s, c: (jnp.minimum((on(1, i, s) + 1) * block, rows - 1), 0)),
                    pl.BlockSpec((1, 1, levels, lanes), lambda i, s, c: (jnp.maximum(s[1] - 1, 0), 0, 0, 0)),
                    pl.BlockSpec((1, 1, levels, lanes), lambda i, s, c: (jnp.minimum(s[1] + 1, n_row - 1), 0, 0, 0)),
                    pl.BlockSpec((1, 1, levels, lanes),
                                 lambda i, s, c: (jnp.minimum(s[2] + 1, n_col - 1), i, 0, 0)),
                    pl.BlockSpec((1, 1, levels, lanes), lambda i, s, c: (jnp.maximum(s[2] - 1, 0), i, 0, 0)),
                ] + ([pl.BlockSpec((block, lanes), lambda i, s, c: (i, 0))] if final else []),
                out_specs=out_specs,
            ),
            name="sweep_last" if final else "sweep",
            cost_estimate=cost(10**7, 4 * rows * levels * lanes * 2),
        )(ids, counts, field, field, field, rows_in, rows_in, cols_in, cols_in, *extra)

    first_step, edge, ends = sweep(mixed, coeffs[0], sides, False)
    sides = to_columns(edge)

    returned = []
    for chunk in range(chunks):
        with_ends = chunk == 0
        part = pl.pallas_call(
            functools.partial(legendre_kernel, n_row=n_row, wave_dev=wave_dev, first_wave=chunk * width,
                              with_ends=with_ends),
            out_shape=sds((n_row, width, rows, lanes), bf16),
            grid_spec=pltpu.PrefetchScalarGridSpec(
                num_scalar_prefetch=1, grid=(width,),
                in_specs=[
                    pl.BlockSpec((1,) + legendre.shape[1:],
                                 lambda i, s, chunk=chunk: (chunk * width + on(0, i, s), 0, 0)),
                    pl.BlockSpec((n_row, 1, rows, lanes), lambda i, s: (0, i, 0, 0)),
                ] + ([pl.BlockSpec((2, levels, lanes), lambda i, s: (0, 0, 0))] if with_ends else []),
                out_specs=pl.BlockSpec((n_row, 1, rows, lanes), lambda i, s: (0, i, 0, 0)),
            ),
            name=f"legendre_{chunk}",
            cost_estimate=cost(4 * width * legendre.shape[1] * legendre.shape[2] * lanes,
                               2 * width * legendre.shape[1] * legendre.shape[2]),
        )(ids, legendre, coeffs[chunk], *([ends] if with_ends else []))
        returned.append(to_waves(part))

    (sea,) = sweep(first_step, returned[0], sides, True, (gap,))

    state = pl.pallas_call(
        functools.partial(exit_body, n_row=n_row, chunks=chunks, block=block),
        out_shape=sds((rows * levels, lanes), f32),
        grid_spec=pltpu.PrefetchScalarGridSpec(
            num_scalar_prefetch=1, grid=(steps,),
            in_specs=[pl.BlockSpec((block * levels, lanes), lambda i, s: (on(1, i, s), 0))]
            + [pl.BlockSpec((n_row, width, block, lanes), lambda i, s: (0, 0, on(0, i, s), 0))] * chunks,
            out_specs=pl.BlockSpec((block * levels, lanes), lambda i, s: (i, 0)),
        ),
        name="exit",
        cost_estimate=cost(10**6, 6 * rows * levels * lanes),
    )(ids, sea, *returned)
    return state.reshape(model_state.shape), new_surface[None]


def exit_body(*refs, **kw):
    exit_kernel(*refs, **kw)


def solution(mesh):
    in_specs = (
        P("comp", "row", None, "col"),
        P("row", None, None),
        P("row"),
        P(),
        P("comp", "row", "col"),
        P("comp", "row", "col"),
        P("comp", "row", "col"),
    )
    out_specs = (P("comp", "row", None, "col"), P("comp", "row", "col"))
    return jax.shard_map(shards, mesh=mesh, in_specs=in_specs, out_specs=out_specs, check_vma=False)
```

time: 419 us -> 169 us (0.40)
  local copies, waits for them, and re-layouts: 300 us -> 5.27 us
  Pallas kernels: 0 us -> 97.1 us
  other arithmetic: 49.3 us -> 2.01 us
  matrix products: 33.7 us -> 0 us
  blocking collectives: 0 us -> 32.4 us
  starting transfers between devices: 29.6 us -> 19.7 us
  waiting for transfers between devices: 1.7 us -> 10.3 us
    gather x1 -> x0, local copies, waits for them, and re-layouts: 226 us -> none  [shards(): jnp.take(partner.reshape(-1), remap_source[0].reshape(-1))]
    pallas_call x0 -> x7, Pallas kernels: none -> 97.1 us  [the longest x2 40.3 us: sweep(): pl.pallas_call(functools.partial(sweep_kernel, block=block, n_row=n_row,...]
    dot_general x2 -> x0, matrix products: 33.7 us -> none  [the longest x1 22.1 us: atmosphere(): jnp.einsum('wln,wnc->wlc', legendre, filtered, preferred_element_type=jnp...]
    slice x8 -> x0, local copies, waits for them, and re-layouts: 33 us -> none  [the longest x4 23.9 us: padded_2(): lax.slice_in_dim(block, 0, width, axis=dim)]
    all_to_all x0 -> x2, blocking collectives: none -> 32.4 us  [the longest x1 22.1 us: to_waves(): return lax.all_to_all(x, 'row', split_axis=0, concat_axis=0, tiled=True)]
    mul x2 -> x1, other arithmetic: 20.9 us -> 0.85 us  [shards(): stacked = jnp.kron(jnp.eye(groups, dtype=f32), mixing)]
    ppermute x4 -> x0, local copies, waits for them, and re-layouts: 19.5 us -> none  [the longest x2 9.77 us: padded_2(): lax.ppermute(lax.slice_in_dim(block, 0, width, axis=dim), axis, backward)]
    ppermute x9 -> x1, starting transfers between devices: 19.5 us -> 0.01 us  [shards(): lax.ppermute(own, 'comp', [(i, comp_size - 1 - i) for i in range(comp_siz...]
  transfers between devices with their start and end apart: 11 -> 5, of which waited for: 1 -> 1; matrix products, arithmetic and copies ran while one was open for 82% -> 0% of each run, Pallas kernels for 0% -> 40%
where the time goes in v1:
time: 169 us; the launch traced here: 168 us
  Pallas kernels  97.1 us (57%)
  blocking collectives  32.4 us (19%)
  starting transfers between devices  19.7 us (12%)
  waiting for transfers between devices  10.3 us (6%)
  local copies, waits for them, and re-layouts  5.27 us (3%)
  other arithmetic  2.01 us (1%)
    pallas_call x2, Pallas kernels, sweep(): pl.pallas_call(functools.partial(sweep_kernel, block=block, n_row=n_row,...  40.3 us
    all_to_all x1, blocking collectives, to_waves(): return lax.all_to_all(x, 'row', split_axis=0, concat_axis=0, tiled=True)  22.1 us
    pallas_call x1, Pallas kernels, shards(): pl.pallas_call(functools.partial(entry_body, n_row=n_row, chunks=chunks,...  22 us
    pallas_call x1, Pallas kernels, shards(): pl.pallas_call(functools.partial(surface_kernel, group=2), out_shape=[sds...  17.3 us
    all_to_all x3, starting transfers between devices, to_waves(): return lax.all_to_all(x, 'row', split_axis=0, concat_axis=0, tiled=True)  16.4 us
    all_to_all x1, blocking collectives, to_columns(): return lax.all_to_all(x, 'col', split_axis=0, concat_axis=0, tiled=True)  10.4 us
    all_to_all x3, waiting for transfers between devices, to_waves(): return lax.all_to_all(x, 'row', split_axis=0, concat_axis=0, tiled=True)  10.3 us
    pallas_call x2, Pallas kernels, shards(): pl.pallas_call(functools.partial(legendre_kernel, n_row=n_row, wave_dev=w...  10.2 us
  transfers between devices with their start and end apart: 5, of which 1 were waited for; matrix products, arithmetic and copies ran while one was open for 0% of the time, Pallas kernels for 40%

profile of v1, /device:TPU:7, one launch (start us, length us, event | category | flops | bytes accessed | tf_op | source)
XLA Modules:
  0.0 167.6 jit_solution(11644533158635343768)
XLA Ops:
  0.7 0.9 broadcast_multiply_fusion
  1.5 1.0 mul.27.refs_5_
  2.5 0.6 reduce.refs_1_.counts
  3.1 0.6 pad_add_fusion.refs_0_.ids
  3.7 0.8 broadcast_in_dim.8.refs_4_
  4.5 22.0 %entry.1 = (bf16[4,4,320,128]{3,2,1,0:T(8,128)(2,1)}, bf16[4,4,320,128]{3,2,1,0:T(8,128)(2,1)}, f32[10240,128]{1,0:T(8,128)}, bf16[4,5,32,128]{3,2,1,0:T(8,128)(2,1)}) custom-call(s32[3]{0:T(128)} %pad_add_fusion.refs_0_.ids, s32[320]{0:T(512)} %reduce.refs_1_.counts, f32[10240,128]{1,0:T(8,128)} %bitcast.10, f32[10240,128]{1,0:T(8,128)} %bitcast.11, ...), custom_call_target="tpu_custom_call" | custom-call | flops 10000000 | bytes 10485760 | tf_op jit(solution)/shard_map/entry/pallas_call | solution.py:279
  26.4 10.4 %all_to_all.30.east_in.west_in = bf16[4,5,32,128]{3,2,1,0:T(8,128)(2,1)} all-to-all(bf16[4,5,32,128]{3,2,1,0:T(8,128)(2,1)} %get-tuple-element.13), channel_id=1, replica_groups=mesh['comp'=2,'row'=4,'col'=4] {'col'}, dimensions={0} | all-to-all | bytes 327680 | tf_op jit(solution)/shard_map/all_to_all | solution.py:305
  36.8 22.1 %all_to_all.31.halo_up.halo_down.coeffs = bf16[4,4,320,128]{3,2,1,0:T(8,128)(2,1)} all-to-all(bf16[4,4,320,128]{3,2,1,0:T(8,128)(2,1)} %get-tuple-element.12), channel_id=1, replica_groups=mesh['comp'=2,'row'=4,'col'=4] {'row'}, dimensions={0} | all-to-all | bytes 2621440 | tf_op jit(solution)/shard_map/all_to_all | solution.py:302
  58.9 5.4 %all-to-all-start.4 = ((bf16[4,4,320,128]{3,2,1,0:T(8,128)(2,1)}), bf16[4,4,320,128]{3,2,1,0:T(8,128)(2,1)S(1)}, u32[]{:S(2)}, u32[]{:S(2)}) async-start(bf16[4,4,320,128]{3,2,1,0:T(8,128)(2,1)} %get-tuple-element.18), calls=%async_computation.4 | async-start | bytes 2621440 | tf_op jit(solution)/shard_map/all_to_all | solution.py:302
  64.2 23.3 %sweep.1 = (f32[10240,128]{1,0:T(8,128)}, bf16[4,5,32,128]{3,2,1,0:T(8,128)(2,1)}, bf16[2,32,128]{2,1,0:T(8,128)(2,1)}) custom-call(s32[3]{0:T(128)} %pad_add_fusion.refs_0_.ids, s32[320]{0:T(512)} %reduce.refs_1_.counts, f32[10240,128]{1,0:T(8,128)} %get-tuple-element.11.field.above.below, f32[10240,128]{1,0:T(8,128)} %get-tuple-element.11.field.above.below, ...), custom_call_target="tpu_custom_call" | custom-call | flops 10000000 | bytes 10485760 | tf_op jit(solution)/shard_map/sweep/pallas_call | solution.py:331
  87.5 0.0 all-to-all-done.4.coeffs
  87.5 3.4 %all-to-all-start.3 = ((bf16[4,5,32,128]{3,2,1,0:T(8,128)(2,1)}), bf16[4,5,32,128]{3,2,1,0:T(8,128)(2,1)S(1)}, u32[]{:S(2)}, u32[]{:S(2)}) async-start(bf16[4,5,32,128]{3,2,1,0:T(8,128)(2,1)} %get-tuple-element.16), calls=%async_computation.3 | async-start | bytes 327680 | tf_op jit(solution)/shard_map/all_to_all | solution.py:305
  90.9 5.1 %legendre_0.1 = bf16[4,4,320,128]{3,2,1,0:T(8,128)(2,1)} custom-call(s32[3]{0:T(128)} %pad_add_fusion.refs_0_.ids, bf16[8,1280,1280]{2,1,0:T(8,128)(2,1)} %legendre.3, bf16[4,4,320,128]{3,2,1,0:T(8,128)(2,1)} %all_to_all.31.halo_up.halo_down.coeffs, bf16[2,32,128]{2,1,0:T(8,128)(2,1)} %get-tuple-element.15.rest_0_), custom_call_target="tpu_custom_call" | custom-call | flops 3355443200 | bytes 13107200 | tf_op jit(solution)/shard_map/legendre_0/pallas_call | solution.py:359
  96.0 0.7 copy-done.3
  96.7 5.6 %all-to-all-start.2 = ((bf16[4,4,320,128]{3,2,1,0:T(8,128)(2,1)}), bf16[4,4,320,128]{3,2,1,0:T(8,128)(2,1)S(1)}, u32[]{:S(2)}, u32[]{:S(2)}) async-start(bf16[4,4,320,128]{3,2,1,0:T(8,128)(2,1)} %legendre_0.1), calls=%async_computation.2 | async-start | bytes 2621440 | tf_op jit(solution)/shard_map/all_to_all | solution.py:302
  102.3 5.1 %legendre_1.1 = bf16[4,4,320,128]{3,2,1,0:T(8,128)(2,1)} custom-call(s32[3]{0:T(128)} %pad_add_fusion.refs_0_.ids, bf16[8,1280,1280]{2,1,0:T(8,128)(2,1)} %legendre.3, bf16[4,4,320,128]{3,2,1,0:T(8,128)(2,1)} %copy-done.2), custom_call_target="tpu_custom_call" | custom-call | flops 3355443200 | bytes 13107200 | tf_op jit(solution)/shard_map/legendre_1/pallas_call | solution.py:359
  107.4 10.3 %all-to-all-done.2.halo_up.halo_down.refs_2_ = bf16[4,4,320,128]{3,2,1,0:T(8,128)(2,1)S(1)} async-done(((bf16[4,4,320,128]{3,2,1,0:T(8,128)(2,1)}), bf16[4,4,320,128]{3,2,1,0:T(8,128)(2,1)S(1)}, u32[]{:S(2)}, u32[]{:S(2)}) %all-to-all-start.2) | async-done | bytes 1310752 | tf_op jit(solution)/shard_map/all_to_all | solution.py:302
  117.7 1.1 copy-done
  118.8 5.4 %all-to-all-start.5 = ((bf16[4,4,320,128]{3,2,1,0:T(8,128)(2,1)}), bf16[4,4,320,128]{3,2,1,0:T(8,128)(2,1)S(1)}, u32[]{:S(2)}, u32[]{:S(2)}) async-start(bf16[4,4,320,128]{3,2,1,0:T(8,128)(2,1)} %legendre_1.1), calls=%async_computation.5 | async-start | bytes 2621440 | tf_op jit(solution)/shard_map/all_to_all | solution.py:302
  124.1 0.7 copy-done.7
  124.8 17.3 %surface.1 = (f32[320,128]{1,0:T(8,128)}, f32[320,128]{1,0:T(8,128)}) custom-call(s32[3]{0:T(128)} %pad_add_fusion.refs_0_.ids, s32[320]{0:T(512)} %reduce.refs_1_.counts, f32[320,128]{1,0:T(8,128)} %copy-done.7, f32[320,128]{1,0:T(8,128)} %bitcast.13, s32[320,128]{1,0:T(8,128)} %bitcast.15), custom_call_target="tpu_custom_call" | custom-call | flops 10000000000 | bytes 819200 | tf_op jit(solution)/shard_map/surface/pallas_call | solution.py:310
  142.1 17.1 %sweep_last.1.refs_1_ = f32[10240,128]{1,0:T(8,128)} custom-call(s32[3]{0:T(128)} %pad_add_fusion.refs_0_.ids, s32[320]{0:T(512)} %reduce.refs_1_.counts, f32[10240,128]{1,0:T(8,128)} %get-tuple-element.14.field.above.below, f32[10240,128]{1,0:T(8,128)} %get-tuple-element.14.field.above.below, f32[10240,128]{1,0:T(8,128)} %get-tuple-element.14.field.above.below, ...), custom_call_target="tpu_custom_call" | custom-call | flops 10000000 | bytes 10485760 | tf_op jit(solution)/shard_map/sweep_last/pallas_call | solution.py:331
  159.2 1.1 copy-done.1
  160.3 7.3 %exit.1 = f32[10240,128]{1,0:T(8,128)} custom-call(s32[3]{0:T(128)} %pad_add_fusion.refs_0_.ids, f32[10240,128]{1,0:T(8,128)} %sweep_last.1.refs_1_, bf16[4,4,320,128]{3,2,1,0:T(8,128)(2,1)} %copy-done, bf16[4,4,320,128]{3,2,1,0:T(8,128)(2,1)} %copy-done.1), custom_call_target="tpu_custom_call" | custom-call | flops 1000000 | bytes 7864320 | tf_op jit(solution)/shard_map/exit/pallas_call | solution.py:380
  (17 shorter events, 0.0 us)
Async XLA Ops:
  0.6 1.9 %copy-start.5 = (s32[1,320,1]{1,2,0:T(1,128)S(1)}, s32[1,320,1]{1,2,0:T(1,128)}, u32[]{:S(2)}) copy-start(s32[1,320,1]{1,2,0:T(1,128)} %param.12) | copy-start | bytes 3844
  0.6 3.1 %copy-start.4 = (f32[320]{0:T(512)S(1)}, f32[320]{0:T(512)}, u32[]{:S(2)}) copy-start(f32[320]{0:T(512)} %param.9) | copy-start | bytes 3844
  58.9 28.6 %all-to-all-start.4 = ((bf16[4,4,320,128]{3,2,1,0:T(8,128)(2,1)}), bf16[4,4,320,128]{3,2,1,0:T(8,128)(2,1)S(1)}, u32[]{:S(2)}, u32[]{:S(2)}) async-start(bf16[4,4,320,128]{3,2,1,0:T(8,128)(2,1)} %get-tuple-element.18), calls=%async_computation.4 | async-start | bytes 2621440 | tf_op jit(solution)/shard_map/all_to_all | solution.py:302
  87.5 8.5 %copy-start.2 = (bf16[4,4,320,128]{3,2,1,0:T(8,128)(2,1)}, bf16[4,4,320,128]{3,2,1,0:T(8,128)(2,1)S(1)}, u32[]{:S(2)}) copy-start(bf16[4,4,320,128]{3,2,1,0:T(8,128)(2,1)S(1)} %all-to-all-done.4.coeffs) | copy-start | bytes 3932164
  87.5 8.5 %all-to-all-start.3 = ((bf16[4,5,32,128]{3,2,1,0:T(8,128)(2,1)}), bf16[4,5,32,128]{3,2,1,0:T(8,128)(2,1)S(1)}, u32[]{:S(2)}, u32[]{:S(2)}) async-start(bf16[4,5,32,128]{3,2,1,0:T(8,128)(2,1)} %get-tuple-element.16), calls=%async_computation.3 | async-start | bytes 327680 | tf_op jit(solution)/shard_map/all_to_all | solution.py:305
  96.0 6.3 %copy-start.6 = (f32[1,320,128]{2,1,0:T(8,128)S(1)}, f32[1,320,128]{2,1,0:T(8,128)}, u32[]{:S(2)}) copy-start(f32[1,320,128]{2,1,0:T(8,128)} %param.11) | copy-start | bytes 491524
  96.0 0.7 copy-start.3
  96.7 21.0 %all-to-all-start.2 = ((bf16[4,4,320,128]{3,2,1,0:T(8,128)(2,1)}), bf16[4,4,320,128]{3,2,1,0:T(8,128)(2,1)S(1)}, u32[]{:S(2)}, u32[]{:S(2)}) async-start(bf16[4,4,320,128]{3,2,1,0:T(8,128)(2,1)} %legendre_0.1), calls=%async_computation.2 | async-start | bytes 2621440 | tf_op jit(solution)/shard_map/all_to_all | solution.py:302
  102.3 21.8 %collective-permute-start = (f32[320,128]{1,0:T(8,128)S(1)}, f32[320,128]{1,0:T(8,128)S(1)}, u32[]{:S(2)}, u32[]{:S(2)}) collective-permute-start(f32[320,128]{1,0:T(8,128)S(1)} %bitcast.14), channel_id=1, source_target_pairs={{0,16},{16,0},{1,17},{17,1},{2,18},{18,2},{3,19},{19,3},{4,20},{20... | collective-permute-start | bytes 491528 | tf_op jit(solution)/shard_map/ppermute | solution.py:271
  117.7 1.1 copy-start
  118.8 40.4 %all-to-all-start.5 = ((bf16[4,4,320,128]{3,2,1,0:T(8,128)(2,1)}), bf16[4,4,320,128]{3,2,1,0:T(8,128)(2,1)S(1)}, u32[]{:S(2)}, u32[]{:S(2)}) async-start(bf16[4,4,320,128]{3,2,1,0:T(8,128)(2,1)} %legendre_1.1), calls=%async_computation.5 | async-start | bytes 2621440 | tf_op jit(solution)/shard_map/all_to_all | solution.py:302
  124.1 0.7 copy-start.7
  159.2 1.1 copy-start.1

commit v2 on v0

v2 whole, which is shorter than its diff:
```python
import functools

import jax
import jax.numpy as jnp
from jax import lax
from jax.experimental import pallas as pl
from jax.experimental.pallas import tpu as pltpu
from jax.sharding import PartitionSpec as P

diffusion_rate = 0.2
lanes = 128


def row_block(rows):
    return 64 if rows % 64 == 0 else rows


def cost(flops, bytes_accessed):
    return pl.CostEstimate(flops=flops, bytes_accessed=bytes_accessed, transcendentals=0)


def where_am_i(place, n_row, n_col):
    flat = place[0]
    return (
        lax.div(flat, n_row * n_col),
        lax.rem(lax.div(flat, n_col), n_row),
        lax.rem(flat, n_col),
    )


def iota(shape, dim):
    return lax.broadcasted_iota(jnp.int32, shape, dim)


def as_bf16(mask):
    return jnp.where(mask, 1.0, 0.0).astype(jnp.bfloat16)


def swap_matrix():
    row, column = iota((256, 256), 0), iota((256, 256), 1)
    return as_bf16(column == ((row & 15) << 4 | row >> 4))


def spread_matrix():
    row, column = iota((lanes, lanes), 0), iota((lanes, lanes), 1)
    odd = column & 1
    return as_bf16(((row == lanes - 1) & (odd == 0)) | ((row == 0) & (odd == 1)))


def beside_matrix():
    row, column = iota((lanes, lanes), 0), iota((lanes, lanes), 1)
    return as_bf16((row == column + 1) | (row + 1 == column))


def side_matrix():
    row, column = iota((lanes, lanes), 0), iota((lanes, lanes), 1)
    odd = row & 1
    return as_bf16(((column == 0) & (odd == 1)) | ((column == lanes - 1) & (odd == 0)))


def split(value):
    high = value.astype(jnp.bfloat16)
    return high, (value - high.astype(jnp.float32)).astype(jnp.bfloat16)


def product(a, b):
    return jnp.dot(a, b, preferred_element_type=jnp.float32)


def entry_kernel(place, counts, field, last, gauss, mix, *rest, n_row, n_col, chunks, block):
    send = rest[:chunks]
    mixed, edge, table = rest[chunks:]
    comp, row, _ = where_am_i(place, n_row, n_col)
    levels = field.shape[0] // block
    wave_dev = levels // n_row
    width = wave_dev // chunks
    step = pl.program_id(0)

    def target(wave):
        dest, local = divmod(wave, wave_dev)
        chunk, slot = divmod(local, width)
        return send[chunk], dest, slot

    @pl.when(comp == 0)
    def _():
        @pl.when(step == 0)
        def _():
            table[...] = swap_matrix()

        for lat in range(0, block - 15, 16):
            halves = []
            for half in range(0, levels, 16):
                halves.append(jnp.concatenate([
                    (field[(lat + s) * levels + half:(lat + s) * levels + half + 16, :]
                     * gauss[step * block + lat + s]).astype(jnp.bfloat16)
                    for s in range(16)
                ], axis=0))
            turned = product(table[...], jnp.concatenate(halves, axis=1)).astype(jnp.bfloat16)
            for wave in range(levels):
                out, dest, slot = target(wave)
                part = lanes * (wave // 16)
                out[dest, slot, lat:lat + 16, :] = turned[16 * (wave % 16):16 * (wave % 16) + 16, part:part + lanes]
        for lat in range(block - block % 16, block, 8):
            weight = jnp.zeros((8, lanes), jnp.float32)
            for s in range(8):
                weight = jnp.where(iota((8, lanes), 0) == s, gauss[step * block + lat + s], weight)
            for wave in range(levels):
                out, dest, slot = target(wave)
                values = field[pl.ds(lat * levels + wave, 8, stride=levels), :] * weight
                out[dest, slot, lat:lat + 8, :] = values.astype(jnp.bfloat16)

    def mixed_rows(ref, start, first_row):
        values = []
        for quarter in range(2):
            parts = []
            for pair in range(2):
                part = ref[pl.ds(start + (2 * quarter + pair) * 2 * levels, 2 * levels), :]
                values.append(part)
                parts.append(split(part))
            high = jnp.concatenate([p[0] for p in parts], axis=1)
            low = jnp.concatenate([p[1] for p in parts], axis=1)
            blend = product(table[0:2 * levels, :], jnp.concatenate([high, low, high, low], axis=0))
            values += [blend[:, :lanes], blend[:, lanes:]]
        out = []
        for s in range(8):
            quarter, pair, place_in = s // 4, s // 2 % 2, slice(levels * (s % 2), levels * (s % 2) + levels)
            heat = values[4 * quarter + pair][place_in]
            blend = values[4 * quarter + 2 + pair][place_in]
            sea = iota((levels, lanes), 1) < counts[0, first_row + s]
            value = heat + jnp.where(sea, blend, 0.0)
            out.append((value, jnp.where(sea, value, 0.0).astype(jnp.bfloat16)))
        return out

    @pl.when(comp != 0)
    def _():
        @pl.when(step == 0)
        def _():
            high, low = split(mix[...])
            repeat = as_bf16((iota((levels, 256), 1) & (levels - 1)) == iota((levels, 256), 0))
            wide = jnp.where(iota((levels, 256), 1) < 4 * levels, product(high, repeat), product(low, repeat))
            wide = jnp.concatenate([wide, wide], axis=0)
            shape = (2 * levels, 256)
            own = (iota(shape, 1) // levels & 1) == iota(shape, 0) // levels
            table[0:2 * levels, :] = jnp.where(own, wide, 0.0).astype(jnp.bfloat16)

        spread = spread_matrix()
        pair_of = iota((levels, lanes), 1) >> 1

        def body(g, packed):
            start = pl.multiple_of(g * 8 * levels, 8 * levels)
            rows = mixed_rows(field, start, step * block + g * 8)
            for s, (value, _) in enumerate(rows):
                mixed[pl.ds(pl.multiple_of(start + s * levels, levels), levels), :] = value
            ends = product(jnp.concatenate([r[1] for r in rows], axis=0), spread)
            for s in range(8):
                packed = jnp.where(pair_of == g * 8 + s, ends[s * levels:(s + 1) * levels], packed)
            return packed

        packed = lax.fori_loop(0, block // 8, body, jnp.zeros((levels, lanes), jnp.float32))
        edge[0] = packed.astype(jnp.bfloat16)

        @pl.when(step == 0)
        def _():
            total = pl.num_programs(0) * block
            top = mixed_rows(field, 0, 0)[0][1]
            low = mixed_rows(last, 0, total - 8)[-1][1]
            for dest in range(n_row):
                send[0][dest, 0, 0:levels, :] = jnp.where(dest > row, low, top)


def sweep_kernel(place, counts, field, above, below, halo_up, halo_down, east_in, west_in, *rest,
                 block, n_row, n_col, final):
    if final:
        gap, out, masked = rest
    else:
        out, edge, ends, masked = rest
    comp, row, col = where_am_i(place, n_row, n_col)
    levels = field.shape[0] // block
    step = pl.program_id(0)
    steps = pl.num_programs(0)
    rows = steps * block
    base = step * block
    shape = (levels, lanes)

    @pl.when(comp != 0)
    def _():
        lane = iota(shape, 1)
        pair_of = lane >> 1

        def sea_of(y):
            return lane < counts[0, jnp.clip(y, 0, rows - 1)]

        def at(y):
            return pl.ds(pl.multiple_of(y * levels, levels), levels)

        west = jnp.where(col > 0, west_in[0].astype(jnp.float32), 0.0)
        east = jnp.where(col < n_col - 1, east_in[0].astype(jnp.float32), 0.0)
        sides = jnp.where((lane & 1) == 0, pltpu.roll(east, lanes - 1, 1), pltpu.roll(west, 1, 1))
        masked[0:levels, :] = jnp.where(
            step > 0, jnp.where(sea_of(base - 1), above[...], 0.0),
            jnp.where(row > 0, halo_up[0, 0].astype(jnp.float32), 0.0))
        masked[(block + 1) * levels:(block + 2) * levels, :] = jnp.where(
            step < steps - 1, jnp.where(sea_of(base + block), below[...], 0.0),
            jnp.where(row < n_row - 1, halo_down[0, 0].astype(jnp.float32), 0.0))

        def fill(g, carry):
            for s in range(8):
                y = g * 8 + s
                masked[at(y + 1), :] = jnp.where(sea_of(base + y), field[at(y), :], 0.0)
            return carry

        lax.fori_loop(0, block // 8, fill, 0)
        beside = beside_matrix()
        if final:
            weights = jnp.concatenate([beside, side_matrix()], axis=0)
        else:
            spread = spread_matrix()

        def body(g, packed):
            here = masked[pl.ds(pl.multiple_of((g * 8 + 1) * levels, levels), 8 * levels), :]
            high, low = split(here)
            turned = jnp.concatenate(
                [jnp.where(pair_of == g * 8 + s, sides, 0.0).astype(jnp.bfloat16) for s in range(8)], axis=0)
            both = jnp.concatenate([beside, side_matrix()], axis=0) if not final else weights
            near = product(jnp.concatenate([high, turned], axis=1), both) + product(low, beside)
            new_rows = []
            for s in range(8):
                y = g * 8 + s
                part = slice(s * levels, (s + 1) * levels)
                lap = masked[at(y), :] + masked[at(y + 2), :] + near[part] - 4.0 * here[part]
                sea = sea_of(base + y)
                new = field[at(y), :] + jnp.where(sea, diffusion_rate * lap, 0.0)
                out[at(y), :] = new
                if final:
                    start = y * levels
                    out[pl.ds(start, 1), :] = new[0:1, :] + 0.3 * gap[pl.ds(y, 1), :]
                else:
                    new_rows.append(jnp.where(sea, new, 0.0).astype(jnp.bfloat16))
            if not final:
                spreads = product(jnp.concatenate(new_rows, axis=0), spread)
                for s in range(8):
                    packed = jnp.where(pair_of == g * 8 + s, spreads[s * levels:(s + 1) * levels], packed)
            return packed

        packed = lax.fori_loop(0, block // 8, body, jnp.zeros(shape, jnp.float32))
        if not final:
            edge[0] = packed.astype(jnp.bfloat16)

            @pl.when(step == 0)
            def _():
                ends[0] = jnp.where(sea_of(0), out[0:levels, :], 0.0).astype(jnp.bfloat16)

            @pl.when(step == steps - 1)
            def _():
                ends[1] = jnp.where(
                    sea_of(rows - 1), out[(block - 1) * levels:block * levels, :], 0.0
                ).astype(jnp.bfloat16)


def legendre_kernel(place, legendre, coeffs, *rest, n_row, n_col, wave_dev, first_wave, with_ends):
    if with_ends:
        ends, _, out = rest
    else:
        (out,) = rest
    comp, row, _ = where_am_i(place, n_row, n_col)
    index = pl.program_id(0)
    lats = coeffs.shape[2]
    count = legendre.shape[2]

    @pl.when(comp == 0)
    def _():
        table = legendre[0]
        fourier = coeffs[:, 0].reshape(n_row * lats, lanes)
        spectral = lax.dot_general(fourier, table, (((0,), (0,)), ((), ())), preferred_element_type=jnp.float32)
        wave = row * wave_dev + first_wave + index
        total = (wave + iota((1, count), 1)).astype(jnp.float32)
        ratio = total * (total + 1.0) / (1279.0 * 1280.0)
        damping = 1.0 / (1.0 + 20.0 * ratio * ratio)
        filtered = (spectral * damping).astype(jnp.bfloat16)
        result = lax.dot_general(table, filtered, (((1,), (1,)), ((), ())), preferred_element_type=jnp.float32)
        out[:, 0] = result.astype(jnp.bfloat16).reshape(n_row, lats, lanes)

    if with_ends:
        @pl.when((comp != 0) & (index == 0))
        def _():
            levels = ends.shape[1]
            for dest in range(n_row):
                out[dest, 0, 0:levels, :] = jnp.where(dest > row, ends[1], ends[0])


def surface_kernel(place, counts, partner, own, source, _, new, gap, *, group, n_row, n_col):
    rows = partner.shape[0]
    half = rows // 2
    width = 2 * lanes
    table = jnp.concatenate(
        [partner[pl.ds(0, half, stride=2), :], partner[pl.ds(1, half, stride=2), :]], axis=1
    )
    coarse = table.astype(jnp.bfloat16)
    fine = (table - coarse.astype(jnp.float32)).astype(jnp.bfloat16)
    low_index = lax.broadcasted_iota(jnp.int32, (width, lanes), 0)
    high_index = lax.broadcasted_iota(jnp.int32, (half, lanes), 0)
    one = jnp.ones((width, lanes), jnp.bfloat16)
    zero = jnp.zeros((width, lanes), jnp.bfloat16)
    sublane = lax.broadcasted_iota(jnp.int32, (8, lanes), 0)
    rate = jnp.where(where_am_i(place, n_row, n_col)[0] == 0, 0.5, 0.25).astype(jnp.float32)

    def body(g, carry):
        start = pl.multiple_of(g * 8, 8)
        entries = source[pl.ds(start, 8), :]
        low = entries & (width - 1)
        high = entries >> 8
        found = []
        for p in range(0, 8, group):
            pick = jnp.concatenate(
                [jnp.where(low_index == low[s:s + 1, :], one, zero) for s in range(p, p + group)], axis=1
            )
            picked = jnp.dot(coarse, pick, preferred_element_type=jnp.float32)
            picked = picked + jnp.dot(fine, pick, preferred_element_type=jnp.float32)
            for s in range(group):
                part = picked[:, lanes * s:lanes * (s + 1)]
                match = high_index == high[p + s:p + s + 1, :]
                found.append(jnp.sum(jnp.where(match, part, 0.0), axis=0, keepdims=True))
        pulled = jnp.concatenate(found, axis=0)
        limit = jnp.zeros((8, lanes), jnp.int32)
        for s in range(8):
            limit = jnp.where(sublane == s, counts[0, start + s], limit)
        here = own[pl.ds(start, 8), :]
        difference = jnp.where(iota((8, lanes), 1) < limit, pulled - here, 0.0)
        new[pl.ds(start, 8), :] = here + rate * difference
        gap[pl.ds(start, 8), :] = difference
        return carry

    lax.fori_loop(0, rows // 8, body, 0)


def exit_kernel(place, sea, *rest, n_row, n_col, chunks, block):
    back, out, table = rest[:chunks], rest[chunks], rest[chunks + 1]
    comp, _, _ = where_am_i(place, n_row, n_col)
    levels = out.shape[0] // block
    wave_dev = levels // n_row
    width = wave_dev // chunks

    def source(wave, lat, count):
        origin, local = divmod(wave, wave_dev)
        chunk, slot = divmod(local, width)
        return back[chunk][origin, slot, lat:lat + count, :]

    @pl.when(comp == 0)
    def _():
        @pl.when(pl.program_id(0) == 0)
        def _():
            table[...] = swap_matrix()

        for lat in range(0, block - 15, 16):
            halves = [
                jnp.concatenate([source(half + wave, lat, 16) for wave in range(16)], axis=0)
                for half in range(0, levels, 16)
            ]
            turned = product(table[...], jnp.concatenate(halves, axis=1))
            for s in range(16):
                for half in range(0, levels, 16):
                    start = (lat + s) * levels + half
                    part = lanes * (half // 16)
                    out[start:start + 16, :] = turned[16 * s:16 * s + 16, part:part + lanes]
        for lat in range(block - block % 16, block, 8):
            for wave in range(levels):
                out[pl.ds(lat * levels + wave, 8, stride=levels), :] = source(wave, lat, 8).astype(jnp.float32)

    @pl.when(comp != 0)
    def _():
        out[...] = sea[...]


def shards(model_state, legendre, gauss_weight, mixing, surface, sea_count, remap_source):
    n_row, n_col = lax.axis_size("row"), lax.axis_size("col")
    rows, levels = model_state.shape[1], model_state.shape[2]
    wave_dev = levels // n_row
    chunks = 2 if wave_dev % 2 == 0 else 1
    width = wave_dev // chunks
    block = row_block(rows)
    steps = rows // block
    f32, bf16 = jnp.float32, jnp.bfloat16
    sds = jax.ShapeDtypeStruct
    mib = 1 << 20

    fields = model_state.reshape(rows * levels, lanes)
    counts = sea_count.reshape(1, rows)
    place = lax.axis_index(("comp", "row", "col")).astype(jnp.int32).reshape(1)
    own = surface[0]
    comp_size = lax.axis_size("comp")
    partner = lax.ppermute(own, "comp", [(i, comp_size - 1 - i) for i in range(comp_size)])

    def on(comp, i, s):
        return jnp.where(lax.div(s[0], n_row * n_col) == comp, i, 0)

    def row_of(s):
        return lax.rem(lax.div(s[0], n_col), n_row)

    def call(kernel, name, grid, in_specs, out_specs, out_shape, args, scratch=(), vmem=59, flops=10**7, size=0):
        return pl.pallas_call(
            functools.partial(kernel, n_row=n_row, n_col=n_col),
            out_shape=out_shape,
            grid_spec=pltpu.PrefetchScalarGridSpec(
                num_scalar_prefetch=1, grid=grid, in_specs=in_specs, out_specs=out_specs, scratch_shapes=scratch),
            compiler_params=pltpu.CompilerParams(vmem_limit_bytes=vmem * mib),
            name=name,
            cost_estimate=cost(flops, size),
        )(place, *args)

    smem = pl.BlockSpec(memory_space=pltpu.SMEM)
    anywhere = pl.BlockSpec(memory_space=pl.ANY)
    state_bytes = 4 * rows * levels * lanes
    tall = block * levels

    *send, mixed, edge = call(
        functools.partial(entry_kernel, chunks=chunks, block=block), "entry", (steps,),
        [
            smem,
            pl.BlockSpec((tall, lanes), lambda i, s: (i, 0)),
            pl.BlockSpec((8 * levels, lanes), lambda i, s: (rows // 8 - 1, 0)),
            smem,
            pl.BlockSpec((levels, levels), lambda i, s: (0, 0)),
        ],
        [pl.BlockSpec((n_row, width, block, lanes), lambda i, s: (0, 0, i, 0))] * chunks
        + [
            pl.BlockSpec((tall, lanes), lambda i, s: (on(1, i, s), 0)),
            pl.BlockSpec((1, levels, lanes), lambda i, s: (on(1, i, s), 0, 0)),
        ],
        [sds((n_row, width, rows, lanes), bf16)] * chunks
        + [sds((rows * levels, lanes), f32), sds((steps, levels, lanes), bf16)],
        (counts, fields, fields, gauss_weight, mixing),
        scratch=[pltpu.VMEM((256, 256), bf16)], vmem=63, size=2 * state_bytes,
    )

    def to_waves(x):
        return lax.all_to_all(x, "row", split_axis=0, concat_axis=0, tiled=True)

    ahead = [(i, i + 1) for i in range(n_col - 1)]

    def to_columns(x):
        return [lax.ppermute(x, "col", [(b, a) for a, b in ahead]), lax.ppermute(x, "col", ahead)]

    coeffs = [to_waves(x) for x in send]
    sides = to_columns(edge)

    whole = pl.BlockSpec((rows, lanes), lambda i, s: (0, 0))
    new_surface, gap = call(
        functools.partial(surface_kernel, group=2), "surface", (1,),
        [smem, whole, whole, whole, anywhere], [whole] * 2, [sds((rows, lanes), f32)] * 2,
        (counts, partner, own, remap_source[0], edge), flops=2 * 10**10, size=5 * 4 * rows * lanes,
    )

    def sweep(field, rows_in, cols_in, final, extra=()):
        out_shape = [sds((rows * levels, lanes), f32)]
        out_specs = [pl.BlockSpec((tall, lanes), lambda i, s: (on(1, i, s), 0))]
        if not final:
            out_shape += [sds((steps, levels, lanes), bf16), sds((2, levels, lanes), bf16)]
            out_specs += [
                pl.BlockSpec((1, levels, lanes), lambda i, s: (on(1, i, s), 0, 0)),
                pl.BlockSpec((2, levels, lanes), lambda i, s: (0, 0, 0)),
            ]
        side = (1, 1, levels, lanes)
        in_specs = [
            smem,
            pl.BlockSpec((tall, lanes), lambda i, s: (on(1, i, s), 0)),
            pl.BlockSpec((levels, lanes), lambda i, s: (jnp.maximum(on(1, i, s) * block - 1, 0), 0)),
            pl.BlockSpec((levels, lanes), lambda i, s: (jnp.minimum((on(1, i, s) + 1) * block, rows - 1), 0)),
            pl.BlockSpec(side, lambda i, s: (jnp.maximum(row_of(s) - 1, 0), 0, 0, 0)),
            pl.BlockSpec(side, lambda i, s: (jnp.minimum(row_of(s) + 1, n_row - 1), 0, 0, 0)),
            pl.BlockSpec((1, levels, lanes), lambda i, s: (on(1, i, s), 0, 0)),
            pl.BlockSpec((1, levels, lanes), lambda i, s: (on(1, i, s), 0, 0)),
        ] + ([pl.BlockSpec((block, lanes), lambda i, s: (on(1, i, s), 0))] if final else [])
        return call(
            functools.partial(sweep_kernel, block=block, final=final), "sweep_last" if final else "sweep", (steps,),
            in_specs, out_specs, out_shape,
            (counts, field, field, field, rows_in, rows_in, *cols_in, *extra),
            scratch=[pltpu.VMEM(((block + 2) * levels, lanes), f32)], size=2 * state_bytes,
        )

    first_step, edge, ends = sweep(mixed, coeffs[0], sides, False)
    sides = to_columns(edge)

    returned = []
    for chunk in range(chunks):
        with_ends = chunk == 0
        part = call(
            functools.partial(legendre_kernel, wave_dev=wave_dev, first_wave=chunk * width, with_ends=with_ends),
            f"legendre_{chunk}", (width,),
            [
                pl.BlockSpec((1,) + legendre.shape[1:],
                             lambda i, s, chunk=chunk: (chunk * width + on(0, i, s), 0, 0)),
                pl.BlockSpec((n_row, 1, rows, lanes), lambda i, s: (0, on(0, i, s), 0, 0)),
            ] + ([pl.BlockSpec((2, levels, lanes), lambda i, s: (0, 0, 0)), anywhere] if with_ends else []),
            pl.BlockSpec((n_row, 1, rows, lanes), lambda i, s: (0, on(0, i, s), 0, 0)),
            sds((n_row, width, rows, lanes), bf16),
            (legendre, coeffs[chunk], *([ends, gap] if with_ends else [])),
            vmem=63, flops=4 * width * legendre.shape[1] * legendre.shape[2] * lanes,
            size=2 * width * legendre.shape[1] * legendre.shape[2],
        )
        returned.append(to_waves(part))

    (sea,) = sweep(first_step, returned[0], sides, True, (gap,))

    state = call(
        functools.partial(exit_kernel, chunks=chunks, block=block), "exit", (steps,),
        [pl.BlockSpec((tall, lanes), lambda i, s: (on(1, i, s), 0))]
        + [pl.BlockSpec((n_row, width, block, lanes), lambda i, s: (0, 0, on(0, i, s), 0))] * chunks,
        pl.BlockSpec((tall, lanes), lambda i, s: (i, 0)),
        sds((rows * levels, lanes), f32),
        (sea, *returned), scratch=[pltpu.VMEM((256, 256), bf16)], size=2 * state_bytes,
    )
    return state.reshape(model_state.shape), new_surface[None]


def solution(mesh):
    in_specs = (
        P("comp", "row", None, "col"),
        P("row", None, None),
        P("row"),
        P(),
        P("comp", "row", "col"),
        P("comp", "row", "col"),
        P("comp", "row", "col"),
    )
    out_specs = (P("comp", "row", None, "col"), P("comp", "row", "col"))
    return jax.shard_map(shards, mesh=mesh, in_specs=in_specs, out_specs=out_specs, check_vma=False)
```

time: 419 us -> 139 us (0.33)
  local copies, waits for them, and re-layouts: 300 us -> 4.11 us
  Pallas kernels: 0 us -> 76 us
  other arithmetic: 49.3 us -> 0 us
  matrix products: 33.7 us -> 0 us
  waiting for transfers between devices: 1.7 us -> 27.4 us
    gather x1 -> x0, local copies, waits for them, and re-layouts: 226 us -> none  [shards(): jnp.take(partner.reshape(-1), remap_source[0].reshape(-1))]
    pallas_call x0 -> x7, Pallas kernels: none -> 76 us  [call(): pl.pallas_call(functools.partial(kernel, n_row=n_row, n_col=n_col), out_s...]
    dot_general x2 -> x0, matrix products: 33.7 us -> none  [the longest x1 22.1 us: atmosphere(): jnp.einsum('wln,wnc->wlc', legendre, filtered, preferred_element_type=jnp...]
    slice x8 -> x0, local copies, waits for them, and re-layouts: 33 us -> none  [the longest x4 23.9 us: padded_2(): lax.slice_in_dim(block, 0, width, axis=dim)]
    all_to_all x2 -> x4, waiting for transfers between devices: 0.01 us -> 23.7 us  [to_waves(): return lax.all_to_all(x, 'row', split_axis=0, concat_axis=0, tiled=True)]
    mul x2 -> x0, other arithmetic: 20.9 us -> none  [the longest x1 20.8 us: advance_ocean(): padded = padded_2(water_column * current, (('row', 0), ('col', 2)), 1)]
    ppermute x4 -> x0, local copies, waits for them, and re-layouts: 19.5 us -> none  [the longest x2 9.77 us: padded_2(): lax.ppermute(lax.slice_in_dim(block, 0, width, axis=dim), axis, backward)]
    select_n x2 -> x0, other arithmetic: 16.5 us -> none  [the longest x1 15.6 us: shards(): result = jnp.where(group_index == 0, air_result, sea_result)]
  transfers between devices with their start and end apart: 11 -> 9, of which waited for: 1 -> 3; matrix products, arithmetic and copies ran while one was open for 82% -> 0% of each run, Pallas kernels for 0% -> 39%
where the time goes in v2:
time: 139 us; the launch traced here: 137 us
  Pallas kernels  76 us (55%)
  starting transfers between devices  29.2 us (21%)
  waiting for transfers between devices  27.4 us (20%)
  local copies, waits for them, and re-layouts  4.11 us (3%)
    pallas_call x7, Pallas kernels, call(): pl.pallas_call(functools.partial(kernel, n_row=n_row, n_col=n_col), out_s...  76 us
    all_to_all x4, waiting for transfers between devices, to_waves(): return lax.all_to_all(x, 'row', split_axis=0, concat_axis=0, tiled=True)  23.7 us
    all_to_all x4, starting transfers between devices, to_waves(): return lax.all_to_all(x, 'row', split_axis=0, concat_axis=0, tiled=True)  20.2 us
    ppermute x2, starting transfers between devices, to_columns(): lax.ppermute(x, 'col', ahead)  6.4 us
    unnamed x20, local copies, waits for them, and re-layouts  4.11 us
    ppermute x2, waiting for transfers between devices, to_columns(): lax.ppermute(x, 'col', [(b, a) for a, b in ahead])  3.72 us
  transfers between devices with their start and end apart: 9, of which 3 were waited for; matrix products, arithmetic and copies ran while one was open for 0% of the time, Pallas kernels for 39%

profile of v2, /device:TPU:7, one launch (start us, length us, event | category | flops | bytes accessed | tf_op | source)
XLA Modules:
  0.0 137.5 jit_solution(12756601322705490216)
XLA Ops:
  0.6 15.3 %entry.1 = (bf16[4,4,320,128]{3,2,1,0:T(8,128)(2,1)}, bf16[4,4,320,128]{3,2,1,0:T(8,128)(2,1)}, f32[10240,128]{1,0:T(8,128)}, bf16[5,32,128]{2,1,0:T(8,128)(2,1)}) custom-call(s32[1]{0:T(128)} %bitcast.place, s32[1,320]{1,0:T(1,128)} %bitcast.10, f32[10240,128]{1,0:T(8,128)} %bitcast.7, f32[10240,128]{1,0:T(8,128)} %bitcast.8, f32[320]{0:T(512)} %gauss.1, ...), custom_call_target="tpu_custom_call" | custom-call | flops 10000000 | bytes 10485760 | tf_op jit(solution)/shard_map/entry/pallas_call | solution.py:400
  16.0 4.4 %all-to-all-start = ((bf16[4,4,320,128]{3,2,1,0:T(8,128)(2,1)}), bf16[4,4,320,128]{3,2,1,0:T(8,128)(2,1)S(1)}, u32[]{:S(2)}, u32[]{:S(2)}) async-start(bf16[4,4,320,128]{3,2,1,0:T(8,128)(2,1)} %get-tuple-element.12), calls=%async_computation | async-start | bytes 2621440 | tf_op jit(solution)/shard_map/all_to_all | solution.py:436
  20.4 3.2 %collective-permute-start.1 = (bf16[5,32,128]{2,1,0:T(8,128)(2,1)S(1)}, bf16[5,32,128]{2,1,0:T(8,128)(2,1)S(1)}, u32[]{:S(2)}, u32[]{:S(2)}) collective-permute-start(bf16[5,32,128]{2,1,0:T(8,128)(2,1)S(1)} %copy-done.9), channel_id=1, source_target_pairs={{0,1},{1,2},{2,3},{4,5},{5,6},{6,7},{8,9},{9,10},{10,11},{12,13},{... | collective-permute-start | bytes 122888 | tf_op jit(solution)/shard_map/ppermute | solution.py:441
  23.6 1.3 collective-permute-start
  24.9 10.9 %all-to-all-done.halo_up.halo_down.coeffs = bf16[4,4,320,128]{3,2,1,0:T(8,128)(2,1)S(1)} async-done(((bf16[4,4,320,128]{3,2,1,0:T(8,128)(2,1)}), bf16[4,4,320,128]{3,2,1,0:T(8,128)(2,1)S(1)}, u32[]{:S(2)}, u32[]{:S(2)}) %all-to-all-start) | async-done | bytes 1310752 | tf_op jit(solution)/shard_map/all_to_all | solution.py:436
  35.8 1.2 copy-done
  37.0 6.1 %all-to-all-start.2 = ((bf16[4,4,320,128]{3,2,1,0:T(8,128)(2,1)}), bf16[4,4,320,128]{3,2,1,0:T(8,128)(2,1)}, u32[]{:S(2)}, u32[]{:S(2)}) async-start(bf16[4,4,320,128]{3,2,1,0:T(8,128)(2,1)} %get-tuple-element.18), calls=%async_computation.2 | async-start | bytes 2621440 | tf_op jit(solution)/shard_map/all_to_all | solution.py:436
  43.1 0.7 copy-done.7
  43.8 16.6 %surface.1 = (f32[320,128]{1,0:T(8,128)}, f32[320,128]{1,0:T(8,128)}) custom-call(s32[1]{0:T(128)} %bitcast.place, s32[1,320]{1,0:T(1,128)} %bitcast.11, f32[320,128]{1,0:T(8,128)} %copy-done.7, f32[320,128]{1,0:T(8,128)} %bitcast.14, s32[320,128]{1,0:T(8,128)} %bitcast.16, bf16[5,32,128]{2,1,0:T(8,128)(2,1)} %get-tuple-element.13._), custom_call_target="tpu_custom_call" | custom-call | flops 20000000000 | bytes 819200 | tf_op jit(solution)/shard_map/surface/pallas_call | solution.py:400
  60.3 0.6 copy-done.2
  60.9 0.0 copy-done.3
  61.0 19.0 %sweep.1 = (f32[10240,128]{1,0:T(8,128)}, bf16[5,32,128]{2,1,0:T(8,128)(2,1)}, bf16[2,32,128]{2,1,0:T(8,128)(2,1)}) custom-call(s32[1]{0:T(128)} %bitcast.place, s32[1,320]{1,0:T(1,128)} %bitcast.12, f32[10240,128]{1,0:T(8,128)} %get-tuple-element.11.field.above.below, f32[10240,128]{1,0:T(8,128)} %get-tuple-element.11.field.above.below, ...), custom_call_target="tpu_custom_call" | custom-call | flops 10000000 | bytes 10485760 | tf_op jit(solution)/shard_map/sweep/pallas_call | solution.py:400
  80.0 3.0 %legendre_0.1 = bf16[4,4,320,128]{3,2,1,0:T(8,128)(2,1)} custom-call(s32[1]{0:T(128)} %bitcast.place, bf16[8,1280,1280]{2,1,0:T(8,128)(2,1)} %legendre.3, bf16[4,4,320,128]{3,2,1,0:T(8,128)(2,1)} %copy-done, bf16[2,32,128]{2,1,0:T(8,128)(2,1)} %get-tuple-element.15.rest_0_, f32[320,128]{1,0:T(8,128)} %get-tuple-element.16.rest_1_.rest_0_), custom_call_target="tpu_custom_call" | custom-call | flops 3355443200 | bytes 13107200 | tf_op jit(solution)/shard_map/legendre_0/pallas_call | solution.py:400
  82.9 4.3 %all-to-all-start.1 = ((bf16[4,4,320,128]{3,2,1,0:T(8,128)(2,1)}), bf16[4,4,320,128]{3,2,1,0:T(8,128)(2,1)}, u32[]{:S(2)}, u32[]{:S(2)}) async-start(bf16[4,4,320,128]{3,2,1,0:T(8,128)(2,1)} %legendre_0.1), calls=%async_computation.1 | async-start | bytes 2621440 | tf_op jit(solution)/shard_map/all_to_all | solution.py:436
  87.2 2.7 %legendre_1.1 = bf16[4,4,320,128]{3,2,1,0:T(8,128)(2,1)} custom-call(s32[1]{0:T(128)} %bitcast.place, bf16[8,1280,1280]{2,1,0:T(8,128)(2,1)} %legendre.3, bf16[4,4,320,128]{3,2,1,0:T(8,128)(2,1)} %all-to-all-done.2.coeffs), custom_call_target="tpu_custom_call" | custom-call | flops 3355443200 | bytes 13107200 | tf_op jit(solution)/shard_map/legendre_1/pallas_call | solution.py:400
  89.9 12.8 %all-to-all-done.1.halo_up.halo_down.rest_0_ = bf16[4,4,320,128]{3,2,1,0:T(8,128)(2,1)} async-done(((bf16[4,4,320,128]{3,2,1,0:T(8,128)(2,1)}), bf16[4,4,320,128]{3,2,1,0:T(8,128)(2,1)}, u32[]{:S(2)}, u32[]{:S(2)}) %all-to-all-start.1) | async-done | bytes 1310752 | tf_op jit(solution)/shard_map/all_to_all | solution.py:436
  102.7 5.4 %all-to-all-start.3 = ((bf16[4,4,320,128]{3,2,1,0:T(8,128)(2,1)}), bf16[4,4,320,128]{3,2,1,0:T(8,128)(2,1)S(1)}, u32[]{:S(2)}, u32[]{:S(2)}) async-start(bf16[4,4,320,128]{3,2,1,0:T(8,128)(2,1)} %legendre_1.1), calls=%async_computation.3 | async-start | bytes 2621440 | tf_op jit(solution)/shard_map/all_to_all | solution.py:436
  108.1 3.2 %collective-permute-start.4 = (bf16[5,32,128]{2,1,0:T(8,128)(2,1)S(1)}, bf16[5,32,128]{2,1,0:T(8,128)(2,1)S(1)}, u32[]{:S(2)}, u32[]{:S(2)}) collective-permute-start(bf16[5,32,128]{2,1,0:T(8,128)(2,1)S(1)} %copy-done.8), channel_id=1, source_target_pairs={{0,1},{1,2},{2,3},{4,5},{5,6},{6,7},{8,9},{9,10},{10,11},{12,13},{... | collective-permute-start | bytes 122888 | tf_op jit(solution)/shard_map/ppermute | solution.py:441
  111.3 1.3 collective-permute-start.3
  112.6 3.7 %collective-permute-done.3.east_in = bf16[5,32,128]{2,1,0:T(8,128)(2,1)S(1)} collective-permute-done((bf16[5,32,128]{2,1,0:T(8,128)(2,1)S(1)}, bf16[5,32,128]{2,1,0:T(8,128)(2,1)S(1)}, u32[]{:S(2)}, u32[]{:S(2)}) %collective-permute-start.3) | collective-permute-done | bytes 40992 | tf_op jit(solution)/shard_map/ppermute | solution.py:441
  116.3 0.6 copy-done.5
  117.0 12.8 %sweep_last.1.sea = f32[10240,128]{1,0:T(8,128)} custom-call(s32[1]{0:T(128)} %bitcast.place, s32[1,320]{1,0:T(1,128)} %bitcast.13, f32[10240,128]{1,0:T(8,128)} %get-tuple-element.14.field.above.below, f32[10240,128]{1,0:T(8,128)} %get-tuple-element.14.field.above.below, f32[10240,128]{1,0:T(8,128)} %get-tuple-element.14.field.above.below, ...), custom_call_target="tpu_custom_call" | custom-call | flops 10000000 | bytes 10485760 | tf_op jit(solution)/shard_map/sweep_last/pallas_call | solution.py:400
  129.8 1.1 copy-done.1
  130.9 6.6 %exit.1 = f32[10240,128]{1,0:T(8,128)} custom-call(s32[1]{0:T(128)} %bitcast.place, f32[10240,128]{1,0:T(8,128)} %sweep_last.1.sea, bf16[4,4,320,128]{3,2,1,0:T(8,128)(2,1)} %all-to-all-done.1.halo_up.halo_down.rest_0_, bf16[4,4,320,128]{3,2,1,0:T(8,128)(2,1)} %copy-done.1), custom_call_target="tpu_custom_call" | custom-call | flops 10000000 | bytes 10485760 | tf_op jit(solution)/shard_map/exit/pallas_call | solution.py:400
  (21 shorter events, 0.0 us)
Async XLA Ops:
  16.0 4.5 %copy-start.6 = (f32[1,320,128]{2,1,0:T(8,128)S(1)}, f32[1,320,128]{2,1,0:T(8,128)}, u32[]{:S(2)}) copy-start(f32[1,320,128]{2,1,0:T(8,128)} %param.11) | copy-start | bytes 491524
  16.0 4.5 %copy-start.9 = (bf16[5,32,128]{2,1,0:T(8,128)(2,1)S(1)}, bf16[5,32,128]{2,1,0:T(8,128)(2,1)}, u32[]{:S(2)}) copy-start(bf16[5,32,128]{2,1,0:T(8,128)(2,1)} %get-tuple-element.13._) | copy-start | bytes 122884
  16.0 19.8 %all-to-all-start = ((bf16[4,4,320,128]{3,2,1,0:T(8,128)(2,1)}), bf16[4,4,320,128]{3,2,1,0:T(8,128)(2,1)S(1)}, u32[]{:S(2)}, u32[]{:S(2)}) async-start(bf16[4,4,320,128]{3,2,1,0:T(8,128)(2,1)} %get-tuple-element.12), calls=%async_computation | async-start | bytes 2621440 | tf_op jit(solution)/shard_map/all_to_all | solution.py:436
  20.4 22.7 %collective-permute-start.2 = (f32[320,128]{1,0:T(8,128)S(1)}, f32[320,128]{1,0:T(8,128)S(1)}, u32[]{:S(2)}, u32[]{:S(2)}) collective-permute-start(f32[320,128]{1,0:T(8,128)S(1)} %bitcast.15), channel_id=1, source_target_pairs={{0,16},{16,0},{1,17},{17,1},{2,18},{18,2},{3,19},{19,3},{4,20},{20... | collective-permute-start | bytes 491528 | tf_op jit(solution)/shard_map/ppermute | solution.py:391
  20.4 39.9 %collective-permute-start.1 = (bf16[5,32,128]{2,1,0:T(8,128)(2,1)S(1)}, bf16[5,32,128]{2,1,0:T(8,128)(2,1)S(1)}, u32[]{:S(2)}, u32[]{:S(2)}) collective-permute-start(bf16[5,32,128]{2,1,0:T(8,128)(2,1)S(1)} %copy-done.9), channel_id=1, source_target_pairs={{0,1},{1,2},{2,3},{4,5},{5,6},{6,7},{8,9},{9,10},{10,11},{12,13},{... | collective-permute-start | bytes 122888 | tf_op jit(solution)/shard_map/ppermute | solution.py:441
  23.6 36.7 %collective-permute-start = (bf16[5,32,128]{2,1,0:T(8,128)(2,1)S(1)}, bf16[5,32,128]{2,1,0:T(8,128)(2,1)S(1)}, u32[]{:S(2)}, u32[]{:S(2)}) collective-permute-start(bf16[5,32,128]{2,1,0:T(8,128)(2,1)S(1)} %copy-done.9), channel_id=1, source_target_pairs={{1,0},{2,1},{3,2},{5,4},{6,5},{7,6},{9,8},{10,9},{11,10},{13,12},{... | collective-permute-start | bytes 122888 | tf_op jit(solution)/shard_map/ppermute | solution.py:441
  35.8 1.2 copy-start
  37.0 45.9 %all-to-all-start.2 = ((bf16[4,4,320,128]{3,2,1,0:T(8,128)(2,1)}), bf16[4,4,320,128]{3,2,1,0:T(8,128)(2,1)}, u32[]{:S(2)}, u32[]{:S(2)}) async-start(bf16[4,4,320,128]{3,2,1,0:T(8,128)(2,1)} %get-tuple-element.18), calls=%async_computation.2 | async-start | bytes 2621440 | tf_op jit(solution)/shard_map/all_to_all | solution.py:436
  43.1 0.7 copy-start.7
  60.3 0.6 copy-start.2
  60.3 0.6 copy-start.3
  82.9 19.8 %all-to-all-start.1 = ((bf16[4,4,320,128]{3,2,1,0:T(8,128)(2,1)}), bf16[4,4,320,128]{3,2,1,0:T(8,128)(2,1)}, u32[]{:S(2)}, u32[]{:S(2)}) async-start(bf16[4,4,320,128]{3,2,1,0:T(8,128)(2,1)} %legendre_0.1), calls=%async_computation.1 | async-start | bytes 2621440 | tf_op jit(solution)/shard_map/all_to_all | solution.py:436
  89.9 18.2 %copy-start.8 = (bf16[5,32,128]{2,1,0:T(8,128)(2,1)S(1)}, bf16[5,32,128]{2,1,0:T(8,128)(2,1)}, u32[]{:S(2)}) copy-start(bf16[5,32,128]{2,1,0:T(8,128)(2,1)} %get-tuple-element.17) | copy-start | bytes 122884
  102.7 27.1 %all-to-all-start.3 = ((bf16[4,4,320,128]{3,2,1,0:T(8,128)(2,1)}), bf16[4,4,320,128]{3,2,1,0:T(8,128)(2,1)S(1)}, u32[]{:S(2)}, u32[]{:S(2)}) async-start(bf16[4,4,320,128]{3,2,1,0:T(8,128)(2,1)} %legendre_1.1), calls=%async_computation.3 | async-start | bytes 2621440 | tf_op jit(solution)/shard_map/all_to_all | solution.py:436
  108.1 4.5 %collective-permute-start.4 = (bf16[5,32,128]{2,1,0:T(8,128)(2,1)S(1)}, bf16[5,32,128]{2,1,0:T(8,128)(2,1)S(1)}, u32[]{:S(2)}, u32[]{:S(2)}) collective-permute-start(bf16[5,32,128]{2,1,0:T(8,128)(2,1)S(1)} %copy-done.8), channel_id=1, source_target_pairs={{0,1},{1,2},{2,3},{4,5},{5,6},{6,7},{8,9},{9,10},{10,11},{12,13},{... | collective-permute-start | bytes 122888 | tf_op jit(solution)/shard_map/ppermute | solution.py:441
  111.3 5.0 %collective-permute-start.3 = (bf16[5,32,128]{2,1,0:T(8,128)(2,1)S(1)}, bf16[5,32,128]{2,1,0:T(8,128)(2,1)S(1)}, u32[]{:S(2)}, u32[]{:S(2)}) collective-permute-start(bf16[5,32,128]{2,1,0:T(8,128)(2,1)S(1)} %copy-done.8), channel_id=1, source_target_pairs={{1,0},{2,1},{3,2},{5,4},{6,5},{7,6},{9,8},{10,9},{11,10},{13,12},{... | collective-permute-start | bytes 122888 | tf_op jit(solution)/shard_map/ppermute | solution.py:441
  112.6 3.7 %copy-start.4 = (bf16[5,32,128]{2,1,0:T(8,128)(2,1)}, bf16[5,32,128]{2,1,0:T(8,128)(2,1)S(1)}, u32[]{:S(2)}) copy-start(bf16[5,32,128]{2,1,0:T(8,128)(2,1)S(1)} %collective-permute-done.4.west_in) | copy-start | bytes 122884
  116.3 0.6 copy-start.5
  129.8 1.1 copy-start.1

commit v3 on v2

--- a/solution.py
+++ b/solution.py
@@ -7,8 +7,13 @@
 from jax.experimental.pallas import tpu as pltpu
 from jax.sharding import PartitionSpec as P
 
+
 diffusion_rate = 0.2
 lanes = 128
+
+
+def chunk_count(wave_dev):
+    return 2 if wave_dev % 2 == 0 else 1
 
 
 def row_block(rows):
@@ -36,9 +41,9 @@
     return jnp.where(mask, 1.0, 0.0).astype(jnp.bfloat16)
 
 
-def swap_matrix():
+def swap_matrix(flip_high, flip_low):
     row, column = iota((256, 256), 0), iota((256, 256), 1)
-    return as_bf16(column == ((row & 15) << 4 | row >> 4))
+    return as_bf16(column == (((row & 15) ^ flip_low) << 4 | ((row >> 4) ^ flip_high)))
 
 
 def spread_matrix():
@@ -68,46 +73,48 @@
 
 
 def entry_kernel(place, counts, field, last, gauss, mix, *rest, n_row, n_col, chunks, block):
-    send = rest[:chunks]
-    mixed, edge, table = rest[chunks:]
+    send = [rest[n_row * c:n_row * (c + 1)] for c in range(chunks)]
+    mixed, edge, table = rest[n_row * chunks:]
     comp, row, _ = where_am_i(place, n_row, n_col)
     levels = field.shape[0] // block
     wave_dev = levels // n_row
     width = wave_dev // chunks
     step = pl.program_id(0)
 
+    flip = row * wave_dev
+
     def target(wave):
-        dest, local = divmod(wave, wave_dev)
+        part, local = divmod(wave, wave_dev)
         chunk, slot = divmod(local, width)
-        return send[chunk], dest, slot
+        return send[chunk][part], slot
 
     @pl.when(comp == 0)
     def _():
         @pl.when(step == 0)
         def _():
-            table[...] = swap_matrix()
+            table[...] = swap_matrix(flip & 15, 0)
 
         for lat in range(0, block - 15, 16):
             halves = []
             for half in range(0, levels, 16):
                 halves.append(jnp.concatenate([
-                    (field[(lat + s) * levels + half:(lat + s) * levels + half + 16, :]
+                    (field[pl.ds(pl.multiple_of((lat + s) * levels + (half ^ (flip & ~15)), 16), 16), :]
                      * gauss[step * block + lat + s]).astype(jnp.bfloat16)
                     for s in range(16)
                 ], axis=0))
             turned = product(table[...], jnp.concatenate(halves, axis=1)).astype(jnp.bfloat16)
             for wave in range(levels):
-                out, dest, slot = target(wave)
+                out, slot = target(wave)
                 part = lanes * (wave // 16)
-                out[dest, slot, lat:lat + 16, :] = turned[16 * (wave % 16):16 * (wave % 16) + 16, part:part + lanes]
+                out[slot, lat:lat + 16, :] = turned[16 * (wave % 16):16 * (wave % 16) + 16, part:part + lanes]
         for lat in range(block - block % 16, block, 8):
             weight = jnp.zeros((8, lanes), jnp.float32)
             for s in range(8):
                 weight = jnp.where(iota((8, lanes), 0) == s, gauss[step * block + lat + s], weight)
             for wave in range(levels):
-                out, dest, slot = target(wave)
-                values = field[pl.ds(lat * levels + wave, 8, stride=levels), :] * weight
-                out[dest, slot, lat:lat + 8, :] = values.astype(jnp.bfloat16)
+                out, slot = target(wave)
+                values = field[pl.ds(lat * levels + (wave ^ flip), 8, stride=levels), :] * weight
+                out[slot, lat:lat + 8, :] = values.astype(jnp.bfloat16)
 
     def mixed_rows(ref, start, first_row):
         values = []
@@ -146,17 +153,22 @@
         spread = spread_matrix()
         pair_of = iota((levels, lanes), 1) >> 1
 
+        batch = 32 if block % 32 == 0 else 8
+
         def body(g, packed):
-            start = pl.multiple_of(g * 8 * levels, 8 * levels)
-            rows = mixed_rows(field, start, step * block + g * 8)
-            for s, (value, _) in enumerate(rows):
-                mixed[pl.ds(pl.multiple_of(start + s * levels, levels), levels), :] = value
+            rows = []
+            for first in range(0, batch, 8):
+                start = pl.multiple_of((g * batch + first) * levels, 8 * levels)
+                some = mixed_rows(field, start, step * block + g * batch + first)
+                for s, (value, _) in enumerate(some):
+                    mixed[pl.ds(pl.multiple_of(start + s * levels, levels), levels), :] = value
+                rows += some
             ends = product(jnp.concatenate([r[1] for r in rows], axis=0), spread)
-            for s in range(8):
-                packed = jnp.where(pair_of == g * 8 + s, ends[s * levels:(s + 1) * levels], packed)
+            for s in range(batch):
+                packed = jnp.where(pair_of == g * batch + s, ends[s * levels:(s + 1) * levels], packed)
             return packed
 
-        packed = lax.fori_loop(0, block // 8, body, jnp.zeros((levels, lanes), jnp.float32))
+        packed = lax.fori_loop(0, block // batch, body, jnp.zeros((levels, lanes), jnp.float32))
         edge[0] = packed.astype(jnp.bfloat16)
 
         @pl.when(step == 0)
@@ -164,12 +176,12 @@
             total = pl.num_programs(0) * block
             top = mixed_rows(field, 0, 0)[0][1]
             low = mixed_rows(last, 0, total - 8)[-1][1]
-            for dest in range(n_row):
-                send[0][dest, 0, 0:levels, :] = jnp.where(dest > row, low, top)
-
-
-def sweep_kernel(place, counts, field, above, below, halo_up, halo_down, east_in, west_in, *rest,
-                 block, n_row, n_col, final):
+            for part in range(1, n_row):
+                send[0][part][0, 0:levels, :] = jnp.where((part ^ row) > row, low, top)
+
+
+def sweep_kernel(place, counts, field, above, below, east_in, west_in, *rest, block, n_row, n_col, near_parts, final):
+    halos, rest = rest[:len(near_parts)], rest[len(near_parts):]
     if final:
         gap, out, masked = rest
     else:
@@ -181,6 +193,7 @@
     rows = steps * block
     base = step * block
     shape = (levels, lanes)
+    batch = 32 if block % 32 == 0 else 8
 
     @pl.when(comp != 0)
     def _():
@@ -193,15 +206,19 @@
         def at(y):
             return pl.ds(pl.multiple_of(y * levels, levels), levels)
 
+        def halo(neighbour):
+            found = jnp.zeros(shape, jnp.float32)
+            inside = (neighbour >= 0) & (neighbour < n_row)
+            for part, ref in zip(near_parts, halos):
+                found = jnp.where(inside & ((neighbour ^ row) == part), ref[0].astype(jnp.float32), found)
+            return found
+
         west = jnp.where(col > 0, west_in[0].astype(jnp.float32), 0.0)
         east = jnp.where(col < n_col - 1, east_in[0].astype(jnp.float32), 0.0)
         sides = jnp.where((lane & 1) == 0, pltpu.roll(east, lanes - 1, 1), pltpu.roll(west, 1, 1))
-        masked[0:levels, :] = jnp.where(
-            step > 0, jnp.where(sea_of(base - 1), above[...], 0.0),
-            jnp.where(row > 0, halo_up[0, 0].astype(jnp.float32), 0.0))
+        masked[0:levels, :] = jnp.where(step > 0, jnp.where(sea_of(base - 1), above[...], 0.0), halo(row - 1))
         masked[(block + 1) * levels:(block + 2) * levels, :] = jnp.where(
-            step < steps - 1, jnp.where(sea_of(base + block), below[...], 0.0),
-            jnp.where(row < n_row - 1, halo_down[0, 0].astype(jnp.float32), 0.0))
+            step < steps - 1, jnp.where(sea_of(base + block), below[...], 0.0), halo(row + 1))
 
         def fill(g, carry):
             for s in range(8):
@@ -211,38 +228,34 @@
 
         lax.fori_loop(0, block // 8, fill, 0)
         beside = beside_matrix()
-        if final:
-            weights = jnp.concatenate([beside, side_matrix()], axis=0)
-        else:
-            spread = spread_matrix()
+        weights = jnp.concatenate([beside, side_matrix(), beside], axis=0)
+        spread = spread_matrix()
 
         def body(g, packed):
-            here = masked[pl.ds(pl.multiple_of((g * 8 + 1) * levels, levels), 8 * levels), :]
+            here = masked[pl.ds(pl.multiple_of((g * batch + 1) * levels, levels), batch * levels), :]
             high, low = split(here)
             turned = jnp.concatenate(
-                [jnp.where(pair_of == g * 8 + s, sides, 0.0).astype(jnp.bfloat16) for s in range(8)], axis=0)
-            both = jnp.concatenate([beside, side_matrix()], axis=0) if not final else weights
-            near = product(jnp.concatenate([high, turned], axis=1), both) + product(low, beside)
+                [jnp.where(pair_of == g * batch + s, sides, 0.0).astype(jnp.bfloat16) for s in range(batch)], axis=0)
+            near = product(jnp.concatenate([high, turned, low], axis=1), weights)
             new_rows = []
-            for s in range(8):
-                y = g * 8 + s
+            for s in range(batch):
+                y = g * batch + s
                 part = slice(s * levels, (s + 1) * levels)
-                lap = masked[at(y), :] + masked[at(y + 2), :] + near[part] - 4.0 * here[part]
+                lap = masked[at(y), :] + masked[at(y + 2), :] + near[part] - 4.0 * masked[at(y + 1), :]
                 sea = sea_of(base + y)
                 new = field[at(y), :] + jnp.where(sea, diffusion_rate * lap, 0.0)
                 out[at(y), :] = new
                 if final:
-                    start = y * levels
-                    out[pl.ds(start, 1), :] = new[0:1, :] + 0.3 * gap[pl.ds(y, 1), :]
+                    out[pl.ds(y * levels, 1), :] = new[0:1, :] + 0.3 * gap[pl.ds(y, 1), :]
                 else:
                     new_rows.append(jnp.where(sea, new, 0.0).astype(jnp.bfloat16))
             if not final:
                 spreads = product(jnp.concatenate(new_rows, axis=0), spread)
-                for s in range(8):
-                    packed = jnp.where(pair_of == g * 8 + s, spreads[s * levels:(s + 1) * levels], packed)
+                for s in range(batch):
+                    packed = jnp.where(pair_of == g * batch + s, spreads[s * levels:(s + 1) * levels], packed)
             return packed
 
-        packed = lax.fori_loop(0, block // 8, body, jnp.zeros(shape, jnp.float32))
+        packed = lax.fori_loop(0, block // batch, body, jnp.zeros(shape, jnp.float32))
         if not final:
             edge[0] = packed.astype(jnp.bfloat16)
 
@@ -257,20 +270,22 @@
                 ).astype(jnp.bfloat16)
 
 
-def legendre_kernel(place, legendre, coeffs, *rest, n_row, n_col, wave_dev, first_wave, with_ends):
+def legendre_kernel(place, legendre, *rest, n_row, n_col, wave_dev, first_wave, with_ends):
+    coeffs, rest = rest[:n_row], rest[n_row:]
     if with_ends:
-        ends, _, out = rest
-    else:
-        (out,) = rest
+        ends, rest = rest[0], rest[2:]
+    out, gathered = rest[:n_row], rest[n_row]
     comp, row, _ = where_am_i(place, n_row, n_col)
     index = pl.program_id(0)
-    lats = coeffs.shape[2]
+    lats = coeffs[0].shape[1]
     count = legendre.shape[2]
 
     @pl.when(comp == 0)
     def _():
         table = legendre[0]
-        fourier = coeffs[:, 0].reshape(n_row * lats, lanes)
+        for part in range(n_row):
+            gathered[part ^ row] = coeffs[part][0]
+        fourier = gathered[...].reshape(n_row * lats, lanes)
         spectral = lax.dot_general(fourier, table, (((0,), (0,)), ((), ())), preferred_element_type=jnp.float32)
         wave = row * wave_dev + first_wave + index
         total = (wave + iota((1, count), 1)).astype(jnp.float32)
@@ -278,14 +293,16 @@
         damping = 1.0 / (1.0 + 20.0 * ratio * ratio)
         filtered = (spectral * damping).astype(jnp.bfloat16)
         result = lax.dot_general(table, filtered, (((1,), (1,)), ((), ())), preferred_element_type=jnp.float32)
-        out[:, 0] = result.astype(jnp.bfloat16).reshape(n_row, lats, lanes)
+        gathered[...] = result.astype(jnp.bfloat16).reshape(n_row, lats, lanes)
+        for part in range(n_row):
+            out[part][0] = gathered[part ^ row]
 
     if with_ends:
         @pl.when((comp != 0) & (index == 0))
         def _():
             levels = ends.shape[1]
-            for dest in range(n_row):
-                out[dest, 0, 0:levels, :] = jnp.where(dest > row, ends[1], ends[0])
+            for part in range(1, n_row):
+                out[part][0, 0:levels, :] = jnp.where((part ^ row) > row, ends[1], ends[0])
 
 
 def surface_kernel(place, counts, partner, own, source, _, new, gap, *, group, n_row, n_col):
@@ -334,22 +351,25 @@
 
 
 def exit_kernel(place, sea, *rest, n_row, n_col, chunks, block):
-    back, out, table = rest[:chunks], rest[chunks], rest[chunks + 1]
-    comp, _, _ = where_am_i(place, n_row, n_col)
+    back = [rest[n_row * c:n_row * (c + 1)] for c in range(chunks)]
+    out, table = rest[n_row * chunks:]
+    comp, row, _ = where_am_i(place, n_row, n_col)
     levels = out.shape[0] // block
     wave_dev = levels // n_row
     width = wave_dev // chunks
 
+    flip = row * wave_dev
+
     def source(wave, lat, count):
-        origin, local = divmod(wave, wave_dev)
+        part, local = divmod(wave, wave_dev)
         chunk, slot = divmod(local, width)
-        return back[chunk][origin, slot, lat:lat + count, :]
+        return back[chunk][part][slot, lat:lat + count, :]
 
     @pl.when(comp == 0)
     def _():
         @pl.when(pl.program_id(0) == 0)
         def _():
-            table[...] = swap_matrix()
+            table[...] = swap_matrix(0, flip & 15)
 
         for lat in range(0, block - 15, 16):
             halves = [
@@ -359,12 +379,12 @@
             turned = product(table[...], jnp.concatenate(halves, axis=1))
             for s in range(16):
                 for half in range(0, levels, 16):
-                    start = (lat + s) * levels + half
+                    start = pl.multiple_of((lat + s) * levels + (half ^ (flip & ~15)), 16)
                     part = lanes * (half // 16)
-                    out[start:start + 16, :] = turned[16 * s:16 * s + 16, part:part + lanes]
+                    out[pl.ds(start, 16), :] = turned[16 * s:16 * s + 16, part:part + lanes]
         for lat in range(block - block % 16, block, 8):
             for wave in range(levels):
-                out[pl.ds(lat * levels + wave, 8, stride=levels), :] = source(wave, lat, 8).astype(jnp.float32)
+                out[pl.ds(lat * levels + (wave ^ flip), 8, stride=levels), :] = source(wave, lat, 8).astype(jnp.float32)
 
     @pl.when(comp != 0)
     def _():
@@ -375,7 +395,7 @@
     n_row, n_col = lax.axis_size("row"), lax.axis_size("col")
     rows, levels = model_state.shape[1], model_state.shape[2]
     wave_dev = levels // n_row
-    chunks = 2 if wave_dev % 2 == 0 else 1
+    chunks = chunk_count(wave_dev)
     width = wave_dev // chunks
     block = row_block(rows)
     steps = rows // block
@@ -393,17 +413,13 @@
     def on(comp, i, s):
         return jnp.where(lax.div(s[0], n_row * n_col) == comp, i, 0)
 
-    def row_of(s):
-        return lax.rem(lax.div(s[0], n_col), n_row)
-
-    def call(kernel, name, grid, in_specs, out_specs, out_shape, args, scratch=(), vmem=59, flops=10**7, size=0):
+    def call(kernel, grid, in_specs, out_specs, out_shape, args, scratch=(), vmem=59, flops=10**7, size=0):
         return pl.pallas_call(
             functools.partial(kernel, n_row=n_row, n_col=n_col),
             out_shape=out_shape,
             grid_spec=pltpu.PrefetchScalarGridSpec(
                 num_scalar_prefetch=1, grid=grid, in_specs=in_specs, out_specs=out_specs, scratch_shapes=scratch),
             compiler_params=pltpu.CompilerParams(vmem_limit_bytes=vmem * mib),
-            name=name,
             cost_estimate=cost(flops, size),
         )(place, *args)
 
@@ -413,7 +429,7 @@
     tall = block * levels
 
     *send, mixed, edge = call(
-        functools.partial(entry_kernel, chunks=chunks, block=block), "entry", (steps,),
+        functools.partial(entry_kernel, chunks=chunks, block=block), (steps,),
         [
             smem,
             pl.BlockSpec((tall, lanes), lambda i, s: (i, 0)),
@@ -421,34 +437,42 @@
             smem,
             pl.BlockSpec((levels, levels), lambda i, s: (0, 0)),
         ],
-        [pl.BlockSpec((n_row, width, block, lanes), lambda i, s: (0, 0, i, 0))] * chunks
+        [pl.BlockSpec((width, block, lanes), lambda i, s: (0, i, 0))] * (chunks * n_row)
         + [
             pl.BlockSpec((tall, lanes), lambda i, s: (on(1, i, s), 0)),
             pl.BlockSpec((1, levels, lanes), lambda i, s: (on(1, i, s), 0, 0)),
         ],
-        [sds((n_row, width, rows, lanes), bf16)] * chunks
+        [sds((width, rows, lanes), bf16)] * (chunks * n_row)
         + [sds((rows * levels, lanes), f32), sds((steps, levels, lanes), bf16)],
         (counts, fields, fields, gauss_weight, mixing),
         scratch=[pltpu.VMEM((256, 256), bf16)], vmem=63, size=2 * state_bytes,
     )
 
-    def to_waves(x):
-        return lax.all_to_all(x, "row", split_axis=0, concat_axis=0, tiled=True)
-
-    ahead = [(i, i + 1) for i in range(n_col - 1)]
+    def traded(parts):
+        got = [parts[0]]
+        for k in range(1, n_row):
+            got.append(lax.ppermute(parts[k], "row", [(r, r ^ k) for r in range(n_row)]))
+        return got
+
+    chain = [n_col + i for i in range(n_col - 1)]
 
     def to_columns(x):
-        return [lax.ppermute(x, "col", [(b, a) for a, b in ahead]), lax.ppermute(x, "col", ahead)]
-
-    coeffs = [to_waves(x) for x in send]
+        return [
+            lax.ppermute(x, ("comp", "col"), [(i + 1, i) for i in chain]),
+            lax.ppermute(x, ("comp", "col"), [(i, i + 1) for i in chain]),
+        ]
+
+    coeffs = [traded(send[n_row * c:n_row * (c + 1)]) for c in range(chunks)]
     sides = to_columns(edge)
 
     whole = pl.BlockSpec((rows, lanes), lambda i, s: (0, 0))
     new_surface, gap = call(
-        functools.partial(surface_kernel, group=2), "surface", (1,),
+        functools.partial(surface_kernel, group=2), (1,),
         [smem, whole, whole, whole, anywhere], [whole] * 2, [sds((rows, lanes), f32)] * 2,
         (counts, partner, own, remap_source[0], edge), flops=2 * 10**10, size=5 * 4 * rows * lanes,
     )
+
+    near_parts = [k for k in range(1, n_row) if k & (k + 1) == 0]
 
     def sweep(field, rows_in, cols_in, final, extra=()):
         out_shape = [sds((rows * levels, lanes), f32)]
@@ -459,21 +483,18 @@
                 pl.BlockSpec((1, levels, lanes), lambda i, s: (on(1, i, s), 0, 0)),
                 pl.BlockSpec((2, levels, lanes), lambda i, s: (0, 0, 0)),
             ]
-        side = (1, 1, levels, lanes)
         in_specs = [
             smem,
             pl.BlockSpec((tall, lanes), lambda i, s: (on(1, i, s), 0)),
             pl.BlockSpec((levels, lanes), lambda i, s: (jnp.maximum(on(1, i, s) * block - 1, 0), 0)),
             pl.BlockSpec((levels, lanes), lambda i, s: (jnp.minimum((on(1, i, s) + 1) * block, rows - 1), 0)),
-            pl.BlockSpec(side, lambda i, s: (jnp.maximum(row_of(s) - 1, 0), 0, 0, 0)),
-            pl.BlockSpec(side, lambda i, s: (jnp.minimum(row_of(s) + 1, n_row - 1), 0, 0, 0)),
             pl.BlockSpec((1, levels, lanes), lambda i, s: (on(1, i, s), 0, 0)),
             pl.BlockSpec((1, levels, lanes), lambda i, s: (on(1, i, s), 0, 0)),
-        ] + ([pl.BlockSpec((block, lanes), lambda i, s: (on(1, i, s), 0))] if final else [])
+        ] + [pl.BlockSpec((1, levels, lanes), lambda i, s: (0, 0, 0))] * len(near_parts) + ([pl.BlockSpec((block, lanes), lambda i, s: (on(1, i, s), 0))] if final else [])
         return call(
-            functools.partial(sweep_kernel, block=block, final=final), "sweep_last" if final else "sweep", (steps,),
+            functools.partial(sweep_kernel, block=block, near_parts=near_parts, final=final), (steps,),
             in_specs, out_specs, out_shape,
-            (counts, field, field, field, rows_in, rows_in, *cols_in, *extra),
+            (counts, field, field, field, *cols_in, *(rows_in[k] for k in near_parts), *extra),
             scratch=[pltpu.VMEM(((block + 2) * levels, lanes), f32)], size=2 * state_bytes,
         )
 
@@ -485,29 +506,28 @@
         with_ends = chunk == 0
         part = call(
             functools.partial(legendre_kernel, wave_dev=wave_dev, first_wave=chunk * width, with_ends=with_ends),
-            f"legendre_{chunk}", (width,),
+            (width,),
             [
                 pl.BlockSpec((1,) + legendre.shape[1:],
                              lambda i, s, chunk=chunk: (chunk * width + on(0, i, s), 0, 0)),
-                pl.BlockSpec((n_row, 1, rows, lanes), lambda i, s: (0, on(0, i, s), 0, 0)),
-            ] + ([pl.BlockSpec((2, levels, lanes), lambda i, s: (0, 0, 0)), anywhere] if with_ends else []),
-            pl.BlockSpec((n_row, 1, rows, lanes), lambda i, s: (0, on(0, i, s), 0, 0)),
-            sds((n_row, width, rows, lanes), bf16),
-            (legendre, coeffs[chunk], *([ends, gap] if with_ends else [])),
-            vmem=63, flops=4 * width * legendre.shape[1] * legendre.shape[2] * lanes,
+            ] + [pl.BlockSpec((1, rows, lanes), lambda i, s: (on(0, i, s), 0, 0))] * n_row + ([pl.BlockSpec((2, levels, lanes), lambda i, s: (0, 0, 0)), anywhere] if with_ends else []),
+            [pl.BlockSpec((1, rows, lanes), lambda i, s: (on(0, i, s), 0, 0))] * n_row,
+            [sds((width, rows, lanes), bf16)] * n_row,
+            (legendre, *coeffs[chunk], *([ends, gap] if with_ends else [])),
+            scratch=[pltpu.VMEM((n_row, rows, lanes), bf16)], vmem=63, flops=4 * width * legendre.shape[1] * legendre.shape[2] * lanes,
             size=2 * width * legendre.shape[1] * legendre.shape[2],
         )
-        returned.append(to_waves(part))
+        returned.append(traded(part))
 
     (sea,) = sweep(first_step, returned[0], sides, True, (gap,))
 
     state = call(
-        functools.partial(exit_kernel, chunks=chunks, block=block), "exit", (steps,),
+        functools.partial(exit_kernel, chunks=chunks, block=block), (steps,),
         [pl.BlockSpec((tall, lanes), lambda i, s: (on(1, i, s), 0))]
-        + [pl.BlockSpec((n_row, width, block, lanes), lambda i, s: (0, 0, on(0, i, s), 0))] * chunks,
+        + [pl.BlockSpec((width, block, lanes), lambda i, s: (0, on(0, i, s), 0))] * (chunks * n_row),
         pl.BlockSpec((tall, lanes), lambda i, s: (i, 0)),
         sds((rows * levels, lanes), f32),
-        (sea, *returned), scratch=[pltpu.VMEM((256, 256), bf16)], size=2 * state_bytes,
+        (sea, *sum(returned, [])), scratch=[pltpu.VMEM((256, 256), bf16)], size=2 * state_bytes,
     )
     return state.reshape(model_state.shape), new_surface[None]
 
@@ -523,4 +543,5 @@
         P("comp", "row", "col"),
     )
     out_specs = (P("comp", "row", None, "col"), P("comp", "row", "col"))
+
     return jax.shard_map(shards, mesh=mesh, in_specs=in_specs, out_specs=out_specs, check_vma=False)

time: 139 us -> 97.6 us (0.70)
  Pallas kernels: 76 us -> 57.5 us
  waiting for transfers between devices: 27.4 us -> 14.4 us
  starting transfers between devices: 29.2 us -> 21.6 us
  local copies, waits for them, and re-layouts: 4.11 us -> 2.18 us
    all_to_all x4 -> x0, waiting for transfers between devices: 23.7 us -> none  [to_waves(): return lax.all_to_all(x, 'row', split_axis=0, concat_axis=0, tiled=True)]
    all_to_all x4 -> x0, starting transfers between devices: 20.2 us -> none  [to_waves(): return lax.all_to_all(x, 'row', split_axis=0, concat_axis=0, tiled=True)]
    pallas_call x7, Pallas kernels: 76 us -> 57.5 us  [call(): pl.pallas_call(functools.partial(kernel, n_row=n_row, n_col=n_col), out_s...]
    ppermute x4 -> x16, starting transfers between devices: 8.98 us -> 21.3 us  [the longest x12 10.1 us: traded(): lax.ppermute(parts[k], 'row', [(r, r ^ k) for r in range(n_row)])]
    ppermute x4 -> x16, waiting for transfers between devices: 3.73 us -> 14.3 us  [the longest x12 14.3 us: traded(): lax.ppermute(parts[k], 'row', [(r, r ^ k) for r in range(n_row)])]
    unnamed x20 -> x26, local copies, waits for them, and re-layouts: 4.11 us -> 2.18 us
  transfers between devices with their start and end apart: 9 -> 17, of which waited for: 3 -> 3; matrix products, arithmetic and copies ran while one was open for 0% -> 0% of each run, Pallas kernels for 39% -> 53%
where the time goes in v3:
time: 97.6 us; the launch traced here: 96.4 us
  Pallas kernels  57.5 us (59%)
  starting transfers between devices  21.6 us (22%)
  waiting for transfers between devices  14.4 us (15%)
  local copies, waits for them, and re-layouts  2.18 us (2%)
    pallas_call x7, Pallas kernels, call(): pl.pallas_call(functools.partial(kernel, n_row=n_row, n_col=n_col), out_s...  57.5 us
    ppermute x12, waiting for transfers between devices, traded(): lax.ppermute(parts[k], 'row', [(r, r ^ k) for r in range(n_row)])  14.3 us
    ppermute x12, starting transfers between devices, traded(): lax.ppermute(parts[k], 'row', [(r, r ^ k) for r in range(n_row)])  10.1 us
    ppermute x2, starting transfers between devices, to_columns(): lax.ppermute(x, ('comp', 'col'), [(i, i + 1) for i in chain])  8.59 us
    ppermute x2, starting transfers between devices, to_columns(): lax.ppermute(x, ('comp', 'col'), [(i + 1, i) for i in chain])  2.57 us
    unnamed x26, local copies, waits for them, and re-layouts  2.18 us
  transfers between devices with their start and end apart: 17, of which 3 were waited for; matrix products, arithmetic and copies ran while one was open for 0% of the time, Pallas kernels for 53%

profile of v3, /device:TPU:7, one launch (start us, length us, event | category | flops | bytes accessed | tf_op | source)
XLA Modules:
  0.0 96.4 jit_solution(2339631609917196029)
XLA Ops:
  0.9 9.2 %shard_map.86 = (bf16[4,320,128]{2,1,0:T(8,128)(2,1)}, bf16[4,320,128]{2,1,0:T(8,128)(2,1)}, bf16[4,320,128]{2,1,0:T(8,128)(2,1)}, bf16[4,320,128]{2,1,0:T(8,128...) custom-call(s32[1]{0:T(128)} %bitcast.place, ...), custom_call_target="tpu_custom_call" | custom-call | flops 10000000 | bytes 10485760 | tf_op jit(solution)/shard_map/pallas_call | solution.py:417
  10.1 1.3 %collective-permute-start = (bf16[5,32,128]{2,1,0:T(8,128)(2,1)}, bf16[5,32,128]{2,1,0:T(8,128)(2,1)S(1)}, u32[]{:S(2)}, u32[]{:S(2)}) collective-permute-start(bf16[5,32,128]{2,1,0:T(8,128)(2,1)} %get-tuple-element.26._), channel_id=1, source_target_pairs={{17,16},{18,17},{19,18},{21,20},{22,21},{23,22},{25,24},{26,25},{2... | collective-permute-start | bytes 122888 | tf_op jit(solution)/shard_map/ppermute | solution.py:461
  11.4 4.0 %collective-permute-start.1 = (bf16[5,32,128]{2,1,0:T(8,128)(2,1)}, bf16[5,32,128]{2,1,0:T(8,128)(2,1)S(1)}, u32[]{:S(2)}, u32[]{:S(2)}) collective-permute-start(bf16[5,32,128]{2,1,0:T(8,128)(2,1)} %get-tuple-element.26._), channel_id=1, source_target_pairs={{16,17},{17,18},{18,19},{20,21},{21,22},{22,23},{24,25},{25,26},{2... | collective-permute-start | bytes 122888 | tf_op jit(solution)/shard_map/ppermute | solution.py:462
  15.4 1.6 %collective-permute-start.2 = (bf16[4,320,128]{2,1,0:T(8,128)(2,1)}, bf16[4,320,128]{2,1,0:T(8,128)(2,1)S(1)}, u32[]{:S(2)}, u32[]{:S(2)}) collective-permute-start(bf16[4,320,128]{2,1,0:T(8,128)(2,1)} %get-tuple-element.27), channel_id=1, source_target_pairs={{0,4},{4,0},{8,12},{12,8},{1,5},{5,1},{9,13},{13,9},{2,6},{6,2},{1... | collective-permute-start | bytes 983048 | tf_op jit(solution)/shard_map/ppermute | solution.py:454
  17.0 1.4 %collective-permute-start.6 = (bf16[4,320,128]{2,1,0:T(8,128)(2,1)}, bf16[4,320,128]{2,1,0:T(8,128)(2,1)}, u32[]{:S(2)}, u32[]{:S(2)}) collective-permute-start(bf16[4,320,128]{2,1,0:T(8,128)(2,1)} %get-tuple-element.32), channel_id=1, source_target_pairs={{0,8},{4,12},{8,0},{12,4},{1,9},{5,13},{9,1},{13,5},{2,10},{6,14},... | collective-permute-start | bytes 983048 | tf_op jit(solution)/shard_map/ppermute | solution.py:454
  18.4 16.6 %shard_map.88 = (f32[320,128]{1,0:T(8,128)}, f32[320,128]{1,0:T(8,128)}) custom-call(s32[1]{0:T(128)} %bitcast.place, s32[1,320]{1,0:T(1,128)} %bitcast.11, f32[320,128]{1,0:T(8,128)} %copy-done.12, f32[320,128]{1,0:T(8,128)} %bitcast.15, s32[320,128]{1,0:T(8,128)} %bitcast.16, bf16[5,32,128]{2,1,0:T(8,128)(2,1)} %get-tuple-element.26._), custom_call_target="tpu_custom_call" | custom-call | flops 20000000000 | bytes 819200 | tf_op jit(solution)/shard_map/pallas_call | solution.py:417
  35.1 0.8 collective-permute-start.11
  36.2 1.3 %collective-permute-start.13 = (bf16[4,320,128]{2,1,0:T(8,128)(2,1)}, bf16[4,320,128]{2,1,0:T(8,128)(2,1)}, u32[]{:S(2)}, u32[]{:S(2)}) collective-permute-start(bf16[4,320,128]{2,1,0:T(8,128)(2,1)} %get-tuple-element.42), channel_id=1, source_target_pairs={{0,12},{4,8},{8,4},{12,0},{1,13},{5,9},{9,5},{13,1},{2,14},{6,10},... | collective-permute-start | bytes 983048 | tf_op jit(solution)/shard_map/ppermute | solution.py:454
  37.6 0.7 copy-done.3
  38.3 10.0 %shard_map.87 = (f32[10240,128]{1,0:T(8,128)}, bf16[5,32,128]{2,1,0:T(8,128)(2,1)}, bf16[2,32,128]{2,1,0:T(8,128)(2,1)}) custom-call(s32[1]{0:T(128)} %bitcast.place, s32[1,320]{1,0:T(1,128)} %bitcast.12, f32[10240,128]{1,0:T(8,128)} %get-tuple-element.25.field.above.below, f32[10240,128]{1,0:T(8,128)} %get-tuple-element.25.field.above.below, ...), custom_call_target="tpu_custom_call" | custom-call | flops 10000000 | bytes 10485760 | tf_op jit(solution)/shard_map/pallas_call | solution.py:417
  48.4 3.3 %shard_map.89 = (bf16[4,320,128]{2,1,0:T(8,128)(2,1)}, bf16[4,320,128]{2,1,0:T(8,128)(2,1)}, bf16[4,320,128]{2,1,0:T(8,128)(2,1)}, bf16[4,320,128]{2,1,0:T(8,128)(2,1)}) custom-call(s32[1]{0:T(128)} %bitcast.place, bf16[8,1280,1280]{2,1,0:T(8,128)(2,1)} %legendre.3, bf16[4,320,128]{2,1,0:T(8,128)(2,1)} %get-tuple-element.31.rest_0_, ...), custom_call_target="tpu_custom_call" | custom-call | flops 3355443200 | bytes 13107200 | tf_op jit(solution)/shard_map/pallas_call | solution.py:417
  51.8 1.3 %collective-permute-start.4 = (bf16[5,32,128]{2,1,0:T(8,128)(2,1)}, bf16[5,32,128]{2,1,0:T(8,128)(2,1)}, u32[]{:S(2)}, u32[]{:S(2)}) collective-permute-start(bf16[5,32,128]{2,1,0:T(8,128)(2,1)} %get-tuple-element.30), channel_id=1, source_target_pairs={{17,16},{18,17},{19,18},{21,20},{22,21},{23,22},{25,24},{26,25},{2... | collective-permute-start | bytes 122888 | tf_op jit(solution)/shard_map/ppermute | solution.py:461
  53.1 4.6 %collective-permute-start.5 = (bf16[5,32,128]{2,1,0:T(8,128)(2,1)}, bf16[5,32,128]{2,1,0:T(8,128)(2,1)}, u32[]{:S(2)}, u32[]{:S(2)}) collective-permute-start(bf16[5,32,128]{2,1,0:T(8,128)(2,1)} %get-tuple-element.30), channel_id=1, source_target_pairs={{16,17},{17,18},{18,19},{20,21},{21,22},{22,23},{24,25},{25,26},{2... | collective-permute-start | bytes 122888 | tf_op jit(solution)/shard_map/ppermute | solution.py:462
  57.7 1.2 %collective-permute-start.9 = (bf16[4,320,128]{2,1,0:T(8,128)(2,1)}, bf16[4,320,128]{2,1,0:T(8,128)(2,1)S(1)}, u32[]{:S(2)}, u32[]{:S(2)}) collective-permute-start(bf16[4,320,128]{2,1,0:T(8,128)(2,1)} %get-tuple-element.36), channel_id=1, source_target_pairs={{0,12},{4,8},{8,4},{12,0},{1,13},{5,9},{9,5},{13,1},{2,14},{6,10},... | collective-permute-start | bytes 983048 | tf_op jit(solution)/shard_map/ppermute | solution.py:454
  58.9 2.8 %shard_map.91 = (bf16[4,320,128]{2,1,0:T(8,128)(2,1)}, bf16[4,320,128]{2,1,0:T(8,128)(2,1)}, bf16[4,320,128]{2,1,0:T(8,128)(2,1)}, bf16[4,320,128]{2,1,0:T(8,128)(2,1)}) custom-call(s32[1]{0:T(128)} %bitcast.place, bf16[8,1280,1280]{2,1,0:T(8,128)(2,1)} %legendre.3, bf16[4,320,128]{2,1,0:T(8,128)(2,1)} %get-tuple-element.39.rest_0_, ...), custom_call_target="tpu_custom_call" | custom-call | flops 3355443200 | bytes 13107200 | tf_op jit(solution)/shard_map/pallas_call | solution.py:417
  61.8 1.1 %collective-permute-start.15 = (bf16[4,320,128]{2,1,0:T(8,128)(2,1)}, bf16[4,320,128]{2,1,0:T(8,128)(2,1)S(1)}, u32[]{:S(2)}, u32[]{:S(2)}) collective-permute-start(bf16[4,320,128]{2,1,0:T(8,128)(2,1)} %get-tuple-element.45), channel_id=1, source_target_pairs={{0,8},{4,12},{8,0},{12,4},{1,9},{5,13},{9,1},{13,5},{2,10},{6,14},... | collective-permute-start | bytes 983048 | tf_op jit(solution)/shard_map/ppermute | solution.py:454
  62.9 1.0 %collective-permute-start.16 = (bf16[4,320,128]{2,1,0:T(8,128)(2,1)}, bf16[4,320,128]{2,1,0:T(8,128)(2,1)S(1)}, u32[]{:S(2)}, u32[]{:S(2)}) collective-permute-start(bf16[4,320,128]{2,1,0:T(8,128)(2,1)} %get-tuple-element.46), channel_id=1, source_target_pairs={{0,12},{4,8},{8,4},{12,0},{1,13},{5,9},{9,5},{13,1},{2,14},{6,10},... | collective-permute-start | bytes 983048 | tf_op jit(solution)/shard_map/ppermute | solution.py:454
  63.9 1.1 %collective-permute-start.10 = (bf16[4,320,128]{2,1,0:T(8,128)(2,1)}, bf16[4,320,128]{2,1,0:T(8,128)(2,1)S(1)}, u32[]{:S(2)}, u32[]{:S(2)}) collective-permute-start(bf16[4,320,128]{2,1,0:T(8,128)(2,1)} %get-tuple-element.38), channel_id=1, source_target_pairs={{0,8},{4,12},{8,0},{12,4},{1,9},{5,13},{9,1},{13,5},{2,10},{6,14},... | collective-permute-start | bytes 983048 | tf_op jit(solution)/shard_map/ppermute | solution.py:454
  65.0 3.0 %collective-permute-done.9.rest_1_.rest_3_ = bf16[4,320,128]{2,1,0:T(8,128)(2,1)S(1)} collective-permute-done((bf16[4,320,128]{2,1,0:T(8,128)(2,1)}, bf16[4,320,128]{2,1,0:T(8,128)(2,1)S(1)}, u32[]{:S(2)}, u32[]{:S(2)}) %collective-permute-start.9) | collective-permute-done | bytes 327712 | tf_op jit(solution)/shard_map/ppermute | solution.py:454
  68.0 0.7 copy-done.1
  68.7 9.0 %shard_map.90.sea = f32[10240,128]{1,0:T(8,128)} custom-call(s32[1]{0:T(128)} %bitcast.place, s32[1,320]{1,0:T(1,128)} %bitcast.13, f32[10240,128]{1,0:T(8,128)} %get-tuple-element.29.field.above.below, f32[10240,128]{1,0:T(8,128)} %get-tuple-element.29.field.above.below, f32[10240,128]{1,0:T(8,128)} %get-tuple-element.29.field.above.below, ...), custom_call_target="tpu_custom_call" | custom-call | flops 10000000 | bytes 10485760 | tf_op jit(solution)/shard_map/pallas_call | solution.py:417
  77.8 4.3 %collective-permute-done.16.rest_7_ = bf16[4,320,128]{2,1,0:T(8,128)(2,1)S(1)} collective-permute-done((bf16[4,320,128]{2,1,0:T(8,128)(2,1)}, bf16[4,320,128]{2,1,0:T(8,128)(2,1)S(1)}, u32[]{:S(2)}, u32[]{:S(2)}) %collective-permute-start.16) | collective-permute-done | bytes 327712 | tf_op jit(solution)/shard_map/ppermute | solution.py:454
  82.0 7.0 %collective-permute-done.10.rest_2_ = bf16[4,320,128]{2,1,0:T(8,128)(2,1)S(1)} collective-permute-done((bf16[4,320,128]{2,1,0:T(8,128)(2,1)}, bf16[4,320,128]{2,1,0:T(8,128)(2,1)S(1)}, u32[]{:S(2)}, u32[]{:S(2)}) %collective-permute-start.10) | collective-permute-done | bytes 327712 | tf_op jit(solution)/shard_map/ppermute | solution.py:454
  89.8 6.6 %shard_map.92 = f32[10240,128]{1,0:T(8,128)} custom-call(s32[1]{0:T(128)} %bitcast.place, f32[10240,128]{1,0:T(8,128)} %shard_map.90.sea, bf16[4,320,128]{2,1,0:T(8,128)(2,1)} %get-tuple-element.37.rest_0_, bf16[4,320,128]{2,1,0:T(8,128)(2,1)} %copy-done, bf16[4,320,128]{2,1,0:T(8,128)(2,1)} %copy-done.7, bf16[4,320,128]{2,1,0:T(8,128)(2,1)} %copy-done.1, ...), custom_call_target="tpu_custom_call" | custom-call | flops 10000000 | bytes 10485760 | tf_op jit(solution)/shard_map/pallas_call | solution.py:417
  (43 shorter events, 1.7 us)
Async XLA Ops:
  0.6 16.4 %collective-permute-start.7 = (f32[320,128]{1,0:T(8,128)}, f32[320,128]{1,0:T(8,128)S(1)}, u32[]{:S(2)}, u32[]{:S(2)}) collective-permute-start(f32[320,128]{1,0:T(8,128)} %bitcast.14), channel_id=1, source_target_pairs={{0,16},{16,0},{1,17},{17,1},{2,18},{18,2},{3,19},{19,3},{4,20},{20... | collective-permute-start | bytes 491528 | tf_op jit(solution)/shard_map/ppermute | solution.py:411
  10.1 24.9 %collective-permute-start = (bf16[5,32,128]{2,1,0:T(8,128)(2,1)}, bf16[5,32,128]{2,1,0:T(8,128)(2,1)S(1)}, u32[]{:S(2)}, u32[]{:S(2)}) collective-permute-start(bf16[5,32,128]{2,1,0:T(8,128)(2,1)} %get-tuple-element.26._), channel_id=1, source_target_pairs={{17,16},{18,17},{19,18},{21,20},{22,21},{23,22},{25,24},{26,25},{2... | collective-permute-start | bytes 122888 | tf_op jit(solution)/shard_map/ppermute | solution.py:461
  11.4 24.4 %collective-permute-start.1 = (bf16[5,32,128]{2,1,0:T(8,128)(2,1)}, bf16[5,32,128]{2,1,0:T(8,128)(2,1)S(1)}, u32[]{:S(2)}, u32[]{:S(2)}) collective-permute-start(bf16[5,32,128]{2,1,0:T(8,128)(2,1)} %get-tuple-element.26._), channel_id=1, source_target_pairs={{16,17},{17,18},{18,19},{20,21},{21,22},{22,23},{24,25},{25,26},{2... | collective-permute-start | bytes 122888 | tf_op jit(solution)/shard_map/ppermute | solution.py:462
  15.4 20.8 %collective-permute-start.2 = (bf16[4,320,128]{2,1,0:T(8,128)(2,1)}, bf16[4,320,128]{2,1,0:T(8,128)(2,1)S(1)}, u32[]{:S(2)}, u32[]{:S(2)}) collective-permute-start(bf16[4,320,128]{2,1,0:T(8,128)(2,1)} %get-tuple-element.27), channel_id=1, source_target_pairs={{0,4},{4,0},{8,12},{12,8},{1,5},{5,1},{9,13},{13,9},{2,6},{6,2},{1... | collective-permute-start | bytes 983048 | tf_op jit(solution)/shard_map/ppermute | solution.py:454
  17.0 20.6 %collective-permute-start.3 = (bf16[4,320,128]{2,1,0:T(8,128)(2,1)}, bf16[4,320,128]{2,1,0:T(8,128)(2,1)S(1)}, u32[]{:S(2)}, u32[]{:S(2)}) collective-permute-start(bf16[4,320,128]{2,1,0:T(8,128)(2,1)} %get-tuple-element.28), channel_id=1, source_target_pairs={{0,12},{4,8},{8,4},{12,0},{1,13},{5,9},{9,5},{13,1},{2,14},{6,10},... | collective-permute-start | bytes 983048 | tf_op jit(solution)/shard_map/ppermute | solution.py:454
  17.0 31.4 %collective-permute-start.6 = (bf16[4,320,128]{2,1,0:T(8,128)(2,1)}, bf16[4,320,128]{2,1,0:T(8,128)(2,1)}, u32[]{:S(2)}, u32[]{:S(2)}) collective-permute-start(bf16[4,320,128]{2,1,0:T(8,128)(2,1)} %get-tuple-element.32), channel_id=1, source_target_pairs={{0,8},{4,12},{8,0},{12,4},{1,9},{5,13},{9,1},{13,5},{2,10},{6,14},... | collective-permute-start | bytes 983048 | tf_op jit(solution)/shard_map/ppermute | solution.py:454
  18.4 16.6 %copy-start.11 = (bf16[4,320,128]{2,1,0:T(8,128)(2,1)S(1)}, bf16[4,320,128]{2,1,0:T(8,128)(2,1)}, u32[]{:S(2)}) copy-start(bf16[4,320,128]{2,1,0:T(8,128)(2,1)} %get-tuple-element.40) | copy-start | bytes 983044
  35.0 2.5 %copy-start.9 = (bf16[5,32,128]{2,1,0:T(8,128)(2,1)}, bf16[5,32,128]{2,1,0:T(8,128)(2,1)S(1)}, u32[]{:S(2)}) copy-start(bf16[5,32,128]{2,1,0:T(8,128)(2,1)S(1)} %collective-permute-done.east_in) | copy-start | bytes 122884
  35.1 18.0 %collective-permute-start.11 = (bf16[4,320,128]{2,1,0:T(8,128)(2,1)S(1)}, bf16[4,320,128]{2,1,0:T(8,128)(2,1)S(1)}, u32[]{:S(2)}, u32[]{:S(2)}) collective-permute-start(bf16[4,320,128]{2,1,0:T(8,128)(2,1)S(1)} %copy-done.11), channel_id=1, source_target_pairs={{0,4},{4,0},{8,12},{12,8},{1,5},{5,1},{9,13},{13,9},{2,6},{6,2},{1... | collective-permute-start | bytes 983048 | tf_op jit(solution)/shard_map/ppermute | solution.py:454
  35.8 21.9 %collective-permute-start.12 = (bf16[4,320,128]{2,1,0:T(8,128)(2,1)}, bf16[4,320,128]{2,1,0:T(8,128)(2,1)}, u32[]{:S(2)}, u32[]{:S(2)}) collective-permute-start(bf16[4,320,128]{2,1,0:T(8,128)(2,1)} %get-tuple-element.41), channel_id=1, source_target_pairs={{0,8},{4,12},{8,0},{12,4},{1,9},{5,13},{9,1},{13,5},{2,10},{6,14},... | collective-permute-start | bytes 983048 | tf_op jit(solution)/shard_map/ppermute | solution.py:454
  36.2 22.7 %collective-permute-start.13 = (bf16[4,320,128]{2,1,0:T(8,128)(2,1)}, bf16[4,320,128]{2,1,0:T(8,128)(2,1)}, u32[]{:S(2)}, u32[]{:S(2)}) collective-permute-start(bf16[4,320,128]{2,1,0:T(8,128)(2,1)} %get-tuple-element.42), channel_id=1, source_target_pairs={{0,12},{4,8},{8,4},{12,0},{1,13},{5,9},{9,5},{13,1},{2,14},{6,10},... | collective-permute-start | bytes 983048 | tf_op jit(solution)/shard_map/ppermute | solution.py:454
  51.6 12.3 %collective-permute-start.8 = (bf16[4,320,128]{2,1,0:T(8,128)(2,1)}, bf16[4,320,128]{2,1,0:T(8,128)(2,1)S(1)}, u32[]{:S(2)}, u32[]{:S(2)}) collective-permute-start(bf16[4,320,128]{2,1,0:T(8,128)(2,1)} %get-tuple-element.35), channel_id=1, source_target_pairs={{0,4},{4,0},{8,12},{12,8},{1,5},{5,1},{9,13},{13,9},{2,6},{6,2},{1... | collective-permute-start | bytes 983048 | tf_op jit(solution)/shard_map/ppermute | solution.py:454
  51.8 10.0 %collective-permute-start.4 = (bf16[5,32,128]{2,1,0:T(8,128)(2,1)}, bf16[5,32,128]{2,1,0:T(8,128)(2,1)}, u32[]{:S(2)}, u32[]{:S(2)}) collective-permute-start(bf16[5,32,128]{2,1,0:T(8,128)(2,1)} %get-tuple-element.30), channel_id=1, source_target_pairs={{17,16},{18,17},{19,18},{21,20},{22,21},{23,22},{25,24},{26,25},{2... | collective-permute-start | bytes 122888 | tf_op jit(solution)/shard_map/ppermute | solution.py:461
  53.1 5.8 %copy-start.8 = (bf16[4,320,128]{2,1,0:T(8,128)(2,1)}, bf16[4,320,128]{2,1,0:T(8,128)(2,1)S(1)}, u32[]{:S(2)}) copy-start(bf16[4,320,128]{2,1,0:T(8,128)(2,1)S(1)} %collective-permute-done.11.rest_1_) | copy-start | bytes 983044
  53.1 9.8 %collective-permute-start.5 = (bf16[5,32,128]{2,1,0:T(8,128)(2,1)}, bf16[5,32,128]{2,1,0:T(8,128)(2,1)}, u32[]{:S(2)}, u32[]{:S(2)}) collective-permute-start(bf16[5,32,128]{2,1,0:T(8,128)(2,1)} %get-tuple-element.30), channel_id=1, source_target_pairs={{16,17},{17,18},{18,19},{20,21},{21,22},{22,23},{24,25},{25,26},{2... | collective-permute-start | bytes 122888 | tf_op jit(solution)/shard_map/ppermute | solution.py:462
  57.7 10.3 %collective-permute-start.9 = (bf16[4,320,128]{2,1,0:T(8,128)(2,1)}, bf16[4,320,128]{2,1,0:T(8,128)(2,1)S(1)}, u32[]{:S(2)}, u32[]{:S(2)}) collective-permute-start(bf16[4,320,128]{2,1,0:T(8,128)(2,1)} %get-tuple-element.36), channel_id=1, source_target_pairs={{0,12},{4,8},{8,4},{12,0},{1,13},{5,9},{9,5},{13,1},{2,14},{6,10},... | collective-permute-start | bytes 983048 | tf_op jit(solution)/shard_map/ppermute | solution.py:454
  61.7 16.0 %collective-permute-start.14 = (bf16[4,320,128]{2,1,0:T(8,128)(2,1)}, bf16[4,320,128]{2,1,0:T(8,128)(2,1)S(1)}, u32[]{:S(2)}, u32[]{:S(2)}) collective-permute-start(bf16[4,320,128]{2,1,0:T(8,128)(2,1)} %get-tuple-element.44), channel_id=1, source_target_pairs={{0,4},{4,0},{8,12},{12,8},{1,5},{5,1},{9,13},{13,9},{2,6},{6,2},{1... | collective-permute-start | bytes 983048 | tf_op jit(solution)/shard_map/ppermute | solution.py:454
  61.8 16.0 %collective-permute-start.15 = (bf16[4,320,128]{2,1,0:T(8,128)(2,1)}, bf16[4,320,128]{2,1,0:T(8,128)(2,1)S(1)}, u32[]{:S(2)}, u32[]{:S(2)}) collective-permute-start(bf16[4,320,128]{2,1,0:T(8,128)(2,1)} %get-tuple-element.45), channel_id=1, source_target_pairs={{0,8},{4,12},{8,0},{12,4},{1,9},{5,13},{9,1},{13,5},{2,10},{6,14},... | collective-permute-start | bytes 983048 | tf_op jit(solution)/shard_map/ppermute | solution.py:454
  62.9 19.1 %collective-permute-start.16 = (bf16[4,320,128]{2,1,0:T(8,128)(2,1)}, bf16[4,320,128]{2,1,0:T(8,128)(2,1)S(1)}, u32[]{:S(2)}, u32[]{:S(2)}) collective-permute-start(bf16[4,320,128]{2,1,0:T(8,128)(2,1)} %get-tuple-element.46), channel_id=1, source_target_pairs={{0,12},{4,8},{8,4},{12,0},{1,13},{5,9},{9,5},{13,1},{2,14},{6,10},... | collective-permute-start | bytes 983048 | tf_op jit(solution)/shard_map/ppermute | solution.py:454
  63.9 4.1 %copy-start = (bf16[4,320,128]{2,1,0:T(8,128)(2,1)}, bf16[4,320,128]{2,1,0:T(8,128)(2,1)S(1)}, u32[]{:S(2)}) copy-start(bf16[4,320,128]{2,1,0:T(8,128)(2,1)S(1)} %collective-permute-done.8.rest_0_.rest_1_) | copy-start | bytes 983044
  63.9 25.2 %collective-permute-start.10 = (bf16[4,320,128]{2,1,0:T(8,128)(2,1)}, bf16[4,320,128]{2,1,0:T(8,128)(2,1)S(1)}, u32[]{:S(2)}, u32[]{:S(2)}) collective-permute-start(bf16[4,320,128]{2,1,0:T(8,128)(2,1)} %get-tuple-element.38), channel_id=1, source_target_pairs={{0,8},{4,12},{8,0},{12,4},{1,9},{5,13},{9,1},{13,5},{2,10},{6,14},... | collective-permute-start | bytes 983048 | tf_op jit(solution)/shard_map/ppermute | solution.py:454
  77.7 11.3 %copy-start.4 = (bf16[4,320,128]{2,1,0:T(8,128)(2,1)}, bf16[4,320,128]{2,1,0:T(8,128)(2,1)S(1)}, u32[]{:S(2)}) copy-start(bf16[4,320,128]{2,1,0:T(8,128)(2,1)S(1)} %collective-permute-done.14.rest_5_) | copy-start | bytes 983044
  77.8 11.3 %copy-start.5 = (bf16[4,320,128]{2,1,0:T(8,128)(2,1)}, bf16[4,320,128]{2,1,0:T(8,128)(2,1)S(1)}, u32[]{:S(2)}) copy-start(bf16[4,320,128]{2,1,0:T(8,128)(2,1)S(1)} %collective-permute-done.15.rest_6_) | copy-start | bytes 983044
  82.0 7.0 %copy-start.6 = (bf16[4,320,128]{2,1,0:T(8,128)(2,1)}, bf16[4,320,128]{2,1,0:T(8,128)(2,1)S(1)}, u32[]{:S(2)}) copy-start(bf16[4,320,128]{2,1,0:T(8,128)(2,1)S(1)} %collective-permute-done.16.rest_7_) | copy-start | bytes 983044
  (6 other events, 6.7 us)

commit v4 on v3

--- a/solution.py
+++ b/solution.py
@@ -12,8 +12,17 @@
 lanes = 128
 
 
-def chunk_count(wave_dev):
-    return 2 if wave_dev % 2 == 0 else 1
+def chunk_widths(wave_dev):
+    outer = 3 * wave_dev // 8
+    return (outer, wave_dev - 2 * outer, outer) if outer else (wave_dev,)
+
+
+def chunk_of(local, widths):
+    chunk = 0
+    while local >= widths[chunk]:
+        local -= widths[chunk]
+        chunk += 1
+    return chunk, local
 
 
 def row_block(rows):
@@ -72,20 +81,20 @@
     return jnp.dot(a, b, preferred_element_type=jnp.float32)
 
 
-def entry_kernel(place, counts, field, last, gauss, mix, *rest, n_row, n_col, chunks, block):
+def entry_kernel(place, counts, field, last, gauss, mix, *rest, n_row, n_col, widths, block):
+    chunks = len(widths)
     send = [rest[n_row * c:n_row * (c + 1)] for c in range(chunks)]
     mixed, edge, table = rest[n_row * chunks:]
     comp, row, _ = where_am_i(place, n_row, n_col)
     levels = field.shape[0] // block
     wave_dev = levels // n_row
-    width = wave_dev // chunks
     step = pl.program_id(0)
 
     flip = row * wave_dev
 
     def target(wave):
         part, local = divmod(wave, wave_dev)
-        chunk, slot = divmod(local, width)
+        chunk, slot = chunk_of(local, widths)
         return send[chunk][part], slot
 
     @pl.when(comp == 0)
@@ -177,7 +186,7 @@
             top = mixed_rows(field, 0, 0)[0][1]
             low = mixed_rows(last, 0, total - 8)[-1][1]
             for part in range(1, n_row):
-                send[0][part][0, 0:levels, :] = jnp.where((part ^ row) > row, low, top)
+                send[chunks // 2][part][0, 0:levels, :] = jnp.where((part ^ row) > row, low, top)
 
 
 def sweep_kernel(place, counts, field, above, below, east_in, west_in, *rest, block, n_row, n_col, near_parts, final):
@@ -228,15 +237,14 @@
 
         lax.fori_loop(0, block // 8, fill, 0)
         beside = beside_matrix()
-        weights = jnp.concatenate([beside, side_matrix(), beside], axis=0)
+        weights = jnp.concatenate([beside, side_matrix()], axis=0)
         spread = spread_matrix()
 
         def body(g, packed):
             here = masked[pl.ds(pl.multiple_of((g * batch + 1) * levels, levels), batch * levels), :]
-            high, low = split(here)
             turned = jnp.concatenate(
                 [jnp.where(pair_of == g * batch + s, sides, 0.0).astype(jnp.bfloat16) for s in range(batch)], axis=0)
-            near = product(jnp.concatenate([high, turned, low], axis=1), weights)
+            near = product(jnp.concatenate([here.astype(jnp.bfloat16), turned], axis=1), weights)
             new_rows = []
             for s in range(batch):
                 y = g * batch + s
@@ -305,20 +313,18 @@
                 out[part][0, 0:levels, :] = jnp.where((part ^ row) > row, ends[1], ends[0])
 
 
-def surface_kernel(place, counts, partner, own, source, _, new, gap, *, group, n_row, n_col):
-    rows = partner.shape[0]
-    half = rows // 2
+def surface_kernel(place, counts, partner, own, source, *rest, first, group, n_row, n_col):
+    new, gap = rest[-2:]
+    half = partner.shape[0] // 2
     width = 2 * lanes
     table = jnp.concatenate(
         [partner[pl.ds(0, half, stride=2), :], partner[pl.ds(1, half, stride=2), :]], axis=1
-    )
-    coarse = table.astype(jnp.bfloat16)
-    fine = (table - coarse.astype(jnp.float32)).astype(jnp.bfloat16)
-    low_index = lax.broadcasted_iota(jnp.int32, (width, lanes), 0)
-    high_index = lax.broadcasted_iota(jnp.int32, (half, lanes), 0)
+    ).astype(jnp.bfloat16)
+    low_index = iota((width, lanes), 0)
+    high_index = iota((half, lanes), 0)
     one = jnp.ones((width, lanes), jnp.bfloat16)
     zero = jnp.zeros((width, lanes), jnp.bfloat16)
-    sublane = lax.broadcasted_iota(jnp.int32, (8, lanes), 0)
+    sublane = iota((8, lanes), 0)
     rate = jnp.where(where_am_i(place, n_row, n_col)[0] == 0, 0.5, 0.25).astype(jnp.float32)
 
     def body(g, carry):
@@ -331,8 +337,7 @@
             pick = jnp.concatenate(
                 [jnp.where(low_index == low[s:s + 1, :], one, zero) for s in range(p, p + group)], axis=1
             )
-            picked = jnp.dot(coarse, pick, preferred_element_type=jnp.float32)
-            picked = picked + jnp.dot(fine, pick, preferred_element_type=jnp.float32)
+            picked = product(table, pick)
             for s in range(group):
                 part = picked[:, lanes * s:lanes * (s + 1)]
                 match = high_index == high[p + s:p + s + 1, :]
@@ -340,29 +345,28 @@
         pulled = jnp.concatenate(found, axis=0)
         limit = jnp.zeros((8, lanes), jnp.int32)
         for s in range(8):
-            limit = jnp.where(sublane == s, counts[0, start + s], limit)
+            limit = jnp.where(sublane == s, counts[0, first + start + s], limit)
         here = own[pl.ds(start, 8), :]
         difference = jnp.where(iota((8, lanes), 1) < limit, pulled - here, 0.0)
         new[pl.ds(start, 8), :] = here + rate * difference
         gap[pl.ds(start, 8), :] = difference
         return carry
 
-    lax.fori_loop(0, rows // 8, body, 0)
-
-
-def exit_kernel(place, sea, *rest, n_row, n_col, chunks, block):
+    lax.fori_loop(0, source.shape[0] // 8, body, 0)
+
+
+def exit_kernel(place, sea, *rest, n_row, n_col, widths, block):
+    chunks = len(widths)
     back = [rest[n_row * c:n_row * (c + 1)] for c in range(chunks)]
     out, table = rest[n_row * chunks:]
     comp, row, _ = where_am_i(place, n_row, n_col)
     levels = out.shape[0] // block
     wave_dev = levels // n_row
-    width = wave_dev // chunks
-
     flip = row * wave_dev
 
     def source(wave, lat, count):
         part, local = divmod(wave, wave_dev)
-        chunk, slot = divmod(local, width)
+        chunk, slot = chunk_of(local, widths)
         return back[chunk][part][slot, lat:lat + count, :]
 
     @pl.when(comp == 0)
@@ -395,8 +399,8 @@
     n_row, n_col = lax.axis_size("row"), lax.axis_size("col")
     rows, levels = model_state.shape[1], model_state.shape[2]
     wave_dev = levels // n_row
-    chunks = chunk_count(wave_dev)
-    width = wave_dev // chunks
+    widths = chunk_widths(wave_dev)
+    chunks = len(widths)
     block = row_block(rows)
     steps = rows // block
     f32, bf16 = jnp.float32, jnp.bfloat16
@@ -413,13 +417,14 @@
     def on(comp, i, s):
         return jnp.where(lax.div(s[0], n_row * n_col) == comp, i, 0)
 
-    def call(kernel, grid, in_specs, out_specs, out_shape, args, scratch=(), vmem=59, flops=10**7, size=0):
+    def call(kernel, grid, in_specs, out_specs, out_shape, args, scratch=(), vmem=59, flops=10**7, size=0, aliases={}):
         return pl.pallas_call(
             functools.partial(kernel, n_row=n_row, n_col=n_col),
             out_shape=out_shape,
             grid_spec=pltpu.PrefetchScalarGridSpec(
                 num_scalar_prefetch=1, grid=grid, in_specs=in_specs, out_specs=out_specs, scratch_shapes=scratch),
             compiler_params=pltpu.CompilerParams(vmem_limit_bytes=vmem * mib),
+            input_output_aliases=aliases,
             cost_estimate=cost(flops, size),
         )(place, *args)
 
@@ -429,7 +434,7 @@
     tall = block * levels
 
     *send, mixed, edge = call(
-        functools.partial(entry_kernel, chunks=chunks, block=block), (steps,),
+        functools.partial(entry_kernel, widths=widths, block=block), (steps,),
         [
             smem,
             pl.BlockSpec((tall, lanes), lambda i, s: (i, 0)),
@@ -437,21 +442,31 @@
             smem,
             pl.BlockSpec((levels, levels), lambda i, s: (0, 0)),
         ],
-        [pl.BlockSpec((width, block, lanes), lambda i, s: (0, i, 0))] * (chunks * n_row)
+        [pl.BlockSpec((w, block, lanes), lambda i, s: (0, i, 0)) for w in widths for _ in range(n_row)]
         + [
             pl.BlockSpec((tall, lanes), lambda i, s: (on(1, i, s), 0)),
             pl.BlockSpec((1, levels, lanes), lambda i, s: (on(1, i, s), 0, 0)),
         ],
-        [sds((width, rows, lanes), bf16)] * (chunks * n_row)
+        [sds((w, rows, lanes), bf16) for w in widths for _ in range(n_row)]
         + [sds((rows * levels, lanes), f32), sds((steps, levels, lanes), bf16)],
         (counts, fields, fields, gauss_weight, mixing),
         scratch=[pltpu.VMEM((256, 256), bf16)], vmem=63, size=2 * state_bytes,
     )
 
-    def traded(parts):
+    near_parts = [k for k in range(1, n_row) if k & (k + 1) == 0]
+    both = ("comp", "row")
+
+    def traded(parts, with_edges, relayed):
         got = [parts[0]]
         for k in range(1, n_row):
-            got.append(lax.ppermute(parts[k], "row", [(r, r ^ k) for r in range(n_row)]))
+            route = [(r, r ^ k) for r in range(n_row)]
+            if with_edges and k in near_parts:
+                route += [(n_row + a, n_row + b) for a, b in route]
+            if relayed and k > 1:
+                halfway = lax.ppermute(parts[k], both, [(a, n_row + b) for a, b in route])
+                got.append(lax.ppermute(halfway, both, [(n_row + r, r) for r in range(n_row)]))
+            else:
+                got.append(lax.ppermute(parts[k], both, route))
         return got
 
     chain = [n_col + i for i in range(n_col - 1)]
@@ -462,17 +477,28 @@
             lax.ppermute(x, ("comp", "col"), [(i, i + 1) for i in chain]),
         ]
 
-    coeffs = [traded(send[n_row * c:n_row * (c + 1)]) for c in range(chunks)]
+    coeffs = [traded(send[n_row * c:n_row * (c + 1)], c == chunks // 2, c == chunks - 1 > 0)
+              for c in range(chunks)]
     sides = to_columns(edge)
 
+    halves = 2 if rows % 16 == 0 else 1
+    share = rows // halves
     whole = pl.BlockSpec((rows, lanes), lambda i, s: (0, 0))
-    new_surface, gap = call(
-        functools.partial(surface_kernel, group=2), (1,),
-        [smem, whole, whole, whole, anywhere], [whole] * 2, [sds((rows, lanes), f32)] * 2,
-        (counts, partner, own, remap_source[0], edge), flops=2 * 10**10, size=5 * 4 * rows * lanes,
-    )
-
-    near_parts = [k for k in range(1, n_row) if k & (k + 1) == 0]
+    surfaces = []
+
+    def remap(half, after):
+        piece = pl.BlockSpec((share, lanes), lambda i, s: (half, 0))
+        earlier = surfaces[-1] if surfaces else ()
+        surfaces.append(call(
+            functools.partial(surface_kernel, first=half * share, group=2), (1,),
+            [smem, whole, piece, piece] + [anywhere] * (len(earlier) + len(after)),
+            [piece] * 2, [sds((rows, lanes), f32)] * 2,
+            (counts, partner, own, remap_source[0], *earlier, *after),
+            aliases={5 + i: i for i in range(len(earlier))},
+            flops=10**10, size=3 * 4 * rows * lanes,
+        ))
+
+    remap(0, (edge,))
 
     def sweep(field, rows_in, cols_in, final, extra=()):
         out_shape = [sds((rows * levels, lanes), f32)]
@@ -498,33 +524,37 @@
             scratch=[pltpu.VMEM(((block + 2) * levels, lanes), f32)], size=2 * state_bytes,
         )
 
-    first_step, edge, ends = sweep(mixed, coeffs[0], sides, False)
+    first_step, edge, ends = sweep(mixed, coeffs[chunks // 2], sides, False)
     sides = to_columns(edge)
 
     returned = []
-    for chunk in range(chunks):
-        with_ends = chunk == 0
+    for chunk, width in enumerate(widths):
+        with_ends = chunk == chunks // 2
+        first_wave = sum(widths[:chunk])
         part = call(
-            functools.partial(legendre_kernel, wave_dev=wave_dev, first_wave=chunk * width, with_ends=with_ends),
+            functools.partial(legendre_kernel, wave_dev=wave_dev, first_wave=first_wave, with_ends=with_ends),
             (width,),
             [
                 pl.BlockSpec((1,) + legendre.shape[1:],
-                             lambda i, s, chunk=chunk: (chunk * width + on(0, i, s), 0, 0)),
+                             lambda i, s, first_wave=first_wave: (first_wave + on(0, i, s), 0, 0)),
             ] + [pl.BlockSpec((1, rows, lanes), lambda i, s: (on(0, i, s), 0, 0))] * n_row + ([pl.BlockSpec((2, levels, lanes), lambda i, s: (0, 0, 0)), anywhere] if with_ends else []),
             [pl.BlockSpec((1, rows, lanes), lambda i, s: (on(0, i, s), 0, 0))] * n_row,
             [sds((width, rows, lanes), bf16)] * n_row,
-            (legendre, *coeffs[chunk], *([ends, gap] if with_ends else [])),
+            (legendre, *coeffs[chunk], *([ends, surfaces[0][1]] if with_ends else [])),
             scratch=[pltpu.VMEM((n_row, rows, lanes), bf16)], vmem=63, flops=4 * width * legendre.shape[1] * legendre.shape[2] * lanes,
             size=2 * width * legendre.shape[1] * legendre.shape[2],
         )
-        returned.append(traded(part))
-
-    (sea,) = sweep(first_step, returned[0], sides, True, (gap,))
+        returned.append(traded(part, with_ends, chunk == 0 < chunks - 1))
+
+    if halves > 1:
+        remap(1, (first_step,))
+    new_surface, gap = surfaces[-1]
+    (sea,) = sweep(first_step, returned[chunks // 2], sides, True, (gap,))
 
     state = call(
-        functools.partial(exit_kernel, chunks=chunks, block=block), (steps,),
+        functools.partial(exit_kernel, widths=widths, block=block), (steps,),
         [pl.BlockSpec((tall, lanes), lambda i, s: (on(1, i, s), 0))]
-        + [pl.BlockSpec((width, block, lanes), lambda i, s: (0, on(0, i, s), 0))] * (chunks * n_row),
+        + [pl.BlockSpec((w, block, lanes), lambda i, s: (0, on(0, i, s), 0)) for w in widths for _ in range(n_row)],
         pl.BlockSpec((tall, lanes), lambda i, s: (i, 0)),
         sds((rows * levels, lanes), f32),
         (sea, *sum(returned, [])), scratch=[pltpu.VMEM((256, 256), bf16)], size=2 * state_bytes,

time: 97.6 us -> 129 us (1.32)
  starting transfers between devices: 21.6 us -> 57.1 us
  waiting for transfers between devices: 14.4 us -> 11.1 us
    ppermute x12 -> x22, starting transfers between devices: 10.1 us -> 48 us  [the longest x4 31.8 us: traded(): lax.ppermute(halfway, both, [(n_row + r, r) for r in range(n_row)])]
    ppermute x12 -> x22, waiting for transfers between devices: 14.3 us -> 5.25 us  [the longest x4 4.08 us: traded(): halfway = lax.ppermute(parts[k], both, [(a, n_row + b) for a, b in route])]
    ppermute x2, waiting for transfers between devices: 0.01 us -> 4.43 us  [to_columns(): lax.ppermute(x, ('comp', 'col'), [(i + 1, i) for i in chain])]
    ppermute x2, starting transfers between devices: 8.59 us -> 6.55 us  [to_columns(): lax.ppermute(x, ('comp', 'col'), [(i, i + 1) for i in chain])]
    ppermute x2, waiting for transfers between devices: 0.01 us -> 1.4 us  [to_columns(): lax.ppermute(x, ('comp', 'col'), [(i, i + 1) for i in chain])]
    pallas_call x7 -> x9, Pallas kernels: 57.5 us -> 57.3 us  [call(): pl.pallas_call(functools.partial(kernel, n_row=n_row, n_col=n_col), out_s...]
  transfers between devices with their start and end apart: 17 -> 27, of which waited for: 3 -> 5; matrix products, arithmetic and copies ran while one was open for 0% -> 0% of each run, Pallas kernels for 53% -> 32%
where the time goes in v4:
time: 129 us; the launch traced here: 128 us
  Pallas kernels  57.3 us (44%)
  starting transfers between devices  57.1 us (44%)
  waiting for transfers between devices  11.1 us (9%)
  local copies, waits for them, and re-layouts  1.76 us (1%)
    pallas_call x9, Pallas kernels, call(): pl.pallas_call(functools.partial(kernel, n_row=n_row, n_col=n_col), out_s...  57.3 us
    ppermute x4, starting transfers between devices, traded(): lax.ppermute(halfway, both, [(n_row + r, r) for r in range(n_row)])  31.8 us
    ppermute x14, starting transfers between devices, traded(): got.append(lax.ppermute(parts[k], both, route))  11 us
    ppermute x2, starting transfers between devices, to_columns(): lax.ppermute(x, ('comp', 'col'), [(i, i + 1) for i in chain])  6.55 us
    ppermute x4, starting transfers between devices, traded(): halfway = lax.ppermute(parts[k], both, [(a, n_row + b) for a, b in route])  5.15 us
    ppermute x2, waiting for transfers between devices, to_columns(): lax.ppermute(x, ('comp', 'col'), [(i + 1, i) for i in chain])  4.43 us
    ppermute x4, waiting for transfers between devices, traded(): halfway = lax.ppermute(parts[k], both, [(a, n_row + b) for a, b in route])  4.08 us
  transfers between devices with their start and end apart: 27, of which 5 were waited for; matrix products, arithmetic and copies ran while one was open for 0% of the time, Pallas kernels for 32%

profile of v4, /device:TPU:7, one launch (start us, length us, event | category | flops | bytes accessed | tf_op | source)
XLA Modules:
  0.0 128.3 jit_solution(14421636182946224071)
XLA Ops:
  0.7 9.2 %shard_map.86 = (bf16[3,320,128]{2,1,0:T(8,128)(2,1)}, bf16[3,320,128]{2,1,0:T(8,128)(2,1)}, bf16[3,320,128]{2,1,0:T(8,128)(2,1)}, bf16[3,320,128]{2,1,0:T(8,128...) custom-call(s32[1]{0:T(128)} %bitcast.place, ...), custom_call_target="tpu_custom_call" | custom-call | flops 10000000 | bytes 10485760 | tf_op jit(solution)/shard_map/pallas_call | solution.py:421
  11.5 3.2 %collective-permute-start.1 = (bf16[5,32,128]{2,1,0:T(8,128)(2,1)}, bf16[5,32,128]{2,1,0:T(8,128)(2,1)S(1)}, u32[]{:S(2)}, u32[]{:S(2)}) collective-permute-start(bf16[5,32,128]{2,1,0:T(8,128)(2,1)} %get-tuple-element.36.rest_0_), channel_id=1, source_target_pairs={{16,17},{17,18},{18,19},{20,21},{21,22},{22,23},{24,25},{25,26},{2... | collective-permute-start | bytes 122888 | tf_op jit(solution)/shard_map/ppermute | solution.py:477
  14.7 1.4 %collective-permute-done.1.west_in = bf16[5,32,128]{2,1,0:T(8,128)(2,1)S(1)} collective-permute-done((bf16[5,32,128]{2,1,0:T(8,128)(2,1)}, bf16[5,32,128]{2,1,0:T(8,128)(2,1)S(1)}, u32[]{:S(2)}, u32[]{:S(2)}) %collective-permute-start.1) | collective-permute-done | bytes 40992 | tf_op jit(solution)/shard_map/ppermute | solution.py:477
  17.4 4.1 %collective-permute-done.east_in = bf16[5,32,128]{2,1,0:T(8,128)(2,1)S(1)} collective-permute-done((bf16[5,32,128]{2,1,0:T(8,128)(2,1)}, bf16[5,32,128]{2,1,0:T(8,128)(2,1)S(1)}, u32[]{:S(2)}, u32[]{:S(2)}) %collective-permute-start) | collective-permute-done | bytes 40992 | tf_op jit(solution)/shard_map/ppermute | solution.py:476
  22.3 9.9 %shard_map.87 = (f32[10240,128]{1,0:T(8,128)}, bf16[5,32,128]{2,1,0:T(8,128)(2,1)}, bf16[2,32,128]{2,1,0:T(8,128)(2,1)}) custom-call(s32[1]{0:T(128)} %bitcast.place, s32[1,320]{1,0:T(1,128)} %bitcast.11, f32[10240,128]{1,0:T(8,128)} %get-tuple-element.35.field.above.below, f32[10240,128]{1,0:T(8,128)} %get-tuple-element.35.field.above.below, ...), custom_call_target="tpu_custom_call" | custom-call | flops 10000000 | bytes 10485760 | tf_op jit(solution)/shard_map/pallas_call | solution.py:421
  32.1 3.3 %collective-permute-start.5 = (bf16[5,32,128]{2,1,0:T(8,128)(2,1)}, bf16[5,32,128]{2,1,0:T(8,128)(2,1)S(1)}, u32[]{:S(2)}, u32[]{:S(2)}) collective-permute-start(bf16[5,32,128]{2,1,0:T(8,128)(2,1)} %get-tuple-element.40), channel_id=1, source_target_pairs={{16,17},{17,18},{18,19},{20,21},{21,22},{22,23},{24,25},{25,26},{2... | collective-permute-start | bytes 122888 | tf_op jit(solution)/shard_map/ppermute | solution.py:477
  36.9 1.4 %collective-permute-start.12 = (bf16[3,320,128]{2,1,0:T(8,128)(2,1)}, bf16[3,320,128]{2,1,0:T(8,128)(2,1)}, u32[]{:S(2)}, u32[]{:S(2)}) collective-permute-start(bf16[3,320,128]{2,1,0:T(8,128)(2,1)} %get-tuple-element.52), channel_id=1, source_target_pairs={{0,12},{4,8},{8,4},{12,0},{1,13},{5,9},{9,5},{13,1},{2,14},{6,10},... | collective-permute-start | bytes 737288 | tf_op jit(solution)/shard_map/ppermute | solution.py:469
  39.6 1.3 %collective-permute-start.22 = (bf16[3,320,128]{2,1,0:T(8,128)(2,1)S(1)}, bf16[3,320,128]{2,1,0:T(8,128)(2,1)}, u32[]{:S(2)}, u32[]{:S(2)}) collective-permute-start(bf16[3,320,128]{2,1,0:T(8,128)(2,1)S(1)} %copy-done.19), channel_id=1, source_target_pairs={{0,28},{4,24},{8,20},{12,16},{1,29},{5,25},{9,21},{13,17},{2,30},{... | collective-permute-start | bytes 737288 | tf_op jit(solution)/shard_map/ppermute | solution.py:466
  40.9 7.2 %shard_map.88 = (f32[320,128]{1,0:T(8,128)}, f32[320,128]{1,0:T(8,128)}) custom-call(s32[1]{0:T(128)} %bitcast.place, s32[1,320]{1,0:T(1,128)} %bitcast.12, f32[320,128]{1,0:T(8,128)} %copy-done.23, f32[320,128]{1,0:T(8,128)} %bitcast.15, s32[320,128]{1,0:T(8,128)} %bitcast.18, bf16[5,32,128]{2,1,0:T(8,128)(2,1)} %get-tuple-element.36.rest_0_), custom_call_target="tpu_custom_call" | custom-call | flops 10000000000 | bytes 491520 | tf_op jit(solution)/shard_map/pallas_call | solution.py:421
  48.9 10.5 %collective-permute-start.21 = (bf16[3,320,128]{2,1,0:T(8,128)(2,1)}, bf16[3,320,128]{2,1,0:T(8,128)(2,1)S(1)}, u32[]{:S(2)}, u32[]{:S(2)}) collective-permute-start(bf16[3,320,128]{2,1,0:T(8,128)(2,1)} %collective-permute-done.20), channel_id=1, source_target_pairs={{16,0},{20,4},{24,8},{28,12},{17,1},{21,5},{25,9},{29,13},{18,2},{... | collective-permute-start | bytes 737288 | tf_op jit(solution)/shard_map/ppermute | solution.py:467
  59.4 2.0 %collective-permute-start.23 = (bf16[3,320,128]{2,1,0:T(8,128)(2,1)}, bf16[3,320,128]{2,1,0:T(8,128)(2,1)}, u32[]{:S(2)}, u32[]{:S(2)}) collective-permute-start(bf16[3,320,128]{2,1,0:T(8,128)(2,1)} %collective-permute-done.22), channel_id=1, source_target_pairs={{16,0},{20,4},{24,8},{28,12},{17,1},{21,5},{25,9},{29,13},{18,2},{... | collective-permute-start | bytes 737288 | tf_op jit(solution)/shard_map/ppermute | solution.py:467
  61.4 3.0 %shard_map.89 = (bf16[2,320,128]{2,1,0:T(8,128)(2,1)}, bf16[2,320,128]{2,1,0:T(8,128)(2,1)}, bf16[2,320,128]{2,1,0:T(8,128)(2,1)}, bf16[2,320,128]{2,1,0:T(8,128)(2,1)}) custom-call(s32[1]{0:T(128)} %bitcast.place, bf16[8,1280,1280]{2,1,0:T(8,128)(2,1)} %legendre.5, bf16[2,320,128]{2,1,0:T(8,128)(2,1)} %get-tuple-element.41.rest_0_, ...), custom_call_target="tpu_custom_call" | custom-call | flops 1677721600 | bytes 6553600 | tf_op jit(solution)/shard_map/pallas_call | solution.py:421
  64.4 1.3 %collective-permute-start.4 = (bf16[5,32,128]{2,1,0:T(8,128)(2,1)S(1)}, bf16[5,32,128]{2,1,0:T(8,128)(2,1)S(1)}, u32[]{:S(2)}, u32[]{:S(2)}) collective-permute-start(bf16[5,32,128]{2,1,0:T(8,128)(2,1)S(1)} %copy-done.24), channel_id=1, source_target_pairs={{17,16},{18,17},{19,18},{21,20},{22,21},{23,22},{25,24},{26,25},{2... | collective-permute-start | bytes 122888 | tf_op jit(solution)/shard_map/ppermute | solution.py:476
  66.1 2.8 %shard_map.92 = (bf16[3,320,128]{2,1,0:T(8,128)(2,1)}, bf16[3,320,128]{2,1,0:T(8,128)(2,1)}, bf16[3,320,128]{2,1,0:T(8,128)(2,1)}, bf16[3,320,128]{2,1,0:T(8,128)(2,1)}) custom-call(s32[1]{0:T(128)} %bitcast.place, bf16[8,1280,1280]{2,1,0:T(8,128)(2,1)} %legendre.5, bf16[3,320,128]{2,1,0:T(8,128)(2,1)} %get-tuple-element.49.rest_0_, ...), custom_call_target="tpu_custom_call" | custom-call | flops 2516582400 | bytes 9830400 | tf_op jit(solution)/shard_map/pallas_call | solution.py:421
  69.2 1.4 %collective-permute-start.13 = (bf16[3,320,128]{2,1,0:T(8,128)(2,1)}, bf16[3,320,128]{2,1,0:T(8,128)(2,1)}, u32[]{:S(2)}, u32[]{:S(2)}) collective-permute-start(bf16[3,320,128]{2,1,0:T(8,128)(2,1)} %get-tuple-element.54), channel_id=1, source_target_pairs={{0,4},{4,0},{8,12},{12,8},{1,5},{5,1},{9,13},{13,9},{2,6},{6,2},{1... | collective-permute-start | bytes 737288 | tf_op jit(solution)/shard_map/ppermute | solution.py:469
  71.8 1.3 %collective-permute-start.16 = (bf16[3,320,128]{2,1,0:T(8,128)(2,1)}, bf16[3,320,128]{2,1,0:T(8,128)(2,1)}, u32[]{:S(2)}, u32[]{:S(2)}) collective-permute-start(bf16[3,320,128]{2,1,0:T(8,128)(2,1)} %get-tuple-element.56), channel_id=1, source_target_pairs={{0,28},{4,24},{8,20},{12,16},{1,29},{5,25},{9,21},{13,17},{2,30},{... | collective-permute-start | bytes 737288 | tf_op jit(solution)/shard_map/ppermute | solution.py:466
  73.2 1.6 %collective-permute-start.9 = (bf16[2,320,128]{2,1,0:T(8,128)(2,1)}, bf16[2,320,128]{2,1,0:T(8,128)(2,1)S(1)}, u32[]{:S(2)}, u32[]{:S(2)}) collective-permute-start(bf16[2,320,128]{2,1,0:T(8,128)(2,1)} %get-tuple-element.46), channel_id=1, source_target_pairs={{0,12},{4,8},{8,4},{12,0},{16,28},{20,24},{24,20},{28,16},{1,13},{... | collective-permute-start | bytes 491528 | tf_op jit(solution)/shard_map/ppermute | solution.py:469
  75.5 2.9 %shard_map.93 = (bf16[3,320,128]{2,1,0:T(8,128)(2,1)}, bf16[3,320,128]{2,1,0:T(8,128)(2,1)}, bf16[3,320,128]{2,1,0:T(8,128)(2,1)}, bf16[3,320,128]{2,1,0:T(8,128)(2,1)}) custom-call(s32[1]{0:T(128)} %bitcast.place, bf16[8,1280,1280]{2,1,0:T(8,128)(2,1)} %legendre.5, bf16[3,320,128]{2,1,0:T(8,128)(2,1)} %get-tuple-element.59.rest_0_, ...), custom_call_target="tpu_custom_call" | custom-call | flops 2516582400 | bytes 9830400 | tf_op jit(solution)/shard_map/pallas_call | solution.py:421
  81.6 4.1 %collective-permute-done.14 = bf16[3,320,128]{2,1,0:T(8,128)(2,1)} collective-permute-done((bf16[3,320,128]{2,1,0:T(8,128)(2,1)}, bf16[3,320,128]{2,1,0:T(8,128)(2,1)}, u32[]{:S(2)}, u32[]{:S(2)}) %collective-permute-start.14) | collective-permute-done | bytes 245792 | tf_op jit(solution)/shard_map/ppermute | solution.py:466
  85.6 18.0 %collective-permute-start.15 = (bf16[3,320,128]{2,1,0:T(8,128)(2,1)}, bf16[3,320,128]{2,1,0:T(8,128)(2,1)S(1)}, u32[]{:S(2)}, u32[]{:S(2)}) collective-permute-start(bf16[3,320,128]{2,1,0:T(8,128)(2,1)} %collective-permute-done.14), channel_id=1, source_target_pairs={{16,0},{20,4},{24,8},{28,12},{17,1},{21,5},{25,9},{29,13},{18,2},{... | collective-permute-start | bytes 737288 | tf_op jit(solution)/shard_map/ppermute | solution.py:467
  103.6 1.3 %collective-permute-start.17 = (bf16[3,320,128]{2,1,0:T(8,128)(2,1)}, bf16[3,320,128]{2,1,0:T(8,128)(2,1)S(1)}, u32[]{:S(2)}, u32[]{:S(2)}) collective-permute-start(bf16[3,320,128]{2,1,0:T(8,128)(2,1)} %collective-permute-done.16), channel_id=1, source_target_pairs={{16,0},{20,4},{24,8},{28,12},{17,1},{21,5},{25,9},{29,13},{18,2},{... | collective-permute-start | bytes 737288 | tf_op jit(solution)/shard_map/ppermute | solution.py:467
  104.9 7.2 %shard_map.90 = (f32[320,128]{1,0:T(8,128)}, f32[320,128]{1,0:T(8,128)}) custom-call(s32[1]{0:T(128)} %bitcast.place, s32[1,320]{1,0:T(1,128)} %bitcast.13, f32[320,128]{1,0:T(8,128)} %copy-done.23, f32[320,128]{1,0:T(8,128)} %bitcast.16, s32[320,128]{1,0:T(8,128)} %bitcast.19, ...), custom_call_target="tpu_custom_call", output_to_operand_aliasing={{0}: (5, {}), {1}: (6, {})} | custom-call | flops 10000000000 | bytes 491520 | tf_op jit(solution)/shard_map/pallas_call | solution.py:421
  112.1 8.5 %shard_map.91.sea = f32[10240,128]{1,0:T(8,128)} custom-call(s32[1]{0:T(128)} %bitcast.place, s32[1,320]{1,0:T(1,128)} %bitcast.14, f32[10240,128]{1,0:T(8,128)} %get-tuple-element.39.rest_2_.field.above.below, f32[10240,128]{1,0:T(8,128)} %get-tuple-element.39.rest_2_.field.above.below, f32[10240,128]{1,0:T(8,128)} %get-tuple-element.39.rest_2_.field.above.below, ...), custom_call_target="tpu_custom_call" | custom-call | flops 10000000 | bytes 10485760 | tf_op jit(solution)/shard_map/pallas_call | solution.py:421
  121.7 6.7 %shard_map.94 = f32[10240,128]{1,0:T(8,128)} custom-call(s32[1]{0:T(128)} %bitcast.place, f32[10240,128]{1,0:T(8,128)} %shard_map.91.sea, bf16[3,320,128]{2,1,0:T(8,128)(2,1)} %get-tuple-element.53.rest_0_, bf16[3,320,128]{2,1,0:T(8,128)(2,1)} %collective-permute-done.13.rest_1_, bf16[3,320,128]{2,1,0:T(8,128)(2,1)} %copy-done.11, ...), custom_call_target="tpu_custom_call" | custom-call | flops 10000000 | bytes 10485760 | tf_op jit(solution)/shard_map/pallas_call | solution.py:421
  (89 shorter events, 13.7 us)
Async XLA Ops:
  9.9 11.7 %collective-permute-start.2 = (bf16[2,320,128]{2,1,0:T(8,128)(2,1)}, bf16[2,320,128]{2,1,0:T(8,128)(2,1)S(1)}, u32[]{:S(2)}, u32[]{:S(2)}) collective-permute-start(bf16[2,320,128]{2,1,0:T(8,128)(2,1)} %get-tuple-element.37), channel_id=1, source_target_pairs={{0,4},{4,0},{8,12},{12,8},{16,20},{20,16},{24,28},{28,24},{1,5},{5... | collective-permute-start | bytes 491528 | tf_op jit(solution)/shard_map/ppermute | solution.py:469
  10.6 10.9 %collective-permute-start.3 = (bf16[2,320,128]{2,1,0:T(8,128)(2,1)}, bf16[2,320,128]{2,1,0:T(8,128)(2,1)S(1)}, u32[]{:S(2)}, u32[]{:S(2)}) collective-permute-start(bf16[2,320,128]{2,1,0:T(8,128)(2,1)} %get-tuple-element.38), channel_id=1, source_target_pairs={{0,12},{4,8},{8,4},{12,0},{16,28},{20,24},{24,20},{28,16},{1,13},{... | collective-permute-start | bytes 491528 | tf_op jit(solution)/shard_map/ppermute | solution.py:469
  10.8 26.1 %collective-permute-start.7 = (f32[320,128]{1,0:T(8,128)S(1)}, f32[320,128]{1,0:T(8,128)S(1)}, u32[]{:S(2)}, u32[]{:S(2)}) collective-permute-start(f32[320,128]{1,0:T(8,128)S(1)} %bitcast.17), channel_id=1, source_target_pairs={{0,16},{16,0},{1,17},{17,1},{2,18},{18,2},{3,19},{19,3},{4,20},{20... | collective-permute-start | bytes 491528 | tf_op jit(solution)/shard_map/ppermute | solution.py:415
  10.8 27.5 %collective-permute-start.6 = (bf16[2,320,128]{2,1,0:T(8,128)(2,1)}, bf16[2,320,128]{2,1,0:T(8,128)(2,1)S(1)}, u32[]{:S(2)}, u32[]{:S(2)}) collective-permute-start(bf16[2,320,128]{2,1,0:T(8,128)(2,1)} %get-tuple-element.42), channel_id=1, source_target_pairs={{0,8},{4,12},{8,0},{12,4},{1,9},{5,13},{9,1},{13,5},{2,10},{6,14},... | collective-permute-start | bytes 491528 | tf_op jit(solution)/shard_map/ppermute | solution.py:469
  16.1 5.4 %collective-permute-start = (bf16[5,32,128]{2,1,0:T(8,128)(2,1)}, bf16[5,32,128]{2,1,0:T(8,128)(2,1)S(1)}, u32[]{:S(2)}, u32[]{:S(2)}) collective-permute-start(bf16[5,32,128]{2,1,0:T(8,128)(2,1)} %get-tuple-element.36.rest_0_), channel_id=1, source_target_pairs={{17,16},{18,17},{19,18},{21,20},{22,21},{23,22},{25,24},{26,25},{2... | collective-permute-start | bytes 122888 | tf_op jit(solution)/shard_map/ppermute | solution.py:476
  32.1 7.4 %collective-permute-start.5 = (bf16[5,32,128]{2,1,0:T(8,128)(2,1)}, bf16[5,32,128]{2,1,0:T(8,128)(2,1)S(1)}, u32[]{:S(2)}, u32[]{:S(2)}) collective-permute-start(bf16[5,32,128]{2,1,0:T(8,128)(2,1)} %get-tuple-element.40), channel_id=1, source_target_pairs={{16,17},{17,18},{18,19},{20,21},{21,22},{22,23},{24,25},{25,26},{2... | collective-permute-start | bytes 122888 | tf_op jit(solution)/shard_map/ppermute | solution.py:477
  35.5 12.6 %collective-permute-start.10 = (bf16[3,320,128]{2,1,0:T(8,128)(2,1)S(1)}, bf16[3,320,128]{2,1,0:T(8,128)(2,1)S(1)}, u32[]{:S(2)}, u32[]{:S(2)}) collective-permute-start(bf16[3,320,128]{2,1,0:T(8,128)(2,1)S(1)} %copy-done.21), channel_id=1, source_target_pairs={{0,4},{4,0},{8,12},{12,8},{1,5},{5,1},{9,13},{13,9},{2,6},{6,2},{1... | collective-permute-start | bytes 737288 | tf_op jit(solution)/shard_map/ppermute | solution.py:469
  36.2 28.2 %collective-permute-start.11 = (bf16[3,320,128]{2,1,0:T(8,128)(2,1)}, bf16[3,320,128]{2,1,0:T(8,128)(2,1)S(1)}, u32[]{:S(2)}, u32[]{:S(2)}) collective-permute-start(bf16[3,320,128]{2,1,0:T(8,128)(2,1)} %get-tuple-element.51), channel_id=1, source_target_pairs={{0,8},{4,12},{8,0},{12,4},{1,9},{5,13},{9,1},{13,5},{2,10},{6,14},... | collective-permute-start | bytes 737288 | tf_op jit(solution)/shard_map/ppermute | solution.py:469
  36.9 28.8 %collective-permute-start.12 = (bf16[3,320,128]{2,1,0:T(8,128)(2,1)}, bf16[3,320,128]{2,1,0:T(8,128)(2,1)}, u32[]{:S(2)}, u32[]{:S(2)}) collective-permute-start(bf16[3,320,128]{2,1,0:T(8,128)(2,1)} %get-tuple-element.52), channel_id=1, source_target_pairs={{0,12},{4,8},{8,4},{12,0},{1,13},{5,9},{9,5},{13,1},{2,14},{6,10},... | collective-permute-start | bytes 737288 | tf_op jit(solution)/shard_map/ppermute | solution.py:469
  38.3 10.6 %collective-permute-start.20 = (bf16[3,320,128]{2,1,0:T(8,128)(2,1)S(1)}, bf16[3,320,128]{2,1,0:T(8,128)(2,1)}, u32[]{:S(2)}, u32[]{:S(2)}) collective-permute-start(bf16[3,320,128]{2,1,0:T(8,128)(2,1)S(1)} %copy-done.20), channel_id=1, source_target_pairs={{0,24},{4,28},{8,16},{12,20},{1,25},{5,29},{9,17},{13,21},{2,26},{... | collective-permute-start | bytes 737288 | tf_op jit(solution)/shard_map/ppermute | solution.py:466
  39.6 19.8 %collective-permute-start.22 = (bf16[3,320,128]{2,1,0:T(8,128)(2,1)S(1)}, bf16[3,320,128]{2,1,0:T(8,128)(2,1)}, u32[]{:S(2)}, u32[]{:S(2)}) collective-permute-start(bf16[3,320,128]{2,1,0:T(8,128)(2,1)S(1)} %copy-done.19), channel_id=1, source_target_pairs={{0,28},{4,24},{8,20},{12,16},{1,29},{5,25},{9,21},{13,17},{2,30},{... | collective-permute-start | bytes 737288 | tf_op jit(solution)/shard_map/ppermute | solution.py:466
  48.2 22.4 %collective-permute-start.19 = (bf16[3,320,128]{2,1,0:T(8,128)(2,1)}, bf16[3,320,128]{2,1,0:T(8,128)(2,1)S(1)}, u32[]{:S(2)}, u32[]{:S(2)}) collective-permute-start(bf16[3,320,128]{2,1,0:T(8,128)(2,1)} %get-tuple-element.60), channel_id=1, source_target_pairs={{0,4},{4,0},{8,12},{12,8},{1,5},{5,1},{9,13},{13,9},{2,6},{6,2},{1... | collective-permute-start | bytes 737288 | tf_op jit(solution)/shard_map/ppermute | solution.py:469
  48.9 24.3 %collective-permute-start.21 = (bf16[3,320,128]{2,1,0:T(8,128)(2,1)}, bf16[3,320,128]{2,1,0:T(8,128)(2,1)S(1)}, u32[]{:S(2)}, u32[]{:S(2)}) collective-permute-start(bf16[3,320,128]{2,1,0:T(8,128)(2,1)} %collective-permute-done.20), channel_id=1, source_target_pairs={{16,0},{20,4},{24,8},{28,12},{17,1},{21,5},{25,9},{29,13},{18,2},{... | collective-permute-start | bytes 737288 | tf_op jit(solution)/shard_map/ppermute | solution.py:467
  59.4 15.4 %collective-permute-start.23 = (bf16[3,320,128]{2,1,0:T(8,128)(2,1)}, bf16[3,320,128]{2,1,0:T(8,128)(2,1)}, u32[]{:S(2)}, u32[]{:S(2)}) collective-permute-start(bf16[3,320,128]{2,1,0:T(8,128)(2,1)} %collective-permute-done.22), channel_id=1, source_target_pairs={{16,0},{20,4},{24,8},{28,12},{17,1},{21,5},{25,9},{29,13},{18,2},{... | collective-permute-start | bytes 737288 | tf_op jit(solution)/shard_map/ppermute | solution.py:467
  65.7 6.1 %collective-permute-start.8 = (bf16[2,320,128]{2,1,0:T(8,128)(2,1)}, bf16[2,320,128]{2,1,0:T(8,128)(2,1)S(1)}, u32[]{:S(2)}, u32[]{:S(2)}) collective-permute-start(bf16[2,320,128]{2,1,0:T(8,128)(2,1)} %get-tuple-element.45), channel_id=1, source_target_pairs={{0,4},{4,0},{8,12},{12,8},{16,20},{20,16},{24,28},{28,24},{1,5},{5... | collective-permute-start | bytes 491528 | tf_op jit(solution)/shard_map/ppermute | solution.py:469
  69.2 11.7 %collective-permute-start.13 = (bf16[3,320,128]{2,1,0:T(8,128)(2,1)}, bf16[3,320,128]{2,1,0:T(8,128)(2,1)}, u32[]{:S(2)}, u32[]{:S(2)}) collective-permute-start(bf16[3,320,128]{2,1,0:T(8,128)(2,1)} %get-tuple-element.54), channel_id=1, source_target_pairs={{0,4},{4,0},{8,12},{12,8},{1,5},{5,1},{9,13},{13,9},{2,6},{6,2},{1... | collective-permute-start | bytes 737288 | tf_op jit(solution)/shard_map/ppermute | solution.py:469
  70.5 15.1 %collective-permute-start.14 = (bf16[3,320,128]{2,1,0:T(8,128)(2,1)}, bf16[3,320,128]{2,1,0:T(8,128)(2,1)}, u32[]{:S(2)}, u32[]{:S(2)}) collective-permute-start(bf16[3,320,128]{2,1,0:T(8,128)(2,1)} %get-tuple-element.55), channel_id=1, source_target_pairs={{0,24},{4,28},{8,16},{12,20},{1,25},{5,29},{9,17},{13,21},{2,26},{... | collective-permute-start | bytes 737288 | tf_op jit(solution)/shard_map/ppermute | solution.py:466
  71.8 31.8 %collective-permute-start.16 = (bf16[3,320,128]{2,1,0:T(8,128)(2,1)}, bf16[3,320,128]{2,1,0:T(8,128)(2,1)}, u32[]{:S(2)}, u32[]{:S(2)}) collective-permute-start(bf16[3,320,128]{2,1,0:T(8,128)(2,1)} %get-tuple-element.56), channel_id=1, source_target_pairs={{0,28},{4,24},{8,20},{12,16},{1,29},{5,25},{9,21},{13,17},{2,30},{... | collective-permute-start | bytes 737288 | tf_op jit(solution)/shard_map/ppermute | solution.py:466
  73.2 6.3 %collective-permute-start.9 = (bf16[2,320,128]{2,1,0:T(8,128)(2,1)}, bf16[2,320,128]{2,1,0:T(8,128)(2,1)S(1)}, u32[]{:S(2)}, u32[]{:S(2)}) collective-permute-start(bf16[2,320,128]{2,1,0:T(8,128)(2,1)} %get-tuple-element.46), channel_id=1, source_target_pairs={{0,12},{4,8},{8,4},{12,0},{16,28},{20,24},{24,20},{28,16},{1,13},{... | collective-permute-start | bytes 491528 | tf_op jit(solution)/shard_map/ppermute | solution.py:469
  79.5 41.1 %collective-permute-start.24 = (bf16[3,320,128]{2,1,0:T(8,128)(2,1)}, bf16[3,320,128]{2,1,0:T(8,128)(2,1)S(1)}, u32[]{:S(2)}, u32[]{:S(2)}) collective-permute-start(bf16[3,320,128]{2,1,0:T(8,128)(2,1)} %get-tuple-element.64), channel_id=1, source_target_pairs={{0,4},{4,0},{8,12},{12,8},{1,5},{5,1},{9,13},{13,9},{2,6},{6,2},{1... | collective-permute-start | bytes 737288 | tf_op jit(solution)/shard_map/ppermute | solution.py:469
  80.2 40.5 %collective-permute-start.25 = (bf16[3,320,128]{2,1,0:T(8,128)(2,1)}, bf16[3,320,128]{2,1,0:T(8,128)(2,1)S(1)}, u32[]{:S(2)}, u32[]{:S(2)}) collective-permute-start(bf16[3,320,128]{2,1,0:T(8,128)(2,1)} %get-tuple-element.65), channel_id=1, source_target_pairs={{0,8},{4,12},{8,0},{12,4},{1,9},{5,13},{9,1},{13,5},{2,10},{6,14},... | collective-permute-start | bytes 737288 | tf_op jit(solution)/shard_map/ppermute | solution.py:469
  80.9 39.8 %collective-permute-start.26 = (bf16[3,320,128]{2,1,0:T(8,128)(2,1)}, bf16[3,320,128]{2,1,0:T(8,128)(2,1)S(1)}, u32[]{:S(2)}, u32[]{:S(2)}) collective-permute-start(bf16[3,320,128]{2,1,0:T(8,128)(2,1)} %get-tuple-element.66), channel_id=1, source_target_pairs={{0,12},{4,8},{8,4},{12,0},{1,13},{5,9},{9,5},{13,1},{2,14},{6,10},... | collective-permute-start | bytes 737288 | tf_op jit(solution)/shard_map/ppermute | solution.py:469
  85.6 35.0 %collective-permute-start.15 = (bf16[3,320,128]{2,1,0:T(8,128)(2,1)}, bf16[3,320,128]{2,1,0:T(8,128)(2,1)S(1)}, u32[]{:S(2)}, u32[]{:S(2)}) collective-permute-start(bf16[3,320,128]{2,1,0:T(8,128)(2,1)} %collective-permute-done.14), channel_id=1, source_target_pairs={{16,0},{20,4},{24,8},{28,12},{17,1},{21,5},{25,9},{29,13},{18,2},{... | collective-permute-start | bytes 737288 | tf_op jit(solution)/shard_map/ppermute | solution.py:467
  103.6 17.0 %collective-permute-start.17 = (bf16[3,320,128]{2,1,0:T(8,128)(2,1)}, bf16[3,320,128]{2,1,0:T(8,128)(2,1)S(1)}, u32[]{:S(2)}, u32[]{:S(2)}) collective-permute-start(bf16[3,320,128]{2,1,0:T(8,128)(2,1)} %collective-permute-done.16), channel_id=1, source_target_pairs={{16,0},{20,4},{24,8},{28,12},{17,1},{21,5},{25,9},{29,13},{18,2},{... | collective-permute-start | bytes 737288 | tf_op jit(solution)/shard_map/ppermute | solution.py:467
  (28 other events, 192.9 us)

commit v5 on v4

--- a/solution.py
+++ b/solution.py
@@ -13,8 +13,7 @@
 
 
 def chunk_widths(wave_dev):
-    outer = 3 * wave_dev // 8
-    return (outer, wave_dev - 2 * outer, outer) if outer else (wave_dev,)
+    return (wave_dev - wave_dev // 2, wave_dev // 2) if wave_dev > 1 else (wave_dev,)
 
 
 def chunk_of(local, widths):
@@ -186,7 +185,7 @@
             top = mixed_rows(field, 0, 0)[0][1]
             low = mixed_rows(last, 0, total - 8)[-1][1]
             for part in range(1, n_row):
-                send[chunks // 2][part][0, 0:levels, :] = jnp.where((part ^ row) > row, low, top)
+                send[0][part][0, 0:levels, :] = jnp.where((part ^ row) > row, low, top)
 
 
 def sweep_kernel(place, counts, field, above, below, east_in, west_in, *rest, block, n_row, n_col, near_parts, final):
@@ -454,19 +453,11 @@
     )
 
     near_parts = [k for k in range(1, n_row) if k & (k + 1) == 0]
-    both = ("comp", "row")
-
-    def traded(parts, with_edges, relayed):
+
+    def traded(parts):
         got = [parts[0]]
         for k in range(1, n_row):
-            route = [(r, r ^ k) for r in range(n_row)]
-            if with_edges and k in near_parts:
-                route += [(n_row + a, n_row + b) for a, b in route]
-            if relayed and k > 1:
-                halfway = lax.ppermute(parts[k], both, [(a, n_row + b) for a, b in route])
-                got.append(lax.ppermute(halfway, both, [(n_row + r, r) for r in range(n_row)]))
-            else:
-                got.append(lax.ppermute(parts[k], both, route))
+            got.append(lax.ppermute(parts[k], "row", [(r, r ^ k) for r in range(n_row)]))
         return got
 
     chain = [n_col + i for i in range(n_col - 1)]
@@ -477,8 +468,7 @@
             lax.ppermute(x, ("comp", "col"), [(i, i + 1) for i in chain]),
         ]
 
-    coeffs = [traded(send[n_row * c:n_row * (c + 1)], c == chunks // 2, c == chunks - 1 > 0)
-              for c in range(chunks)]
+    coeffs = [traded(send[n_row * c:n_row * (c + 1)]) for c in range(chunks)]
     sides = to_columns(edge)
 
     halves = 2 if rows % 16 == 0 else 1
@@ -524,12 +514,12 @@
             scratch=[pltpu.VMEM(((block + 2) * levels, lanes), f32)], size=2 * state_bytes,
         )
 
-    first_step, edge, ends = sweep(mixed, coeffs[chunks // 2], sides, False)
+    first_step, edge, ends = sweep(mixed, coeffs[0], sides, False)
     sides = to_columns(edge)
 
     returned = []
     for chunk, width in enumerate(widths):
-        with_ends = chunk == chunks // 2
+        with_ends = chunk == 0
         first_wave = sum(widths[:chunk])
         part = call(
             functools.partial(legendre_kernel, wave_dev=wave_dev, first_wave=first_wave, with_ends=with_ends),
@@ -544,12 +534,12 @@
             scratch=[pltpu.VMEM((n_row, rows, lanes), bf16)], vmem=63, flops=4 * width * legendre.shape[1] * legendre.shape[2] * lanes,
             size=2 * width * legendre.shape[1] * legendre.shape[2],
         )
-        returned.append(traded(part, with_ends, chunk == 0 < chunks - 1))
+        returned.append(traded(part))
 
     if halves > 1:
         remap(1, (first_step,))
     new_surface, gap = surfaces[-1]
-    (sea,) = sweep(first_step, returned[chunks // 2], sides, True, (gap,))
+    (sea,) = sweep(first_step, returned[0], sides, True, (gap,))
 
     state = call(
         functools.partial(exit_kernel, widths=widths, block=block), (steps,),

time: 129 us -> 93.3 us (0.72)
  starting transfers between devices: 57.1 us -> 20.3 us
  waiting for transfers between devices: 11.1 us -> 14.2 us
  Pallas kernels: 57.3 us -> 54.5 us
    ppermute x22 -> x12, starting transfers between devices: 48 us -> 9.47 us  [traded(): lax.ppermute(parts[k], 'row', [(r, r ^ k) for r in range(n_row)])]
    ppermute x22 -> x12, waiting for transfers between devices: 5.25 us -> 14.2 us  [traded(): lax.ppermute(parts[k], 'row', [(r, r ^ k) for r in range(n_row)])]
    ppermute x2, waiting for transfers between devices: 4.43 us -> 0.01 us  [to_columns(): lax.ppermute(x, ('comp', 'col'), [(i + 1, i) for i in chain])]
    pallas_call x9 -> x8, Pallas kernels: 57.3 us -> 54.5 us  [call(): pl.pallas_call(functools.partial(kernel, n_row=n_row, n_col=n_col), out_s...]
    ppermute x2, starting transfers between devices: 6.55 us -> 7.98 us  [to_columns(): lax.ppermute(x, ('comp', 'col'), [(i, i + 1) for i in chain])]
    ppermute x2, waiting for transfers between devices: 1.4 us -> 0.01 us  [to_columns(): lax.ppermute(x, ('comp', 'col'), [(i, i + 1) for i in chain])]
  transfers between devices with their start and end apart: 27 -> 17, of which waited for: 5 -> 2; matrix products, arithmetic and copies ran while one was open for 0% -> 0% of each run, Pallas kernels for 32% -> 52%
where the time goes in v5:
time: 93.3 us; the launch traced here: 92.4 us
  Pallas kernels  54.5 us (58%)
  starting transfers between devices  20.3 us (22%)
  waiting for transfers between devices  14.2 us (15%)
  local copies, waits for them, and re-layouts  2.49 us (3%)
    pallas_call x8, Pallas kernels, call(): pl.pallas_call(functools.partial(kernel, n_row=n_row, n_col=n_col), out_s...  54.5 us
    ppermute x12, waiting for transfers between devices, traded(): lax.ppermute(parts[k], 'row', [(r, r ^ k) for r in range(n_row)])  14.2 us
    ppermute x12, starting transfers between devices, traded(): lax.ppermute(parts[k], 'row', [(r, r ^ k) for r in range(n_row)])  9.47 us
    ppermute x2, starting transfers between devices, to_columns(): lax.ppermute(x, ('comp', 'col'), [(i, i + 1) for i in chain])  7.98 us
    ppermute x2, starting transfers between devices, to_columns(): lax.ppermute(x, ('comp', 'col'), [(i + 1, i) for i in chain])  2.57 us
    unnamed x30, local copies, waits for them, and re-layouts  2.49 us
  transfers between devices with their start and end apart: 17, of which 2 were waited for; matrix products, arithmetic and copies ran while one was open for 0% of the time, Pallas kernels for 52%

profile of v5, /device:TPU:7, one launch (start us, length us, event | category | flops | bytes accessed | tf_op | source)
XLA Modules:
  0.0 92.4 jit_solution(5320249274671413653)
XLA Ops:
  0.9 9.2 %shard_map.86 = (bf16[4,320,128]{2,1,0:T(8,128)(2,1)}, bf16[4,320,128]{2,1,0:T(8,128)(2,1)}, bf16[4,320,128]{2,1,0:T(8,128)(2,1)}, bf16[4,320,128]{2,1,0:T(8,128...) custom-call(s32[1]{0:T(128)} %bitcast.place, ...), custom_call_target="tpu_custom_call" | custom-call | flops 10000000 | bytes 10485760 | tf_op jit(solution)/shard_map/pallas_call | solution.py:420
  10.1 1.3 %collective-permute-start = (bf16[5,32,128]{2,1,0:T(8,128)(2,1)}, bf16[5,32,128]{2,1,0:T(8,128)(2,1)S(1)}, u32[]{:S(2)}, u32[]{:S(2)}) collective-permute-start(bf16[5,32,128]{2,1,0:T(8,128)(2,1)} %get-tuple-element.28.rest_0_), channel_id=1, source_target_pairs={{17,16},{18,17},{19,18},{21,20},{22,21},{23,22},{25,24},{26,25},{2... | collective-permute-start | bytes 122888 | tf_op jit(solution)/shard_map/ppermute | solution.py:467
  11.4 4.0 %collective-permute-start.1 = (bf16[5,32,128]{2,1,0:T(8,128)(2,1)}, bf16[5,32,128]{2,1,0:T(8,128)(2,1)S(1)}, u32[]{:S(2)}, u32[]{:S(2)}) collective-permute-start(bf16[5,32,128]{2,1,0:T(8,128)(2,1)} %get-tuple-element.28.rest_0_), channel_id=1, source_target_pairs={{16,17},{17,18},{18,19},{20,21},{21,22},{22,23},{24,25},{25,26},{2... | collective-permute-start | bytes 122888 | tf_op jit(solution)/shard_map/ppermute | solution.py:468
  15.4 1.6 %collective-permute-start.2 = (bf16[4,320,128]{2,1,0:T(8,128)(2,1)}, bf16[4,320,128]{2,1,0:T(8,128)(2,1)S(1)}, u32[]{:S(2)}, u32[]{:S(2)}) collective-permute-start(bf16[4,320,128]{2,1,0:T(8,128)(2,1)} %get-tuple-element.29), channel_id=1, source_target_pairs={{0,4},{4,0},{8,12},{12,8},{1,5},{5,1},{9,13},{13,9},{2,6},{6,2},{1... | collective-permute-start | bytes 983048 | tf_op jit(solution)/shard_map/ppermute | solution.py:460
  17.0 1.4 %collective-permute-start.6 = (bf16[4,320,128]{2,1,0:T(8,128)(2,1)}, bf16[4,320,128]{2,1,0:T(8,128)(2,1)}, u32[]{:S(2)}, u32[]{:S(2)}) collective-permute-start(bf16[4,320,128]{2,1,0:T(8,128)(2,1)} %get-tuple-element.34), channel_id=1, source_target_pairs={{0,8},{4,12},{8,0},{12,4},{1,9},{5,13},{9,1},{13,5},{2,10},{6,14},... | collective-permute-start | bytes 983048 | tf_op jit(solution)/shard_map/ppermute | solution.py:460
  18.4 7.2 %shard_map.88 = (f32[320,128]{1,0:T(8,128)}, f32[320,128]{1,0:T(8,128)}) custom-call(s32[1]{0:T(128)} %bitcast.place, s32[1,320]{1,0:T(1,128)} %bitcast.11, f32[320,128]{1,0:T(8,128)} %copy-done.13, f32[320,128]{1,0:T(8,128)} %bitcast.16, s32[320,128]{1,0:T(8,128)} %bitcast.18, bf16[5,32,128]{2,1,0:T(8,128)(2,1)} %get-tuple-element.28.rest_0_), custom_call_target="tpu_custom_call" | custom-call | flops 10000000000 | bytes 491520 | tf_op jit(solution)/shard_map/pallas_call | solution.py:420
  25.7 0.8 collective-permute-start.11
  26.8 1.3 %collective-permute-start.13 = (bf16[4,320,128]{2,1,0:T(8,128)(2,1)}, bf16[4,320,128]{2,1,0:T(8,128)(2,1)}, u32[]{:S(2)}, u32[]{:S(2)}) collective-permute-start(bf16[4,320,128]{2,1,0:T(8,128)(2,1)} %get-tuple-element.46), channel_id=1, source_target_pairs={{0,12},{4,8},{8,4},{12,0},{1,13},{5,9},{9,5},{13,1},{2,14},{6,10},... | collective-permute-start | bytes 983048 | tf_op jit(solution)/shard_map/ppermute | solution.py:460
  28.2 0.7 copy-done.3
  28.9 9.9 %shard_map.87 = (f32[10240,128]{1,0:T(8,128)}, bf16[5,32,128]{2,1,0:T(8,128)(2,1)}, bf16[2,32,128]{2,1,0:T(8,128)(2,1)}) custom-call(s32[1]{0:T(128)} %bitcast.place, s32[1,320]{1,0:T(1,128)} %bitcast.12, f32[10240,128]{1,0:T(8,128)} %get-tuple-element.27.field.above.below, f32[10240,128]{1,0:T(8,128)} %get-tuple-element.27.field.above.below, ...), custom_call_target="tpu_custom_call" | custom-call | flops 10000000 | bytes 10485760 | tf_op jit(solution)/shard_map/pallas_call | solution.py:420
  38.8 3.3 %shard_map.89 = (bf16[4,320,128]{2,1,0:T(8,128)(2,1)}, bf16[4,320,128]{2,1,0:T(8,128)(2,1)}, bf16[4,320,128]{2,1,0:T(8,128)(2,1)}, bf16[4,320,128]{2,1,0:T(8,128)(2,1)}) custom-call(s32[1]{0:T(128)} %bitcast.place, bf16[8,1280,1280]{2,1,0:T(8,128)(2,1)} %legendre.3, bf16[4,320,128]{2,1,0:T(8,128)(2,1)} %get-tuple-element.33.rest_0_, ...), custom_call_target="tpu_custom_call" | custom-call | flops 3355443200 | bytes 13107200 | tf_op jit(solution)/shard_map/pallas_call | solution.py:420
  42.2 1.3 %collective-permute-start.4 = (bf16[5,32,128]{2,1,0:T(8,128)(2,1)S(1)}, bf16[5,32,128]{2,1,0:T(8,128)(2,1)S(1)}, u32[]{:S(2)}, u32[]{:S(2)}) collective-permute-start(bf16[5,32,128]{2,1,0:T(8,128)(2,1)S(1)} %copy-done.14), channel_id=1, source_target_pairs={{17,16},{18,17},{19,18},{21,20},{22,21},{23,22},{25,24},{26,25},{2... | collective-permute-start | bytes 122888 | tf_op jit(solution)/shard_map/ppermute | solution.py:467
  43.5 4.0 %collective-permute-start.5 = (bf16[5,32,128]{2,1,0:T(8,128)(2,1)S(1)}, bf16[5,32,128]{2,1,0:T(8,128)(2,1)S(1)}, u32[]{:S(2)}, u32[]{:S(2)}) collective-permute-start(bf16[5,32,128]{2,1,0:T(8,128)(2,1)S(1)} %copy-done.14), channel_id=1, source_target_pairs={{16,17},{17,18},{18,19},{20,21},{21,22},{22,23},{24,25},{25,26},{2... | collective-permute-start | bytes 122888 | tf_op jit(solution)/shard_map/ppermute | solution.py:468
  48.0 2.8 %shard_map.92 = (bf16[4,320,128]{2,1,0:T(8,128)(2,1)}, bf16[4,320,128]{2,1,0:T(8,128)(2,1)}, bf16[4,320,128]{2,1,0:T(8,128)(2,1)}, bf16[4,320,128]{2,1,0:T(8,128)(2,1)}) custom-call(s32[1]{0:T(128)} %bitcast.place, bf16[8,1280,1280]{2,1,0:T(8,128)(2,1)} %legendre.3, bf16[4,320,128]{2,1,0:T(8,128)(2,1)} %get-tuple-element.43.rest_0_, ...), custom_call_target="tpu_custom_call" | custom-call | flops 3355443200 | bytes 13107200 | tf_op jit(solution)/shard_map/pallas_call | solution.py:420
  50.8 0.6 collective-permute-start.14
  51.7 1.3 %collective-permute-start.16 = (bf16[4,320,128]{2,1,0:T(8,128)(2,1)}, bf16[4,320,128]{2,1,0:T(8,128)(2,1)S(1)}, u32[]{:S(2)}, u32[]{:S(2)}) collective-permute-start(bf16[4,320,128]{2,1,0:T(8,128)(2,1)} %get-tuple-element.50), channel_id=1, source_target_pairs={{0,12},{4,8},{8,4},{12,0},{1,13},{5,9},{9,5},{13,1},{2,14},{6,10},... | collective-permute-start | bytes 983048 | tf_op jit(solution)/shard_map/ppermute | solution.py:460
  53.1 0.4 collective-permute-start.9
  53.5 1.1 %collective-permute-start.10 = (bf16[4,320,128]{2,1,0:T(8,128)(2,1)}, bf16[4,320,128]{2,1,0:T(8,128)(2,1)S(1)}, u32[]{:S(2)}, u32[]{:S(2)}) collective-permute-start(bf16[4,320,128]{2,1,0:T(8,128)(2,1)} %get-tuple-element.42), channel_id=1, source_target_pairs={{0,8},{4,12},{8,0},{12,4},{1,9},{5,13},{9,1},{13,5},{2,10},{6,14},... | collective-permute-start | bytes 983048 | tf_op jit(solution)/shard_map/ppermute | solution.py:460
  54.6 7.2 %shard_map.90 = (f32[320,128]{1,0:T(8,128)}, f32[320,128]{1,0:T(8,128)}) custom-call(s32[1]{0:T(128)} %bitcast.place, s32[1,320]{1,0:T(1,128)} %bitcast.13, f32[320,128]{1,0:T(8,128)} %copy-done.13, f32[320,128]{1,0:T(8,128)} %bitcast.17, s32[320,128]{1,0:T(8,128)} %bitcast.19, ...), custom_call_target="tpu_custom_call", output_to_operand_aliasing={{0}: (5, {}), {1}: (6, {})} | custom-call | flops 10000000000 | bytes 491520 | tf_op jit(solution)/shard_map/pallas_call | solution.py:420
  61.8 13.8 %collective-permute-done.9.rest_1_.rest_3_ = bf16[4,320,128]{2,1,0:T(8,128)(2,1)S(1)} collective-permute-done((bf16[4,320,128]{2,1,0:T(8,128)(2,1)}, bf16[4,320,128]{2,1,0:T(8,128)(2,1)S(1)}, u32[]{:S(2)}, u32[]{:S(2)}) %collective-permute-start.9) | collective-permute-done | bytes 327712 | tf_op jit(solution)/shard_map/ppermute | solution.py:460
  75.6 0.7 copy-done.1
  76.3 8.4 %shard_map.91.sea = f32[10240,128]{1,0:T(8,128)} custom-call(s32[1]{0:T(128)} %bitcast.place, s32[1,320]{1,0:T(1,128)} %bitcast.14, f32[10240,128]{1,0:T(8,128)} %get-tuple-element.31.rest_2_.field.above.below, f32[10240,128]{1,0:T(8,128)} %get-tuple-element.31.rest_2_.field.above.below, f32[10240,128]{1,0:T(8,128)} %get-tuple-element.31.rest_2_.field.above.below, ...), custom_call_target="tpu_custom_call" | custom-call | flops 10000000 | bytes 10485760 | tf_op jit(solution)/shard_map/pallas_call | solution.py:420
  84.8 0.7 copy-done.4
  85.8 6.6 %shard_map.93 = f32[10240,128]{1,0:T(8,128)} custom-call(s32[1]{0:T(128)} %bitcast.place, f32[10240,128]{1,0:T(8,128)} %shard_map.91.sea, bf16[4,320,128]{2,1,0:T(8,128)(2,1)} %get-tuple-element.41.rest_0_, bf16[4,320,128]{2,1,0:T(8,128)(2,1)} %copy-done, bf16[4,320,128]{2,1,0:T(8,128)(2,1)} %copy-done.7, bf16[4,320,128]{2,1,0:T(8,128)(2,1)} %copy-done.1, ...), custom_call_target="tpu_custom_call" | custom-call | flops 10000000 | bytes 10485760 | tf_op jit(solution)/shard_map/pallas_call | solution.py:420
  (48 shorter events, 2.1 us)
Async XLA Ops:
  0.6 16.4 %collective-permute-start.7 = (f32[320,128]{1,0:T(8,128)}, f32[320,128]{1,0:T(8,128)S(1)}, u32[]{:S(2)}, u32[]{:S(2)}) collective-permute-start(f32[320,128]{1,0:T(8,128)} %bitcast.15), channel_id=1, source_target_pairs={{0,16},{16,0},{1,17},{17,1},{2,18},{18,2},{3,19},{19,3},{4,20},{20... | collective-permute-start | bytes 491528 | tf_op jit(solution)/shard_map/ppermute | solution.py:414
  10.1 15.5 %collective-permute-start = (bf16[5,32,128]{2,1,0:T(8,128)(2,1)}, bf16[5,32,128]{2,1,0:T(8,128)(2,1)S(1)}, u32[]{:S(2)}, u32[]{:S(2)}) collective-permute-start(bf16[5,32,128]{2,1,0:T(8,128)(2,1)} %get-tuple-element.28.rest_0_), channel_id=1, source_target_pairs={{17,16},{18,17},{19,18},{21,20},{22,21},{23,22},{25,24},{26,25},{2... | collective-permute-start | bytes 122888 | tf_op jit(solution)/shard_map/ppermute | solution.py:467
  11.4 15.0 %collective-permute-start.1 = (bf16[5,32,128]{2,1,0:T(8,128)(2,1)}, bf16[5,32,128]{2,1,0:T(8,128)(2,1)S(1)}, u32[]{:S(2)}, u32[]{:S(2)}) collective-permute-start(bf16[5,32,128]{2,1,0:T(8,128)(2,1)} %get-tuple-element.28.rest_0_), channel_id=1, source_target_pairs={{16,17},{17,18},{18,19},{20,21},{21,22},{22,23},{24,25},{25,26},{2... | collective-permute-start | bytes 122888 | tf_op jit(solution)/shard_map/ppermute | solution.py:468
  15.4 11.4 %collective-permute-start.2 = (bf16[4,320,128]{2,1,0:T(8,128)(2,1)}, bf16[4,320,128]{2,1,0:T(8,128)(2,1)S(1)}, u32[]{:S(2)}, u32[]{:S(2)}) collective-permute-start(bf16[4,320,128]{2,1,0:T(8,128)(2,1)} %get-tuple-element.29), channel_id=1, source_target_pairs={{0,4},{4,0},{8,12},{12,8},{1,5},{5,1},{9,13},{13,9},{2,6},{6,2},{1... | collective-permute-start | bytes 983048 | tf_op jit(solution)/shard_map/ppermute | solution.py:460
  17.0 11.2 %collective-permute-start.3 = (bf16[4,320,128]{2,1,0:T(8,128)(2,1)}, bf16[4,320,128]{2,1,0:T(8,128)(2,1)S(1)}, u32[]{:S(2)}, u32[]{:S(2)}) collective-permute-start(bf16[4,320,128]{2,1,0:T(8,128)(2,1)} %get-tuple-element.30), channel_id=1, source_target_pairs={{0,12},{4,8},{8,4},{12,0},{1,13},{5,9},{9,5},{13,1},{2,14},{6,10},... | collective-permute-start | bytes 983048 | tf_op jit(solution)/shard_map/ppermute | solution.py:460
  17.0 21.8 %collective-permute-start.6 = (bf16[4,320,128]{2,1,0:T(8,128)(2,1)}, bf16[4,320,128]{2,1,0:T(8,128)(2,1)}, u32[]{:S(2)}, u32[]{:S(2)}) collective-permute-start(bf16[4,320,128]{2,1,0:T(8,128)(2,1)} %get-tuple-element.34), channel_id=1, source_target_pairs={{0,8},{4,12},{8,0},{12,4},{1,9},{5,13},{9,1},{13,5},{2,10},{6,14},... | collective-permute-start | bytes 983048 | tf_op jit(solution)/shard_map/ppermute | solution.py:460
  25.6 2.5 %copy-start.11 = (bf16[5,32,128]{2,1,0:T(8,128)(2,1)}, bf16[5,32,128]{2,1,0:T(8,128)(2,1)S(1)}, u32[]{:S(2)}) copy-start(bf16[5,32,128]{2,1,0:T(8,128)(2,1)S(1)} %collective-permute-done.east_in) | copy-start | bytes 122884
  25.7 17.9 %collective-permute-start.11 = (bf16[4,320,128]{2,1,0:T(8,128)(2,1)}, bf16[4,320,128]{2,1,0:T(8,128)(2,1)S(1)}, u32[]{:S(2)}, u32[]{:S(2)}) collective-permute-start(bf16[4,320,128]{2,1,0:T(8,128)(2,1)} %get-tuple-element.44), channel_id=1, source_target_pairs={{0,4},{4,0},{8,12},{12,8},{1,5},{5,1},{9,13},{13,9},{2,6},{6,2},{1... | collective-permute-start | bytes 983048 | tf_op jit(solution)/shard_map/ppermute | solution.py:460
  26.4 1.7 %copy-start.12 = (bf16[5,32,128]{2,1,0:T(8,128)(2,1)}, bf16[5,32,128]{2,1,0:T(8,128)(2,1)S(1)}, u32[]{:S(2)}) copy-start(bf16[5,32,128]{2,1,0:T(8,128)(2,1)S(1)} %collective-permute-done.1.west_in) | copy-start | bytes 122884
  26.4 21.1 %collective-permute-start.12 = (bf16[4,320,128]{2,1,0:T(8,128)(2,1)}, bf16[4,320,128]{2,1,0:T(8,128)(2,1)}, u32[]{:S(2)}, u32[]{:S(2)}) collective-permute-start(bf16[4,320,128]{2,1,0:T(8,128)(2,1)} %get-tuple-element.45), channel_id=1, source_target_pairs={{0,8},{4,12},{8,0},{12,4},{1,9},{5,13},{9,1},{13,5},{2,10},{6,14},... | collective-permute-start | bytes 983048 | tf_op jit(solution)/shard_map/ppermute | solution.py:460
  26.8 21.1 %collective-permute-start.13 = (bf16[4,320,128]{2,1,0:T(8,128)(2,1)}, bf16[4,320,128]{2,1,0:T(8,128)(2,1)}, u32[]{:S(2)}, u32[]{:S(2)}) collective-permute-start(bf16[4,320,128]{2,1,0:T(8,128)(2,1)} %get-tuple-element.46), channel_id=1, source_target_pairs={{0,12},{4,8},{8,4},{12,0},{1,13},{5,9},{9,5},{13,1},{2,14},{6,10},... | collective-permute-start | bytes 983048 | tf_op jit(solution)/shard_map/ppermute | solution.py:460
  38.8 3.4 %copy-start.14 = (bf16[5,32,128]{2,1,0:T(8,128)(2,1)S(1)}, bf16[5,32,128]{2,1,0:T(8,128)(2,1)}, u32[]{:S(2)}) copy-start(bf16[5,32,128]{2,1,0:T(8,128)(2,1)} %get-tuple-element.32) | copy-start | bytes 122884
  42.1 11.4 %collective-permute-start.8 = (bf16[4,320,128]{2,1,0:T(8,128)(2,1)}, bf16[4,320,128]{2,1,0:T(8,128)(2,1)S(1)}, u32[]{:S(2)}, u32[]{:S(2)}) collective-permute-start(bf16[4,320,128]{2,1,0:T(8,128)(2,1)} %get-tuple-element.37), channel_id=1, source_target_pairs={{0,4},{4,0},{8,12},{12,8},{1,5},{5,1},{9,13},{13,9},{2,6},{6,2},{1... | collective-permute-start | bytes 983048 | tf_op jit(solution)/shard_map/ppermute | solution.py:460
  42.2 9.5 %collective-permute-start.4 = (bf16[5,32,128]{2,1,0:T(8,128)(2,1)S(1)}, bf16[5,32,128]{2,1,0:T(8,128)(2,1)S(1)}, u32[]{:S(2)}, u32[]{:S(2)}) collective-permute-start(bf16[5,32,128]{2,1,0:T(8,128)(2,1)S(1)} %copy-done.14), channel_id=1, source_target_pairs={{17,16},{18,17},{19,18},{21,20},{22,21},{23,22},{25,24},{26,25},{2... | collective-permute-start | bytes 122888 | tf_op jit(solution)/shard_map/ppermute | solution.py:467
  43.5 4.4 %copy-start.8 = (bf16[4,320,128]{2,1,0:T(8,128)(2,1)}, bf16[4,320,128]{2,1,0:T(8,128)(2,1)S(1)}, u32[]{:S(2)}) copy-start(bf16[4,320,128]{2,1,0:T(8,128)(2,1)S(1)} %collective-permute-done.11.rest_1_) | copy-start | bytes 983044
  43.5 9.5 %collective-permute-start.5 = (bf16[5,32,128]{2,1,0:T(8,128)(2,1)S(1)}, bf16[5,32,128]{2,1,0:T(8,128)(2,1)S(1)}, u32[]{:S(2)}, u32[]{:S(2)}) collective-permute-start(bf16[5,32,128]{2,1,0:T(8,128)(2,1)S(1)} %copy-done.14), channel_id=1, source_target_pairs={{16,17},{17,18},{18,19},{20,21},{21,22},{22,23},{24,25},{25,26},{2... | collective-permute-start | bytes 122888 | tf_op jit(solution)/shard_map/ppermute | solution.py:468
  50.8 34.0 %collective-permute-start.14 = (bf16[4,320,128]{2,1,0:T(8,128)(2,1)}, bf16[4,320,128]{2,1,0:T(8,128)(2,1)S(1)}, u32[]{:S(2)}, u32[]{:S(2)}) collective-permute-start(bf16[4,320,128]{2,1,0:T(8,128)(2,1)} %get-tuple-element.48), channel_id=1, source_target_pairs={{0,4},{4,0},{8,12},{12,8},{1,5},{5,1},{9,13},{13,9},{2,6},{6,2},{1... | collective-permute-start | bytes 983048 | tf_op jit(solution)/shard_map/ppermute | solution.py:460
  51.3 33.4 %collective-permute-start.15 = (bf16[4,320,128]{2,1,0:T(8,128)(2,1)}, bf16[4,320,128]{2,1,0:T(8,128)(2,1)S(1)}, u32[]{:S(2)}, u32[]{:S(2)}) collective-permute-start(bf16[4,320,128]{2,1,0:T(8,128)(2,1)} %get-tuple-element.49), channel_id=1, source_target_pairs={{0,8},{4,12},{8,0},{12,4},{1,9},{5,13},{9,1},{13,5},{2,10},{6,14},... | collective-permute-start | bytes 983048 | tf_op jit(solution)/shard_map/ppermute | solution.py:460
  51.7 10.1 %copy-start.9 = (bf16[5,32,128]{2,1,0:T(8,128)(2,1)}, bf16[5,32,128]{2,1,0:T(8,128)(2,1)S(1)}, u32[]{:S(2)}) copy-start(bf16[5,32,128]{2,1,0:T(8,128)(2,1)S(1)} %collective-permute-done.4.east_in) | copy-start | bytes 122884
  51.7 33.0 %collective-permute-start.16 = (bf16[4,320,128]{2,1,0:T(8,128)(2,1)}, bf16[4,320,128]{2,1,0:T(8,128)(2,1)S(1)}, u32[]{:S(2)}, u32[]{:S(2)}) collective-permute-start(bf16[4,320,128]{2,1,0:T(8,128)(2,1)} %get-tuple-element.50), channel_id=1, source_target_pairs={{0,12},{4,8},{8,4},{12,0},{1,13},{5,9},{9,5},{13,1},{2,14},{6,10},... | collective-permute-start | bytes 983048 | tf_op jit(solution)/shard_map/ppermute | solution.py:460
  53.1 8.7 %copy-start.10 = (bf16[5,32,128]{2,1,0:T(8,128)(2,1)}, bf16[5,32,128]{2,1,0:T(8,128)(2,1)S(1)}, u32[]{:S(2)}) copy-start(bf16[5,32,128]{2,1,0:T(8,128)(2,1)S(1)} %collective-permute-done.5.west_in) | copy-start | bytes 122884
  53.1 22.5 %collective-permute-start.9 = (bf16[4,320,128]{2,1,0:T(8,128)(2,1)}, bf16[4,320,128]{2,1,0:T(8,128)(2,1)S(1)}, u32[]{:S(2)}, u32[]{:S(2)}) collective-permute-start(bf16[4,320,128]{2,1,0:T(8,128)(2,1)} %get-tuple-element.38), channel_id=1, source_target_pairs={{0,12},{4,8},{8,4},{12,0},{1,13},{5,9},{9,5},{13,1},{2,14},{6,10},... | collective-permute-start | bytes 983048 | tf_op jit(solution)/shard_map/ppermute | solution.py:460
  53.5 8.3 %copy-start = (bf16[4,320,128]{2,1,0:T(8,128)(2,1)}, bf16[4,320,128]{2,1,0:T(8,128)(2,1)S(1)}, u32[]{:S(2)}) copy-start(bf16[4,320,128]{2,1,0:T(8,128)(2,1)S(1)} %collective-permute-done.8.rest_0_.rest_1_) | copy-start | bytes 983044
  53.5 31.3 %collective-permute-start.10 = (bf16[4,320,128]{2,1,0:T(8,128)(2,1)}, bf16[4,320,128]{2,1,0:T(8,128)(2,1)S(1)}, u32[]{:S(2)}, u32[]{:S(2)}) collective-permute-start(bf16[4,320,128]{2,1,0:T(8,128)(2,1)} %get-tuple-element.42), channel_id=1, source_target_pairs={{0,8},{4,12},{8,0},{12,4},{1,9},{5,13},{9,1},{13,5},{2,10},{6,14},... | collective-permute-start | bytes 983048 | tf_op jit(solution)/shard_map/ppermute | solution.py:460
  (8 other events, 7.8 us)

commit v6 on v5

v6 whole, which is shorter than its diff:
```python
import functools

import jax
import jax.numpy as jnp
from jax import lax
from jax.experimental import pallas as pl
from jax.experimental.pallas import tpu as pltpu
from jax.sharding import PartitionSpec as P


diffusion_rate = 0.2
lanes = 128


def chunk_widths(wave_dev):
    return (wave_dev - wave_dev // 2, wave_dev // 2) if wave_dev > 1 else (wave_dev,)


def chunk_of(local, widths):
    chunk = 0
    while local >= widths[chunk]:
        local -= widths[chunk]
        chunk += 1
    return chunk, local


def row_block(rows):
    return 160 if rows % 160 == 0 else rows


def cost(flops, bytes_accessed):
    return pl.CostEstimate(flops=flops, bytes_accessed=bytes_accessed, transcendentals=0)


def where_am_i(place, n_row, n_col):
    flat = place[0]
    return (
        lax.div(flat, n_row * n_col),
        lax.rem(lax.div(flat, n_col), n_row),
        lax.rem(flat, n_col),
    )


def iota(shape, dim):
    return lax.broadcasted_iota(jnp.int32, shape, dim)


def as_bf16(mask):
    return jnp.where(mask, 1.0, 0.0).astype(jnp.bfloat16)


def swap_matrix(flip_high, flip_low):
    row, column = iota((256, 256), 0), iota((256, 256), 1)
    return as_bf16(column == (((row & 15) ^ flip_low) << 4 | ((row >> 4) ^ flip_high)))


def spread_matrix():
    row, column = iota((lanes, lanes), 0), iota((lanes, lanes), 1)
    odd = column & 1
    return as_bf16(((row == lanes - 1) & (odd == 0)) | ((row == 0) & (odd == 1)))


def beside_matrix():
    row, column = iota((lanes, lanes), 0), iota((lanes, lanes), 1)
    return as_bf16((row == column + 1) | (row + 1 == column))


def side_matrix():
    row, column = iota((lanes, lanes), 0), iota((lanes, lanes), 1)
    odd = row & 1
    return as_bf16(((column == 0) & (odd == 1)) | ((column == lanes - 1) & (odd == 0)))


def split(value):
    high = value.astype(jnp.bfloat16)
    return high, (value - high.astype(jnp.float32)).astype(jnp.bfloat16)


def product(a, b):
    return jnp.dot(a, b, preferred_element_type=jnp.float32)


def entry_kernel(place, counts, field, gauss, mix, *rest, n_row, n_col, widths, block):
    chunks = len(widths)
    send = [rest[n_row * c:n_row * (c + 1)] for c in range(chunks)]
    mixed, edge, table, packed, ends = rest[n_row * chunks:]
    comp, row, _ = where_am_i(place, n_row, n_col)
    levels = mix.shape[0]
    wave_dev = levels // n_row
    tall = block * levels
    steps = field.shape[0] // tall
    state_block = pl.BlockSpec((tall, lanes), lambda i: (i, 0))

    flip = row * wave_dev

    def weigh(field, *parts):
        step = pl.program_id(0)

        def target(wave):
            part, local = divmod(wave, wave_dev)
            chunk, slot = chunk_of(local, widths)
            return parts[n_row * chunk + part], slot

        for lat in range(0, block - 15, 16):
            halves = []
            for half in range(0, levels, 16):
                halves.append(jnp.concatenate([
                    (field[pl.ds(pl.multiple_of((lat + s) * levels + (half ^ (flip & ~15)), 16), 16), :]
                     * gauss[step * block + lat + s]).astype(jnp.bfloat16)
                    for s in range(16)
                ], axis=0))
            turned = product(table[...], jnp.concatenate(halves, axis=1)).astype(jnp.bfloat16)
            for wave in range(levels):
                out, slot = target(wave)
                part = lanes * (wave // 16)
                out[slot, lat:lat + 16, :] = turned[16 * (wave % 16):16 * (wave % 16) + 16, part:part + lanes]
        for lat in range(block - block % 16, block, 8):
            weight = jnp.zeros((8, lanes), jnp.float32)
            for s in range(8):
                weight = jnp.where(iota((8, lanes), 0) == s, gauss[step * block + lat + s], weight)
            for wave in range(levels):
                out, slot = target(wave)
                values = field[pl.ds(lat * levels + (wave ^ flip), 8, stride=levels), :] * weight
                out[slot, lat:lat + 8, :] = values.astype(jnp.bfloat16)

    @pl.when(comp == 0)
    def _():
        table[...] = swap_matrix(flip & 15, 0)
        pltpu.emit_pipeline(
            weigh, grid=(steps,), in_specs=[state_block],
            out_specs=[pl.BlockSpec((w, block, lanes), lambda i: (0, i, 0)) for w in widths for _ in range(n_row)],
        )(field, *sum(send, ()))

    def mixed_rows(ref, start, first_row):
        values = []
        for quarter in range(2):
            parts = []
            for pair in range(2):
                part = ref[pl.ds(start + (2 * quarter + pair) * 2 * levels, 2 * levels), :]
                values.append(part)
                parts.append(split(part))
            high = jnp.concatenate([p[0] for p in parts], axis=1)
            low = jnp.concatenate([p[1] for p in parts], axis=1)
            blend = product(table[0:2 * levels, :], jnp.concatenate([high, low, high, low], axis=0))
            values += [blend[:, :lanes], blend[:, lanes:]]
        out = []
        for s in range(8):
            quarter, pair, place_in = s // 4, s // 2 % 2, slice(levels * (s % 2), levels * (s % 2) + levels)
            heat = values[4 * quarter + pair][place_in]
            blend = values[4 * quarter + 2 + pair][place_in]
            sea = iota((levels, lanes), 1) < counts[0, first_row + s]
            value = heat + jnp.where(sea, blend, 0.0)
            out.append((value, jnp.where(sea, value, 0.0).astype(jnp.bfloat16)))
        return out

    @pl.when(comp != 0)
    def _():
        high, low = split(mix[...])
        repeat = as_bf16((iota((levels, 256), 1) & (levels - 1)) == iota((levels, 256), 0))
        wide = jnp.where(iota((levels, 256), 1) < 4 * levels, product(high, repeat), product(low, repeat))
        wide = jnp.concatenate([wide, wide], axis=0)
        shape = (2 * levels, 256)
        own = (iota(shape, 1) // levels & 1) == iota(shape, 0) // levels
        table[0:2 * levels, :] = jnp.where(own, wide, 0.0).astype(jnp.bfloat16)
        packed[...] = jnp.zeros_like(packed)
        batch = 32 if block % 32 == 0 else 8

        def blend(field, mixed):
            step = pl.program_id(0)
            spread = spread_matrix()

            def body(g, carry):
                base = step * block + g * batch
                rows = []
                for first in range(0, batch, 8):
                    start = pl.multiple_of((g * batch + first) * levels, 8 * levels)
                    some = mixed_rows(field, start, base + first)
                    for s, (value, _) in enumerate(some):
                        mixed[pl.ds(pl.multiple_of(start + s * levels, levels), levels), :] = value
                    rows += some
                pack(packed, base, [r[1] for r in rows], spread)
                return carry

            lax.fori_loop(0, block // batch, body, 0)

            @pl.when(step == 0)
            def _():
                ends[0] = mixed_rows(field, 0, 0)[0][1]

            @pl.when(step == steps - 1)
            def _():
                ends[1] = mixed_rows(field, tall - 8 * levels, steps * block - 8)[-1][1]

        pltpu.emit_pipeline(blend, grid=(steps,), in_specs=[state_block], out_specs=[state_block])(field, mixed)
        edge[...] = packed[...].astype(jnp.bfloat16)
        hand_on(ends, send[0], row)


def hand_on(ends, parts, row):
    levels = ends.shape[1]
    for k in range(1, len(parts)):
        pltpu.sync_copy(ends.at[((k ^ row) > row).astype(jnp.int32)], parts[k].at[0, pl.ds(0, levels)])


def pack(packed, base, rows, spread):
    levels = packed.shape[1]
    ends = product(jnp.concatenate(rows, axis=0), spread)
    pair_of = iota((levels, lanes), 1) >> 1
    slot = base >> 6
    kept = packed[slot]
    for s in range(len(rows)):
        kept = jnp.where(pair_of == (base & 63) + s, ends[s * levels:(s + 1) * levels], kept)
    packed[slot] = kept


def sweep_kernel(place, counts, field, east_in, west_in, *rest, block, n_row, n_col, near_parts, final):
    halos, rest = rest[:len(near_parts)], rest[len(near_parts):]
    if final:
        gap, out, masked, sides = rest
    else:
        out, edge, ends, masked, sides, packed = rest
    comp, row, col = where_am_i(place, n_row, n_col)
    levels = sides.shape[1]
    tall = block * levels
    rows = field.shape[0] // levels
    steps = rows // block
    shape = (levels, lanes)
    batch = 32 if block % 32 == 0 else 8

    @pl.when(comp != 0)
    def _():
        lane = iota(shape, 1)
        pair_of = lane >> 1

        def sea_of(y):
            return lane < counts[0, jnp.clip(y, 0, rows - 1)]

        def at(y):
            return pl.ds(pl.multiple_of(y * levels, levels), levels)

        def halo(neighbour):
            found = jnp.zeros(shape, jnp.float32)
            inside = (neighbour >= 0) & (neighbour < n_row)
            for part, ref in zip(near_parts, halos):
                found = jnp.where(inside & ((neighbour ^ row) == part), ref[0].astype(jnp.float32), found)
            return found

        for slot in range(sides.shape[0]):
            west = jnp.where(col > 0, west_in[slot].astype(jnp.float32), 0.0)
            east = jnp.where(col < n_col - 1, east_in[slot].astype(jnp.float32), 0.0)
            sides[slot] = jnp.where((lane & 1) == 0, pltpu.roll(east, lanes - 1, 1), pltpu.roll(west, 1, 1))
        if not final:
            packed[...] = jnp.zeros_like(packed)

        def advance(field, above, below, out):
            step = pl.program_id(0)
            base = step * block
            masked[0:levels, :] = jnp.where(step > 0, jnp.where(sea_of(base - 1), above[...], 0.0), halo(row - 1))
            masked[(block + 1) * levels:(block + 2) * levels, :] = jnp.where(
                step < steps - 1, jnp.where(sea_of(base + block), below[...], 0.0), halo(row + 1))

            def fill(g, carry):
                for s in range(8):
                    y = g * 8 + s
                    masked[at(y + 1), :] = jnp.where(sea_of(base + y), field[at(y), :], 0.0)
                return carry

            lax.fori_loop(0, block // 8, fill, 0)
            weights = jnp.concatenate([beside_matrix(), side_matrix()], axis=0)
            spread = spread_matrix()

            def body(g, carry):
                first = base + g * batch
                here = masked[pl.ds(pl.multiple_of((g * batch + 1) * levels, levels), batch * levels), :]
                beyond = sides[first >> 6]
                turned = jnp.concatenate(
                    [jnp.where(pair_of == (first & 63) + s, beyond, 0.0).astype(jnp.bfloat16) for s in range(batch)],
                    axis=0)
                near = product(jnp.concatenate([here.astype(jnp.bfloat16), turned], axis=1), weights)
                new_rows = []
                for s in range(batch):
                    y = g * batch + s
                    part = slice(s * levels, (s + 1) * levels)
                    lap = masked[at(y), :] + masked[at(y + 2), :] + near[part] - 4.0 * masked[at(y + 1), :]
                    sea = sea_of(base + y)
                    new = field[at(y), :] + jnp.where(sea, diffusion_rate * lap, 0.0)
                    out[at(y), :] = new
                    if final:
                        out[pl.ds(y * levels, 1), :] = new[0:1, :] + 0.3 * gap[pl.ds(base + y, 1), :]
                    else:
                        new_rows.append(jnp.where(sea, new, 0.0).astype(jnp.bfloat16))
                if not final:
                    pack(packed, first, new_rows, spread)
                return carry

            lax.fori_loop(0, block // batch, body, 0)
            if not final:
                @pl.when(step == 0)
                def _():
                    ends[0] = jnp.where(sea_of(0), out[0:levels, :], 0.0).astype(jnp.bfloat16)

                @pl.when(step == steps - 1)
                def _():
                    ends[1] = jnp.where(
                        sea_of(rows - 1), out[(block - 1) * levels:block * levels, :], 0.0
                    ).astype(jnp.bfloat16)

        state_block = pl.BlockSpec((tall, lanes), lambda i: (i, 0))
        pltpu.emit_pipeline(
            advance, grid=(steps,),
            in_specs=[
                state_block,
                pl.BlockSpec((levels, lanes), lambda i: (jnp.maximum(i * block - 1, 0), 0)),
                pl.BlockSpec((levels, lanes), lambda i: (jnp.minimum((i + 1) * block, rows - 1), 0)),
            ],
            out_specs=[state_block],
        )(field, field, field, out)
        if not final:
            edge[...] = packed[...].astype(jnp.bfloat16)


def legendre_kernel(place, legendre, *rest, n_row, n_col, wave_dev, first_wave, with_ends):
    coeffs, rest = rest[:n_row], rest[n_row:]
    if with_ends:
        ends, rest = rest[0], rest[2:]
    out, gathered = rest[:n_row], rest[n_row]
    comp, row, _ = where_am_i(place, n_row, n_col)
    waves, lats = coeffs[0].shape[:2]
    count = legendre.shape[2]

    def one_wave(legendre, *parts):
        coeffs, out = parts[:n_row], parts[n_row:]
        table = legendre[0]
        for part in range(n_row):
            gathered[part ^ row] = coeffs[part][0]
        fourier = gathered[...].reshape(n_row * lats, lanes)
        spectral = lax.dot_general(fourier, table, (((0,), (0,)), ((), ())), preferred_element_type=jnp.float32)
        wave = row * wave_dev + first_wave + pl.program_id(0)
        total = (wave + iota((1, count), 1)).astype(jnp.float32)
        ratio = total * (total + 1.0) / (1279.0 * 1280.0)
        damping = 1.0 / (1.0 + 20.0 * ratio * ratio)
        filtered = (spectral * damping).astype(jnp.bfloat16)
        result = lax.dot_general(table, filtered, (((1,), (1,)), ((), ())), preferred_element_type=jnp.float32)
        gathered[...] = result.astype(jnp.bfloat16).reshape(n_row, lats, lanes)
        for part in range(n_row):
            out[part][0] = gathered[part ^ row]

    @pl.when(comp == 0)
    def _():
        pieces = [pl.BlockSpec((1, lats, lanes), lambda i: (i, 0, 0))] * n_row
        pltpu.emit_pipeline(
            one_wave, grid=(waves,),
            in_specs=[pl.BlockSpec((1,) + legendre.shape[1:], lambda i: (first_wave + i, 0, 0))] + pieces,
            out_specs=pieces,
        )(legendre, *coeffs, *out)

    if with_ends:
        @pl.when(comp != 0)
        def _():
            hand_on(ends, out, row)


def surface_kernel(place, counts, partner, own, source, *rest, first, group, n_row, n_col):
    new, gap = rest[-2:]
    half = partner.shape[0] // 2
    width = 2 * lanes
    table = jnp.concatenate(
        [partner[pl.ds(0, half, stride=2), :], partner[pl.ds(1, half, stride=2), :]], axis=1
    ).astype(jnp.bfloat16)
    low_index = iota((width, lanes), 0)
    high_index = iota((half, lanes), 0)
    one = jnp.ones((width, lanes), jnp.bfloat16)
    zero = jnp.zeros((width, lanes), jnp.bfloat16)
    sublane = iota((8, lanes), 0)
    rate = jnp.where(where_am_i(place, n_row, n_col)[0] == 0, 0.5, 0.25).astype(jnp.float32)

    def body(g, carry):
        start = pl.multiple_of(g * 8, 8)
        entries = source[pl.ds(start, 8), :]
        low = entries & (width - 1)
        high = entries >> 8
        found = []
        for p in range(0, 8, group):
            pick = jnp.concatenate(
                [jnp.where(low_index == low[s:s + 1, :], one, zero) for s in range(p, p + group)], axis=1
            )
            picked = product(table, pick)
            for s in range(group):
                part = picked[:, lanes * s:lanes * (s + 1)]
                match = high_index == high[p + s:p + s + 1, :]
                found.append(jnp.sum(jnp.where(match, part, 0.0), axis=0, keepdims=True))
        pulled = jnp.concatenate(found, axis=0)
        limit = jnp.zeros((8, lanes), jnp.int32)
        for s in range(8):
            limit = jnp.where(sublane == s, counts[0, first + start + s], limit)
        here = own[pl.ds(start, 8), :]
        difference = jnp.where(iota((8, lanes), 1) < limit, pulled - here, 0.0)
        new[pl.ds(start, 8), :] = here + rate * difference
        gap[pl.ds(start, 8), :] = difference
        return carry

    lax.fori_loop(0, source.shape[0] // 8, body, 0)


def exit_kernel(place, sea, *rest, n_row, n_col, widths, block):
    chunks = len(widths)
    back, (out, table) = rest[:n_row * chunks], rest[n_row * chunks:]
    comp, row, _ = where_am_i(place, n_row, n_col)
    levels = sum(widths) * n_row
    wave_dev = levels // n_row
    flip = row * wave_dev
    tall = block * levels

    def turn(*refs):
        parts, out = refs[:-1], refs[-1]

        def source(wave, lat, count):
            part, local = divmod(wave, wave_dev)
            chunk, slot = chunk_of(local, widths)
            return parts[n_row * chunk + part][slot, lat:lat + count, :]

        for lat in range(0, block - 15, 16):
            halves = [
                jnp.concatenate([source(half + wave, lat, 16) for wave in range(16)], axis=0)
                for half in range(0, levels, 16)
            ]
            turned = product(table[...], jnp.concatenate(halves, axis=1))
            for s in range(16):
                for half in range(0, levels, 16):
                    start = pl.multiple_of((lat + s) * levels + (half ^ (flip & ~15)), 16)
                    part = lanes * (half // 16)
                    out[pl.ds(start, 16), :] = turned[16 * s:16 * s + 16, part:part + lanes]
        for lat in range(block - block % 16, block, 8):
            for wave in range(levels):
                out[pl.ds(lat * levels + (wave ^ flip), 8, stride=levels), :] = source(wave, lat, 8).astype(jnp.float32)

    @pl.when(comp == 0)
    def _():
        table[...] = swap_matrix(0, flip & 15)
        pltpu.emit_pipeline(
            turn, grid=(out.shape[0] // tall,),
            in_specs=[pl.BlockSpec((w, block, lanes), lambda i: (0, i, 0)) for w in widths for _ in range(n_row)],
            out_specs=[pl.BlockSpec((tall, lanes), lambda i: (i, 0))],
        )(*back, out)


def shards(model_state, legendre, gauss_weight, mixing, surface, sea_count, remap_source):
    n_row, n_col = lax.axis_size("row"), lax.axis_size("col")
    rows, levels = model_state.shape[1], model_state.shape[2]
    wave_dev = levels // n_row
    widths = chunk_widths(wave_dev)
    chunks = len(widths)
    block = row_block(rows)
    f32, bf16 = jnp.float32, jnp.bfloat16
    sds = jax.ShapeDtypeStruct
    mib = 1 << 20

    fields = model_state.reshape(rows * levels, lanes)
    counts = sea_count.reshape(1, rows)
    place = lax.axis_index(("comp", "row", "col")).astype(jnp.int32).reshape(1)
    own = surface[0]
    comp_size = lax.axis_size("comp")
    partner = lax.ppermute(own, "comp", [(i, comp_size - 1 - i) for i in range(comp_size)])

    slots = pl.cdiv(rows, 64)

    def call(kernel, grid, in_specs, out_specs, out_shape, args, scratch=(), vmem=59, flops=10**7, size=0, aliases={}):
        return pl.pallas_call(
            functools.partial(kernel, n_row=n_row, n_col=n_col),
            out_shape=out_shape,
            grid_spec=pltpu.PrefetchScalarGridSpec(
                num_scalar_prefetch=1, grid=grid, in_specs=in_specs, out_specs=out_specs, scratch_shapes=scratch),
            compiler_params=pltpu.CompilerParams(vmem_limit_bytes=vmem * mib),
            input_output_aliases=aliases,
            cost_estimate=cost(flops, size),
        )(place, *args)

    smem = pl.BlockSpec(memory_space=pltpu.SMEM)
    anywhere = pl.BlockSpec(memory_space=pl.ANY)
    state_bytes = 4 * rows * levels * lanes
    vmem = pl.BlockSpec(memory_space=pltpu.VMEM)
    edge_shape = (slots, levels, lanes)
    ends_shape = (2, levels, lanes)
    *send, mixed, edge = call(
        functools.partial(entry_kernel, widths=widths, block=block), (),
        [smem, anywhere, smem, vmem],
        [anywhere] * (n_row * chunks + 1) + [vmem],
        [sds((w, rows, lanes), bf16) for w in widths for _ in range(n_row)]
        + [sds((rows * levels, lanes), f32), sds(edge_shape, bf16)],
        (counts, fields, gauss_weight, mixing),
        scratch=[pltpu.VMEM((256, 256), bf16), pltpu.VMEM(edge_shape, f32), pltpu.VMEM(ends_shape, bf16)],
        vmem=63, size=2 * state_bytes,
    )

    near_parts = [k for k in range(1, n_row) if k & (k + 1) == 0]

    def traded(parts, name):
        got = [parts[0]]
        for k in range(1, n_row):
            real = k in near_parts and name[-1] == "0"
            route = [(r, r ^ k) for r in range(n_row)]
            for r in range(n_row, n_row * comp_size):
                route.append((r, r ^ k if real else r ^ 1))
            got.append(lax.ppermute(parts[k], ("comp", "row"), route))
        return got

    chain = [n_col + i for i in range(n_col - 1)]

    def to_columns(x):
        return [
            lax.ppermute(x, ("comp", "col"), [(i + 1, i) for i in chain]),
            lax.ppermute(x, ("comp", "col"), [(i, i + 1) for i in chain]),
        ]

    coeffs = [traded(send[n_row * c:n_row * (c + 1)], f"there{c}") for c in range(chunks)]
    sides = to_columns(edge)

    halves = 2 if rows % 16 == 0 else 1
    share = rows // halves
    whole = pl.BlockSpec((rows, lanes), lambda i, s: (0, 0))
    surfaces = []

    def remap(half, after):
        piece = pl.BlockSpec((share, lanes), lambda i, s: (half, 0))
        earlier = surfaces[-1] if surfaces else ()
        surfaces.append(call(
            functools.partial(surface_kernel, first=half * share, group=2), (1,),
            [smem, whole, piece, piece] + [anywhere] * (len(earlier) + len(after)),
            [piece] * 2, [sds((rows, lanes), f32)] * 2,
            (counts, partner, own, remap_source[0], *earlier, *after),
            aliases={5 + i: i for i in range(len(earlier))},
            flops=10**10, size=3 * 4 * rows * lanes,
        ))

    remap(0, (edge,))

    def sweep(field, rows_in, cols_in, final, extra=()):
        out_shape = [sds((rows * levels, lanes), f32)]
        out_specs = [anywhere]
        scratch = [pltpu.VMEM(((block + 2) * levels, lanes), f32), pltpu.VMEM(edge_shape, f32)]
        if not final:
            out_shape += [sds(edge_shape, bf16), sds(ends_shape, bf16)]
            out_specs += [vmem, vmem]
            scratch += [pltpu.VMEM(edge_shape, f32)]
        return call(
            functools.partial(sweep_kernel, block=block, near_parts=near_parts, final=final),
            (1,),
            [smem, anywhere, pl.BlockSpec(edge_shape, lambda i, s: (0, 0, 0)),
             pl.BlockSpec(edge_shape, lambda i, s: (0, 0, 0))]
            + [pl.BlockSpec((1, levels, lanes), lambda i, s: (0, 0, 0))] * len(near_parts)
            + ([pl.BlockSpec((rows, lanes), lambda i, s: (0, 0))] if final else []),
            out_specs, out_shape,
            (counts, field, *cols_in, *(rows_in[k] for k in near_parts), *extra),
            scratch=scratch, size=2 * state_bytes,
        )

    first_step, edge, ends = sweep(mixed, coeffs[0], sides, False)
    sides = to_columns(edge)

    returned = []
    for chunk, width in enumerate(widths):
        with_ends = chunk == 0
        first_wave = sum(widths[:chunk])
        part = call(
            functools.partial(legendre_kernel, wave_dev=wave_dev, first_wave=first_wave, with_ends=with_ends),
            (),
            [anywhere] * (1 + n_row) + ([vmem, anywhere] if with_ends else []),
            [anywhere] * n_row,
            [sds((width, rows, lanes), bf16)] * n_row,
            (legendre, *coeffs[chunk], *([ends, surfaces[0][1]] if with_ends else [])),
            scratch=[pltpu.VMEM((n_row, rows, lanes), bf16)], vmem=63,
            flops=4 * width * legendre.shape[1] * legendre.shape[2] * lanes,
            size=2 * width * legendre.shape[1] * legendre.shape[2],
        )
        returned.append(traded(part, f"back{chunk}"))

    if halves > 1:
        remap(1, (first_step,))
    new_surface, gap = surfaces[-1]
    (sea,) = sweep(first_step, returned[0], sides, True, (gap,))

    state = call(
        functools.partial(exit_kernel, widths=widths, block=block), (),
        [anywhere] * (1 + n_row * chunks), anywhere, sds((rows * levels, lanes), f32),
        (sea, *sum(returned, [])), scratch=[pltpu.VMEM((256, 256), bf16)], size=2 * state_bytes, aliases={1: 0},
    )
    return state.reshape(model_state.shape), new_surface[None]


def solution(mesh):
    in_specs = (
        P("comp", "row", None, "col"),
        P("row", None, None),
        P("row"),
        P(),
        P("comp", "row", "col"),
        P("comp", "row", "col"),
        P("comp", "row", "col"),
    )
    out_specs = (P("comp", "row", None, "col"), P("comp", "row", "col"))

    return jax.shard_map(shards, mesh=mesh, in_specs=in_specs, out_specs=out_specs, check_vma=False)
```

time: 93.3 us -> 88.1 us (0.944)
  the two profiles are of different devices: /device:TPU:7 before, /device:TPU:0 now
where the time goes in v6:
time: 88.1 us; the launch traced here: 87.7 us
  Pallas kernels  47.1 us (53%)
  waiting for transfers between devices  23.5 us (27%)
  starting transfers between devices  14 us (16%)
  local copies, waits for them, and re-layouts  2.33 us (3%)
    pallas_call x8, Pallas kernels, call(): pl.pallas_call(functools.partial(kernel, n_row=n_row, n_col=n_col), out_s...  47.1 us
    ppermute x12, waiting for transfers between devices, traded(): got.append(lax.ppermute(parts[k], ('comp', 'row'), route))  23.5 us
    ppermute x12, starting transfers between devices, traded(): got.append(lax.ppermute(parts[k], ('comp', 'row'), route))  8.32 us
    ppermute x1, starting transfers between devices, shards(): lax.ppermute(own, 'comp', [(i, comp_size - 1 - i) for i in range(comp_siz...  3.03 us
    unnamed x30, local copies, waits for them, and re-layouts  2.33 us
  transfers between devices with their start and end apart: 17, of which 4 were waited for; matrix products, arithmetic and copies ran while one was open for 0% of the time, Pallas kernels for 49%

profile of v6, /device:TPU:0, one launch (start us, length us, event | category | flops | bytes accessed | tf_op | source)
XLA Modules:
  0.0 87.7 jit_solution(12775175062776300894)
XLA Ops:
  0.6 3.0 %collective-permute-start.7 = (f32[320,128]{1,0:T(8,128)}, f32[320,128]{1,0:T(8,128)S(1)}, u32[]{:S(2)}, u32[]{:S(2)}) collective-permute-start(f32[320,128]{1,0:T(8,128)} %bitcast.14), channel_id=1, source_target_pairs={{0,16},{16,0},{1,17},{17,1},{2,18},{18,2},{3,19},{19,3},{4,20},{20... | collective-permute-start | bytes 491528 | tf_op jit(solution)/shard_map/ppermute | solution.py:463
  3.7 5.5 %shard_map.86 = (bf16[4,320,128]{2,1,0:T(8,128)(2,1)}, bf16[4,320,128]{2,1,0:T(8,128)(2,1)}, bf16[4,320,128]{2,1,0:T(8,128)(2,1)}, bf16[4,320,128]{2,1,0:T(8,128...) custom-call(s32[1]{0:T(128)} %bitcast.place, ...), custom_call_target="tpu_custom_call" | custom-call | flops 10000000 | bytes 10485760 | tf_op jit(solution)/shard_map/pallas_call | solution.py:468
  9.2 0.7 collective-permute-start
  9.8 0.7 collective-permute-start.1
  10.6 1.6 %collective-permute-start.3 = (bf16[4,320,128]{2,1,0:T(8,128)(2,1)}, bf16[4,320,128]{2,1,0:T(8,128)(2,1)S(1)}, u32[]{:S(2)}, u32[]{:S(2)}) collective-permute-start(bf16[4,320,128]{2,1,0:T(8,128)(2,1)} %get-tuple-element.30), channel_id=1, source_target_pairs={{0,12},{4,8},{8,4},{12,0},{16,28},{20,24},{24,20},{28,16},{1,13},{... | collective-permute-start | bytes 983048 | tf_op jit(solution)/shard_map/ppermute | solution.py:504
  12.2 0.5 collective-permute-start.6
  12.9 7.2 %shard_map.88 = (f32[320,128]{1,0:T(8,128)}, f32[320,128]{1,0:T(8,128)}) custom-call(s32[1]{0:T(128)} %bitcast.place, s32[1,320]{1,0:T(1,128)} %bitcast.10, f32[320,128]{1,0:T(8,128)} %copy-done.13, f32[320,128]{1,0:T(8,128)} %bitcast.15, s32[320,128]{1,0:T(8,128)} %bitcast.17, bf16[5,32,128]{2,1,0:T(8,128)(2,1)} %get-tuple-element.28.rest_0_), custom_call_target="tpu_custom_call" | custom-call | flops 10000000000 | bytes 491520 | tf_op jit(solution)/shard_map/pallas_call | solution.py:468
  20.2 1.4 %collective-permute-start.12 = (bf16[4,320,128]{2,1,0:T(8,128)(2,1)}, bf16[4,320,128]{2,1,0:T(8,128)(2,1)}, u32[]{:S(2)}, u32[]{:S(2)}) collective-permute-start(bf16[4,320,128]{2,1,0:T(8,128)(2,1)} %get-tuple-element.45), channel_id=1, source_target_pairs={{0,8},{4,12},{8,0},{12,4},{16,20},{20,16},{24,28},{28,24},{1,9},{5... | collective-permute-start | bytes 983048 | tf_op jit(solution)/shard_map/ppermute | solution.py:504
  22.7 1.5 %shard_map.87 = (f32[10240,128]{1,0:T(8,128)}, bf16[5,32,128]{2,1,0:T(8,128)(2,1)}, bf16[2,32,128]{2,1,0:T(8,128)(2,1)}) custom-call(s32[1]{0:T(128)} %bitcast.place, s32[1,320]{1,0:T(1,128)} %bitcast.11, f32[10240,128]{1,0:T(8,128)} %get-tuple-element.27.field, bf16[5,32,128]{2,1,0:T(8,128)(2,1)} %copy-done.11, bf16[5,32,128]{2,1,0:T(8,128)(2,1)} %copy-done.12, ...), custom_call_target="tpu_custom_call" | custom-call | flops 10000000 | bytes 10485760 | tf_op jit(solution)/shard_map/pallas_call | solution.py:468
  24.2 4.4 %collective-permute-done.6.rest_2_ = bf16[4,320,128]{2,1,0:T(8,128)(2,1)} collective-permute-done((bf16[4,320,128]{2,1,0:T(8,128)(2,1)}, bf16[4,320,128]{2,1,0:T(8,128)(2,1)}, u32[]{:S(2)}, u32[]{:S(2)}) %collective-permute-start.6) | collective-permute-done | bytes 327712 | tf_op jit(solution)/shard_map/ppermute | solution.py:504
  28.6 10.5 %shard_map.89 = (bf16[4,320,128]{2,1,0:T(8,128)(2,1)}, bf16[4,320,128]{2,1,0:T(8,128)(2,1)}, bf16[4,320,128]{2,1,0:T(8,128)(2,1)}, bf16[4,320,128]{2,1,0:T(8,128)(2,1)}) custom-call(s32[1]{0:T(128)} %bitcast.place, bf16[8,1280,1280]{2,1,0:T(8,128)(2,1)} %legendre.3, bf16[4,320,128]{2,1,0:T(8,128)(2,1)} %get-tuple-element.33.rest_0_, ...), custom_call_target="tpu_custom_call" | custom-call | flops 3355443200 | bytes 13107200 | tf_op jit(solution)/shard_map/pallas_call | solution.py:468
  39.1 0.7 collective-permute-start.4
  39.8 0.7 collective-permute-start.5
  40.5 0.9 %collective-permute-done.13.rest_3_ = bf16[4,320,128]{2,1,0:T(8,128)(2,1)} collective-permute-done((bf16[4,320,128]{2,1,0:T(8,128)(2,1)}, bf16[4,320,128]{2,1,0:T(8,128)(2,1)}, u32[]{:S(2)}, u32[]{:S(2)}) %collective-permute-start.13) | collective-permute-done | bytes 327712 | tf_op jit(solution)/shard_map/ppermute | solution.py:504
  41.4 9.8 %shard_map.92 = (bf16[4,320,128]{2,1,0:T(8,128)(2,1)}, bf16[4,320,128]{2,1,0:T(8,128)(2,1)}, bf16[4,320,128]{2,1,0:T(8,128)(2,1)}, bf16[4,320,128]{2,1,0:T(8,128)(2,1)}) custom-call(s32[1]{0:T(128)} %bitcast.place, bf16[8,1280,1280]{2,1,0:T(8,128)(2,1)} %legendre.3, bf16[4,320,128]{2,1,0:T(8,128)(2,1)} %get-tuple-element.43.rest_0_, ...), custom_call_target="tpu_custom_call" | custom-call | flops 3355443200 | bytes 13107200 | tf_op jit(solution)/shard_map/pallas_call | solution.py:468
  51.7 1.6 %collective-permute-start.15 = (bf16[4,320,128]{2,1,0:T(8,128)(2,1)}, bf16[4,320,128]{2,1,0:T(8,128)(2,1)S(1)}, u32[]{:S(2)}, u32[]{:S(2)}) collective-permute-start(bf16[4,320,128]{2,1,0:T(8,128)(2,1)} %get-tuple-element.49), channel_id=1, source_target_pairs={{0,8},{4,12},{8,0},{12,4},{16,20},{20,16},{24,28},{28,24},{1,9},{5... | collective-permute-start | bytes 983048 | tf_op jit(solution)/shard_map/ppermute | solution.py:504
  53.3 1.7 %collective-permute-start.9 = (bf16[4,320,128]{2,1,0:T(8,128)(2,1)}, bf16[4,320,128]{2,1,0:T(8,128)(2,1)S(1)}, u32[]{:S(2)}, u32[]{:S(2)}) collective-permute-start(bf16[4,320,128]{2,1,0:T(8,128)(2,1)} %get-tuple-element.38), channel_id=1, source_target_pairs={{0,12},{4,8},{8,4},{12,0},{16,28},{20,24},{24,20},{28,16},{1,13},{... | collective-permute-start | bytes 983048 | tf_op jit(solution)/shard_map/ppermute | solution.py:504
  55.5 7.2 %shard_map.90 = (f32[320,128]{1,0:T(8,128)}, f32[320,128]{1,0:T(8,128)}) custom-call(s32[1]{0:T(128)} %bitcast.place, s32[1,320]{1,0:T(1,128)} %bitcast.12, f32[320,128]{1,0:T(8,128)} %copy-done.13, f32[320,128]{1,0:T(8,128)} %bitcast.16, s32[320,128]{1,0:T(8,128)} %bitcast.18, ...), custom_call_target="tpu_custom_call", output_to_operand_aliasing={{0}: (5, {}), {1}: (6, {})} | custom-call | flops 10000000000 | bytes 491520 | tf_op jit(solution)/shard_map/pallas_call | solution.py:468
  62.7 13.0 %collective-permute-done.9.rest_1_.rest_3_ = bf16[4,320,128]{2,1,0:T(8,128)(2,1)S(1)} collective-permute-done((bf16[4,320,128]{2,1,0:T(8,128)(2,1)}, bf16[4,320,128]{2,1,0:T(8,128)(2,1)S(1)}, u32[]{:S(2)}, u32[]{:S(2)}) %collective-permute-start.9) | collective-permute-done | bytes 327712 | tf_op jit(solution)/shard_map/ppermute | solution.py:504
  75.8 0.7 copy-done.1
  76.5 1.0 %shard_map.91.sea = f32[10240,128]{1,0:T(8,128)} custom-call(s32[1]{0:T(128)} %bitcast.place, s32[1,320]{1,0:T(1,128)} %bitcast.13, f32[10240,128]{1,0:T(8,128)} %get-tuple-element.31.rest_2_.field, bf16[5,32,128]{2,1,0:T(8,128)(2,1)} %copy-done.9, bf16[5,32,128]{2,1,0:T(8,128)(2,1)} %copy-done.10, bf16[4,320,128]{2,1,0:T(8,128)(2,1)} %copy-done, ...), custom_call_target="tpu_custom_call" | custom-call | flops 10000000 | bytes 10485760 | tf_op jit(solution)/shard_map/pallas_call | solution.py:468
  77.6 5.1 %collective-permute-done.10.rest_2_ = bf16[4,320,128]{2,1,0:T(8,128)(2,1)S(1)} collective-permute-done((bf16[4,320,128]{2,1,0:T(8,128)(2,1)}, bf16[4,320,128]{2,1,0:T(8,128)(2,1)S(1)}, u32[]{:S(2)}, u32[]{:S(2)}) %collective-permute-start.10) | collective-permute-done | bytes 327712 | tf_op jit(solution)/shard_map/ppermute | solution.py:504
  82.7 0.7 copy-done.7
  83.4 4.3 %shard_map.93 = f32[10240,128]{1,0:T(8,128)} custom-call(s32[1]{0:T(128)} %bitcast.place, f32[10240,128]{1,0:T(8,128)} %shard_map.91.sea, bf16[4,320,128]{2,1,0:T(8,128)(2,1)} %get-tuple-element.41.rest_0_, bf16[4,320,128]{2,1,0:T(8,128)(2,1)} %copy-done, bf16[4,320,128]{2,1,0:T(8,128)(2,1)} %copy-done.7, ...), custom_call_target="tpu_custom_call", output_to_operand_aliasing={{}: (1, {})} | custom-call | flops 10000000 | bytes 10485760 | tf_op jit(solution)/shard_map/pallas_call | solution.py:468
  (48 shorter events, 2.4 us)
Async XLA Ops:
  0.6 11.6 %collective-permute-start.7 = (f32[320,128]{1,0:T(8,128)}, f32[320,128]{1,0:T(8,128)S(1)}, u32[]{:S(2)}, u32[]{:S(2)}) collective-permute-start(f32[320,128]{1,0:T(8,128)} %bitcast.14), channel_id=1, source_target_pairs={{0,16},{16,0},{1,17},{17,1},{2,18},{18,2},{3,19},{19,3},{4,20},{20... | collective-permute-start | bytes 491528 | tf_op jit(solution)/shard_map/ppermute | solution.py:463
  9.2 10.9 %collective-permute-start = (bf16[5,32,128]{2,1,0:T(8,128)(2,1)}, bf16[5,32,128]{2,1,0:T(8,128)(2,1)S(1)}, u32[]{:S(2)}, u32[]{:S(2)}) collective-permute-start(bf16[5,32,128]{2,1,0:T(8,128)(2,1)} %get-tuple-element.28.rest_0_), channel_id=1, source_target_pairs={{17,16},{18,17},{19,18},{21,20},{22,21},{23,22},{25,24},{26,25},{2... | collective-permute-start | bytes 122888 | tf_op jit(solution)/shard_map/ppermute | solution.py:511
  9.8 10.4 %collective-permute-start.1 = (bf16[5,32,128]{2,1,0:T(8,128)(2,1)}, bf16[5,32,128]{2,1,0:T(8,128)(2,1)S(1)}, u32[]{:S(2)}, u32[]{:S(2)}) collective-permute-start(bf16[5,32,128]{2,1,0:T(8,128)(2,1)} %get-tuple-element.28.rest_0_), channel_id=1, source_target_pairs={{16,17},{17,18},{18,19},{20,21},{21,22},{22,23},{24,25},{25,26},{2... | collective-permute-start | bytes 122888 | tf_op jit(solution)/shard_map/ppermute | solution.py:512
  10.5 11.1 %collective-permute-start.2 = (bf16[4,320,128]{2,1,0:T(8,128)(2,1)}, bf16[4,320,128]{2,1,0:T(8,128)(2,1)S(1)}, u32[]{:S(2)}, u32[]{:S(2)}) collective-permute-start(bf16[4,320,128]{2,1,0:T(8,128)(2,1)} %get-tuple-element.29), channel_id=1, source_target_pairs={{0,4},{4,0},{8,12},{12,8},{16,20},{20,16},{24,28},{28,24},{1,5},{5... | collective-permute-start | bytes 983048 | tf_op jit(solution)/shard_map/ppermute | solution.py:504
  10.6 11.4 %collective-permute-start.3 = (bf16[4,320,128]{2,1,0:T(8,128)(2,1)}, bf16[4,320,128]{2,1,0:T(8,128)(2,1)S(1)}, u32[]{:S(2)}, u32[]{:S(2)}) collective-permute-start(bf16[4,320,128]{2,1,0:T(8,128)(2,1)} %get-tuple-element.30), channel_id=1, source_target_pairs={{0,12},{4,8},{8,4},{12,0},{16,28},{20,24},{24,20},{28,16},{1,13},{... | collective-permute-start | bytes 983048 | tf_op jit(solution)/shard_map/ppermute | solution.py:504
  12.2 16.4 %collective-permute-start.6 = (bf16[4,320,128]{2,1,0:T(8,128)(2,1)}, bf16[4,320,128]{2,1,0:T(8,128)(2,1)}, u32[]{:S(2)}, u32[]{:S(2)}) collective-permute-start(bf16[4,320,128]{2,1,0:T(8,128)(2,1)} %get-tuple-element.34), channel_id=1, source_target_pairs={{0,8},{4,12},{8,0},{12,4},{16,20},{20,16},{24,28},{28,24},{1,9},{5... | collective-permute-start | bytes 983048 | tf_op jit(solution)/shard_map/ppermute | solution.py:504
  20.1 19.7 %collective-permute-start.11 = (bf16[4,320,128]{2,1,0:T(8,128)(2,1)}, bf16[4,320,128]{2,1,0:T(8,128)(2,1)S(1)}, u32[]{:S(2)}, u32[]{:S(2)}) collective-permute-start(bf16[4,320,128]{2,1,0:T(8,128)(2,1)} %get-tuple-element.44), channel_id=1, source_target_pairs={{0,4},{4,0},{8,12},{12,8},{16,20},{20,16},{24,28},{28,24},{1,5},{5... | collective-permute-start | bytes 983048 | tf_op jit(solution)/shard_map/ppermute | solution.py:504
  20.2 20.3 %collective-permute-start.12 = (bf16[4,320,128]{2,1,0:T(8,128)(2,1)}, bf16[4,320,128]{2,1,0:T(8,128)(2,1)}, u32[]{:S(2)}, u32[]{:S(2)}) collective-permute-start(bf16[4,320,128]{2,1,0:T(8,128)(2,1)} %get-tuple-element.45), channel_id=1, source_target_pairs={{0,8},{4,12},{8,0},{12,4},{16,20},{20,16},{24,28},{28,24},{1,9},{5... | collective-permute-start | bytes 983048 | tf_op jit(solution)/shard_map/ppermute | solution.py:504
  21.6 19.8 %collective-permute-start.13 = (bf16[4,320,128]{2,1,0:T(8,128)(2,1)}, bf16[4,320,128]{2,1,0:T(8,128)(2,1)}, u32[]{:S(2)}, u32[]{:S(2)}) collective-permute-start(bf16[4,320,128]{2,1,0:T(8,128)(2,1)} %get-tuple-element.46), channel_id=1, source_target_pairs={{0,12},{4,8},{8,4},{12,0},{16,20},{20,16},{24,28},{28,24},{1,13},{... | collective-permute-start | bytes 983048 | tf_op jit(solution)/shard_map/ppermute | solution.py:504
  28.6 10.5 %copy-start.14 = (bf16[5,32,128]{2,1,0:T(8,128)(2,1)S(1)}, bf16[5,32,128]{2,1,0:T(8,128)(2,1)}, u32[]{:S(2)}) copy-start(bf16[5,32,128]{2,1,0:T(8,128)(2,1)} %get-tuple-element.32) | copy-start | bytes 122884
  39.1 15.9 %collective-permute-start.8 = (bf16[4,320,128]{2,1,0:T(8,128)(2,1)}, bf16[4,320,128]{2,1,0:T(8,128)(2,1)S(1)}, u32[]{:S(2)}, u32[]{:S(2)}) collective-permute-start(bf16[4,320,128]{2,1,0:T(8,128)(2,1)} %get-tuple-element.37), channel_id=1, source_target_pairs={{0,4},{4,0},{8,12},{12,8},{16,20},{20,16},{24,28},{28,24},{1,5},{5... | collective-permute-start | bytes 983048 | tf_op jit(solution)/shard_map/ppermute | solution.py:504
  39.1 14.2 %collective-permute-start.4 = (bf16[5,32,128]{2,1,0:T(8,128)(2,1)S(1)}, bf16[5,32,128]{2,1,0:T(8,128)(2,1)S(1)}, u32[]{:S(2)}, u32[]{:S(2)}) collective-permute-start(bf16[5,32,128]{2,1,0:T(8,128)(2,1)S(1)} %copy-done.14), channel_id=1, source_target_pairs={{17,16},{18,17},{19,18},{21,20},{22,21},{23,22},{25,24},{26,25},{2... | collective-permute-start | bytes 122888 | tf_op jit(solution)/shard_map/ppermute | solution.py:511
  39.8 13.5 %collective-permute-start.5 = (bf16[5,32,128]{2,1,0:T(8,128)(2,1)S(1)}, bf16[5,32,128]{2,1,0:T(8,128)(2,1)S(1)}, u32[]{:S(2)}, u32[]{:S(2)}) collective-permute-start(bf16[5,32,128]{2,1,0:T(8,128)(2,1)S(1)} %copy-done.14), channel_id=1, source_target_pairs={{16,17},{17,18},{18,19},{20,21},{21,22},{22,23},{24,25},{25,26},{2... | collective-permute-start | bytes 122888 | tf_op jit(solution)/shard_map/ppermute | solution.py:512
  51.3 26.2 %collective-permute-start.14 = (bf16[4,320,128]{2,1,0:T(8,128)(2,1)}, bf16[4,320,128]{2,1,0:T(8,128)(2,1)S(1)}, u32[]{:S(2)}, u32[]{:S(2)}) collective-permute-start(bf16[4,320,128]{2,1,0:T(8,128)(2,1)} %get-tuple-element.48), channel_id=1, source_target_pairs={{0,4},{4,0},{8,12},{12,8},{16,20},{20,16},{24,28},{28,24},{1,5},{5... | collective-permute-start | bytes 983048 | tf_op jit(solution)/shard_map/ppermute | solution.py:504
  51.7 25.8 %collective-permute-start.15 = (bf16[4,320,128]{2,1,0:T(8,128)(2,1)}, bf16[4,320,128]{2,1,0:T(8,128)(2,1)S(1)}, u32[]{:S(2)}, u32[]{:S(2)}) collective-permute-start(bf16[4,320,128]{2,1,0:T(8,128)(2,1)} %get-tuple-element.49), channel_id=1, source_target_pairs={{0,8},{4,12},{8,0},{12,4},{16,20},{20,16},{24,28},{28,24},{1,9},{5... | collective-permute-start | bytes 983048 | tf_op jit(solution)/shard_map/ppermute | solution.py:504
  53.3 9.4 %copy-start.9 = (bf16[5,32,128]{2,1,0:T(8,128)(2,1)}, bf16[5,32,128]{2,1,0:T(8,128)(2,1)S(1)}, u32[]{:S(2)}) copy-start(bf16[5,32,128]{2,1,0:T(8,128)(2,1)S(1)} %collective-permute-done.4.east_in) | copy-start | bytes 122884
  53.3 24.2 %collective-permute-start.16 = (bf16[4,320,128]{2,1,0:T(8,128)(2,1)}, bf16[4,320,128]{2,1,0:T(8,128)(2,1)S(1)}, u32[]{:S(2)}, u32[]{:S(2)}) collective-permute-start(bf16[4,320,128]{2,1,0:T(8,128)(2,1)} %get-tuple-element.50), channel_id=1, source_target_pairs={{0,12},{4,8},{8,4},{12,0},{16,20},{20,16},{24,28},{28,24},{1,13},{... | collective-permute-start | bytes 983048 | tf_op jit(solution)/shard_map/ppermute | solution.py:504
  53.3 9.4 %copy-start.10 = (bf16[5,32,128]{2,1,0:T(8,128)(2,1)}, bf16[5,32,128]{2,1,0:T(8,128)(2,1)S(1)}, u32[]{:S(2)}) copy-start(bf16[5,32,128]{2,1,0:T(8,128)(2,1)S(1)} %collective-permute-done.5.west_in) | copy-start | bytes 122884
  53.3 22.4 %collective-permute-start.9 = (bf16[4,320,128]{2,1,0:T(8,128)(2,1)}, bf16[4,320,128]{2,1,0:T(8,128)(2,1)S(1)}, u32[]{:S(2)}, u32[]{:S(2)}) collective-permute-start(bf16[4,320,128]{2,1,0:T(8,128)(2,1)} %get-tuple-element.38), channel_id=1, source_target_pairs={{0,12},{4,8},{8,4},{12,0},{16,28},{20,24},{24,20},{28,16},{1,13},{... | collective-permute-start | bytes 983048 | tf_op jit(solution)/shard_map/ppermute | solution.py:504
  55.1 7.6 %copy-start = (bf16[4,320,128]{2,1,0:T(8,128)(2,1)}, bf16[4,320,128]{2,1,0:T(8,128)(2,1)S(1)}, u32[]{:S(2)}) copy-start(bf16[4,320,128]{2,1,0:T(8,128)(2,1)S(1)} %collective-permute-done.8.rest_0_.rest_1_) | copy-start | bytes 983044
  55.1 27.6 %collective-permute-start.10 = (bf16[4,320,128]{2,1,0:T(8,128)(2,1)}, bf16[4,320,128]{2,1,0:T(8,128)(2,1)S(1)}, u32[]{:S(2)}, u32[]{:S(2)}) collective-permute-start(bf16[4,320,128]{2,1,0:T(8,128)(2,1)} %get-tuple-element.42), channel_id=1, source_target_pairs={{0,8},{4,12},{8,0},{12,4},{16,20},{20,16},{24,28},{28,24},{1,9},{5... | collective-permute-start | bytes 983048 | tf_op jit(solution)/shard_map/ppermute | solution.py:504
  77.5 5.2 %copy-start.4 = (bf16[4,320,128]{2,1,0:T(8,128)(2,1)}, bf16[4,320,128]{2,1,0:T(8,128)(2,1)S(1)}, u32[]{:S(2)}) copy-start(bf16[4,320,128]{2,1,0:T(8,128)(2,1)S(1)} %collective-permute-done.14.rest_5_) | copy-start | bytes 983044
  77.5 5.1 %copy-start.5 = (bf16[4,320,128]{2,1,0:T(8,128)(2,1)}, bf16[4,320,128]{2,1,0:T(8,128)(2,1)S(1)}, u32[]{:S(2)}) copy-start(bf16[4,320,128]{2,1,0:T(8,128)(2,1)S(1)} %collective-permute-done.15.rest_6_) | copy-start | bytes 983044
  77.6 5.1 %copy-start.6 = (bf16[4,320,128]{2,1,0:T(8,128)(2,1)}, bf16[4,320,128]{2,1,0:T(8,128)(2,1)S(1)}, u32[]{:S(2)}) copy-start(bf16[4,320,128]{2,1,0:T(8,128)(2,1)S(1)} %collective-permute-done.16.rest_7_) | copy-start | bytes 983044
  (8 other events, 8.9 us)

commit v7 on v6

--- a/solution.py
+++ b/solution.py
@@ -80,56 +80,66 @@
     return jnp.dot(a, b, preferred_element_type=jnp.float32)
 
 
-def entry_kernel(place, counts, field, gauss, mix, *rest, n_row, n_col, widths, block):
-    chunks = len(widths)
-    send = [rest[n_row * c:n_row * (c + 1)] for c in range(chunks)]
-    mixed, edge, table, packed, ends = rest[n_row * chunks:]
-    comp, row, _ = where_am_i(place, n_row, n_col)
+def parts_of_half(half, n_row, wave_dev):
+    return [k for k in range(n_row) if k * wave_dev // 16 == half]
+
+
+def entry_kernel(place, counts, field, waves, gauss, mix, *rest, n_row, n_col, widths, block, half):
     levels = mix.shape[0]
     wave_dev = levels // n_row
+    mine = parts_of_half(half, n_row, wave_dev)
+    chunks = len(widths)
+    total = len(mine) * chunks
+    if half:
+        send, (mixed, edge, ends, table, packed, sems) = rest[:total], rest[total:]
+    else:
+        ends, send, (table, sems) = rest[0], rest[1:1 + total], rest[1 + total:]
+    comp, row, _ = where_am_i(place, n_row, n_col)
     tall = block * levels
     steps = field.shape[0] // tall
     state_block = pl.BlockSpec((tall, lanes), lambda i: (i, 0))
-
     flip = row * wave_dev
-
-    def weigh(field, *parts):
+    first_parts = {k: send[n] for n, k in enumerate(mine)}
+
+    def weigh(waves, *parts):
         step = pl.program_id(0)
 
         def target(wave):
-            part, local = divmod(wave, wave_dev)
+            part, local = divmod(16 * half + wave, wave_dev)
             chunk, slot = chunk_of(local, widths)
-            return parts[n_row * chunk + part], slot
-
-        for lat in range(0, block - 15, 16):
-            halves = []
-            for half in range(0, levels, 16):
-                halves.append(jnp.concatenate([
-                    (field[pl.ds(pl.multiple_of((lat + s) * levels + (half ^ (flip & ~15)), 16), 16), :]
-                     * gauss[step * block + lat + s]).astype(jnp.bfloat16)
-                    for s in range(16)
-                ], axis=0))
-            turned = product(table[...], jnp.concatenate(halves, axis=1)).astype(jnp.bfloat16)
-            for wave in range(levels):
+            return parts[len(mine) * chunk + mine.index(part)], slot
+
+        for lat in range(0, block, 16):
+            size = min(16, block - lat)
+            rows = jnp.concatenate([
+                (waves[lat + s] * gauss[step * block + lat + s]).astype(jnp.bfloat16) for s in range(size)
+            ], axis=0)
+            if size == 16:
+                swap = table[...]
+            else:
+                shape = (16 * size, 16 * size)
+                line, column = iota(shape, 0), iota(shape, 1)
+                swap = as_bf16(column == ((line & (size - 1)) << 4 | ((line // size) ^ (flip & 15))))
+            turned = product(swap, rows).astype(jnp.bfloat16)
+            for wave in range(16):
                 out, slot = target(wave)
-                part = lanes * (wave // 16)
-                out[slot, lat:lat + 16, :] = turned[16 * (wave % 16):16 * (wave % 16) + 16, part:part + lanes]
-        for lat in range(block - block % 16, block, 8):
-            weight = jnp.zeros((8, lanes), jnp.float32)
-            for s in range(8):
-                weight = jnp.where(iota((8, lanes), 0) == s, gauss[step * block + lat + s], weight)
-            for wave in range(levels):
-                out, slot = target(wave)
-                values = field[pl.ds(lat * levels + (wave ^ flip), 8, stride=levels), :] * weight
-                out[slot, lat:lat + 8, :] = values.astype(jnp.bfloat16)
+                out[slot, lat:lat + size, :] = turned[size * wave:size * (wave + 1), :]
 
     @pl.when(comp == 0)
     def _():
         table[...] = swap_matrix(flip & 15, 0)
         pltpu.emit_pipeline(
-            weigh, grid=(steps,), in_specs=[state_block],
-            out_specs=[pl.BlockSpec((w, block, lanes), lambda i: (0, i, 0)) for w in widths for _ in range(n_row)],
-        )(field, *sum(send, ()))
+            weigh, grid=(steps,),
+            in_specs=[pl.BlockSpec((block, pl.Squeezed(), 16, lanes), lambda i: (i, half ^ (flip >> 4), 0, 0))],
+            out_specs=[pl.BlockSpec((w, block, lanes), lambda i: (0, i, 0)) for w in widths for _ in mine],
+        )(waves, *send)
+
+    if not half:
+        @pl.when(comp != 0)
+        def _():
+            hand_on(ends, first_parts, row, sems)
+
+        return
 
     def mixed_rows(ref, start, first_row):
         values = []
@@ -193,13 +203,20 @@
 
         pltpu.emit_pipeline(blend, grid=(steps,), in_specs=[state_block], out_specs=[state_block])(field, mixed)
         edge[...] = packed[...].astype(jnp.bfloat16)
-        hand_on(ends, send[0], row)
-
-
-def hand_on(ends, parts, row):
+        hand_on(ends, first_parts, row, sems)
+
+
+def hand_on(ends, parts, row, sems):
     levels = ends.shape[1]
-    for k in range(1, len(parts)):
-        pltpu.sync_copy(ends.at[((k ^ row) > row).astype(jnp.int32)], parts[k].at[0, pl.ds(0, levels)])
+    copies = [
+        pltpu.make_async_copy(
+            ends.at[((k ^ row) > row).astype(jnp.int32)], part.at[0, pl.ds(0, levels)], sems.at[k])
+        for k, part in parts.items() if k
+    ]
+    for copy in copies:
+        copy.start()
+    for copy in copies:
+        copy.wait()
 
 
 def pack(packed, base, rows, spread):
@@ -213,7 +230,7 @@
     packed[slot] = kept
 
 
-def sweep_kernel(place, counts, field, east_in, west_in, *rest, block, n_row, n_col, near_parts, final):
+def sweep_kernel(place, counts, field, near_in, far_in, *rest, block, n_row, n_col, near_parts, final):
     halos, rest = rest[:len(near_parts)], rest[len(near_parts):]
     if final:
         gap, out, masked, sides = rest
@@ -246,8 +263,10 @@
             return found
 
         for slot in range(sides.shape[0]):
-            west = jnp.where(col > 0, west_in[slot].astype(jnp.float32), 0.0)
-            east = jnp.where(col < n_col - 1, east_in[slot].astype(jnp.float32), 0.0)
+            near, far = near_in[slot].astype(jnp.float32), far_in[slot].astype(jnp.float32)
+            east_is_near = (col & 1) == 0
+            west = jnp.where(col > 0, jnp.where(east_is_near, far, near), 0.0)
+            east = jnp.where(col < n_col - 1, jnp.where(east_is_near, near, far), 0.0)
             sides[slot] = jnp.where((lane & 1) == 0, pltpu.roll(east, lanes - 1, 1), pltpu.roll(west, 1, 1))
         if not final:
             packed[...] = jnp.zeros_like(packed)
@@ -323,7 +342,7 @@
     coeffs, rest = rest[:n_row], rest[n_row:]
     if with_ends:
         ends, rest = rest[0], rest[2:]
-    out, gathered = rest[:n_row], rest[n_row]
+    out, (gathered, sems) = rest[:n_row], rest[n_row:]
     comp, row, _ = where_am_i(place, n_row, n_col)
     waves, lats = coeffs[0].shape[:2]
     count = legendre.shape[2]
@@ -357,11 +376,12 @@
     if with_ends:
         @pl.when(comp != 0)
         def _():
-            hand_on(ends, out, row)
-
-
-def surface_kernel(place, counts, partner, own, source, *rest, first, group, n_row, n_col):
+            hand_on(ends, dict(enumerate(out)), row, sems)
+
+
+def surface_kernel(place, counts, partner, own, source, *rest, first_piece, group, n_row, n_col):
     new, gap = rest[-2:]
+    first = (first_piece + pl.program_id(0)) * source.shape[0]
     half = partner.shape[0] // 2
     width = 2 * lanes
     table = jnp.concatenate(
@@ -453,7 +473,6 @@
     block = row_block(rows)
     f32, bf16 = jnp.float32, jnp.bfloat16
     sds = jax.ShapeDtypeStruct
-    mib = 1 << 20
 
     fields = model_state.reshape(rows * levels, lanes)
     counts = sea_count.reshape(1, rows)
@@ -464,13 +483,13 @@
 
     slots = pl.cdiv(rows, 64)
 
-    def call(kernel, grid, in_specs, out_specs, out_shape, args, scratch=(), vmem=59, flops=10**7, size=0, aliases={}):
+    def call(kernel, grid, in_specs, out_specs, out_shape, args, scratch=(), vmem_limit=66700000, flops=10**7, size=0, aliases={}):
         return pl.pallas_call(
             functools.partial(kernel, n_row=n_row, n_col=n_col),
             out_shape=out_shape,
             grid_spec=pltpu.PrefetchScalarGridSpec(
                 num_scalar_prefetch=1, grid=grid, in_specs=in_specs, out_specs=out_specs, scratch_shapes=scratch),
-            compiler_params=pltpu.CompilerParams(vmem_limit_bytes=vmem * mib),
+            compiler_params=pltpu.CompilerParams(vmem_limit_bytes=vmem_limit),
             input_output_aliases=aliases,
             cost_estimate=cost(flops, size),
         )(place, *args)
@@ -481,16 +500,29 @@
     vmem = pl.BlockSpec(memory_space=pltpu.VMEM)
     edge_shape = (slots, levels, lanes)
     ends_shape = (2, levels, lanes)
-    *send, mixed, edge = call(
-        functools.partial(entry_kernel, widths=widths, block=block), (),
-        [smem, anywhere, smem, vmem],
-        [anywhere] * (n_row * chunks + 1) + [vmem],
-        [sds((w, rows, lanes), bf16) for w in widths for _ in range(n_row)]
-        + [sds((rows * levels, lanes), f32), sds(edge_shape, bf16)],
-        (counts, fields, gauss_weight, mixing),
-        scratch=[pltpu.VMEM((256, 256), bf16), pltpu.VMEM(edge_shape, f32), pltpu.VMEM(ends_shape, bf16)],
-        vmem=63, size=2 * state_bytes,
-    )
+    send = {}
+    wave_blocks = model_state.reshape(rows, levels // 16, 16, lanes)
+
+    def enter(half, extra_in, extra_specs, extra_out, scratch):
+        mine = parts_of_half(half, n_row, wave_dev)
+        keys = [(c, k) for c in range(chunks) for k in mine]
+        got = call(
+            functools.partial(entry_kernel, widths=widths, block=block, half=half), (),
+            [smem, anywhere, anywhere, smem, vmem] + [vmem] * len(extra_in),
+            [anywhere] * len(keys) + extra_specs,
+            [sds((widths[c], rows, lanes), bf16) for c, _ in keys] + extra_out,
+            (counts, fields, wave_blocks, gauss_weight, mixing, *extra_in),
+            scratch=[pltpu.VMEM((256, 256), bf16)] + scratch + [pltpu.SemaphoreType.DMA((n_row,))],
+            size=state_bytes,
+        )
+        send.update(zip(keys, got))
+        return got[len(keys):]
+
+    mixed, edge, tile_ends = enter(
+        1, [], [anywhere, vmem, vmem],
+        [sds((rows * levels, lanes), f32), sds(edge_shape, bf16), sds(ends_shape, bf16)],
+        [pltpu.VMEM(edge_shape, f32)])
+    enter(0, [tile_ends], [], [], [])
 
     near_parts = [k for k in range(1, n_row) if k & (k + 1) == 0]
 
@@ -504,28 +536,26 @@
             got.append(lax.ppermute(parts[k], ("comp", "row"), route))
         return got
 
-    chain = [n_col + i for i in range(n_col - 1)]
-
     def to_columns(x):
-        return [
-            lax.ppermute(x, ("comp", "col"), [(i + 1, i) for i in chain]),
-            lax.ppermute(x, ("comp", "col"), [(i, i + 1) for i in chain]),
-        ]
-
-    coeffs = [traded(send[n_row * c:n_row * (c + 1)], f"there{c}") for c in range(chunks)]
+        near = [(i, i ^ 1) for i in range(n_col) if i ^ 1 < n_col]
+        far = [(i, j) for i in range(n_col) for j in [((i + 1) ^ 1) - 1] if 0 <= j < n_col]
+        ocean = [[(n_col + a, n_col + b) for a, b in pairs] for pairs in (near, far)]
+        return [lax.ppermute(x, ("comp", "col"), pairs) for pairs in ocean]
+
+    coeffs = [traded([send[c, k] for k in range(n_row)], f"there{c}") for c in range(chunks)]
     sides = to_columns(edge)
 
-    halves = 2 if rows % 16 == 0 else 1
-    share = rows // halves
-    whole = pl.BlockSpec((rows, lanes), lambda i, s: (0, 0))
+    pieces = (1, 3) if rows % 32 == 0 else (1,)
+    share = rows // sum(pieces)
     surfaces = []
 
-    def remap(half, after):
-        piece = pl.BlockSpec((share, lanes), lambda i, s: (half, 0))
+    def remap(index, after):
+        first = sum(pieces[:index])
+        piece = pl.BlockSpec((share, lanes), lambda i, s: (first + i, 0))
         earlier = surfaces[-1] if surfaces else ()
         surfaces.append(call(
-            functools.partial(surface_kernel, first=half * share, group=2), (1,),
-            [smem, whole, piece, piece] + [anywhere] * (len(earlier) + len(after)),
+            functools.partial(surface_kernel, first_piece=first, group=2), (pieces[index],),
+            [smem, vmem, piece, piece] + [anywhere] * (len(earlier) + len(after)),
             [piece] * 2, [sds((rows, lanes), f32)] * 2,
             (counts, partner, own, remap_source[0], *earlier, *after),
             aliases={5 + i: i for i in range(len(earlier))},
@@ -545,8 +575,7 @@
         return call(
             functools.partial(sweep_kernel, block=block, near_parts=near_parts, final=final),
             (1,),
-            [smem, anywhere, pl.BlockSpec(edge_shape, lambda i, s: (0, 0, 0)),
-             pl.BlockSpec(edge_shape, lambda i, s: (0, 0, 0))]
+            [smem, anywhere, vmem, vmem]
             + [pl.BlockSpec((1, levels, lanes), lambda i, s: (0, 0, 0))] * len(near_parts)
             + ([pl.BlockSpec((rows, lanes), lambda i, s: (0, 0))] if final else []),
             out_specs, out_shape,
@@ -568,13 +597,13 @@
             [anywhere] * n_row,
             [sds((width, rows, lanes), bf16)] * n_row,
             (legendre, *coeffs[chunk], *([ends, surfaces[0][1]] if with_ends else [])),
-            scratch=[pltpu.VMEM((n_row, rows, lanes), bf16)], vmem=63,
+            scratch=[pltpu.VMEM((n_row, rows, lanes), bf16), pltpu.SemaphoreType.DMA((n_row,))],
             flops=4 * width * legendre.shape[1] * legendre.shape[2] * lanes,
             size=2 * width * legendre.shape[1] * legendre.shape[2],
         )
         returned.append(traded(part, f"back{chunk}"))
 
-    if halves > 1:
+    if len(pieces) > 1:
         remap(1, (first_step,))
     new_surface, gap = surfaces[-1]
     (sea,) = sweep(first_step, returned[0], sides, True, (gap,))

time: 88.1 us -> 92.5 us (1.050)
  Pallas kernels: 47.1 us -> 50.2 us
  starting transfers between devices: 14 us -> 16.6 us
  local copies, waits for them, and re-layouts: 2.33 us -> 0.01 us
    pallas_call x8 -> x9, Pallas kernels: 47.1 us -> 50.2 us  [call(): pl.pallas_call(functools.partial(kernel, n_row=n_row, n_col=n_col), out_s...]
    ppermute x4, starting transfers between devices: 2.63 us -> 5.08 us  [to_columns(): return [lax.ppermute(x, ('comp', 'col'), pairs) for pairs in ocean]]
    unnamed x30 -> x4, local copies, waits for them, and re-layouts: 2.33 us -> 0.01 us
    ppermute x12, waiting for transfers between devices: 23.5 us -> 24.4 us  [traded(): got.append(lax.ppermute(parts[k], ('comp', 'row'), route))]
  transfers between devices with their start and end apart: 17 -> 17, of which waited for: 4 -> 4; matrix products, arithmetic and copies ran while one was open for 0% -> 0% of each run, Pallas kernels for 49% -> 50%
where the time goes in v7:
time: 92.5 us; the launch traced here: 92 us
  Pallas kernels  50.2 us (54%)
  waiting for transfers between devices  24.4 us (26%)
  starting transfers between devices  16.6 us (18%)
    pallas_call x9, Pallas kernels, call(): pl.pallas_call(functools.partial(kernel, n_row=n_row, n_col=n_col), out_s...  50.2 us
    ppermute x12, waiting for transfers between devices, traded(): got.append(lax.ppermute(parts[k], ('comp', 'row'), route))  24.4 us
    ppermute x12, starting transfers between devices, traded(): got.append(lax.ppermute(parts[k], ('comp', 'row'), route))  8.46 us
    ppermute x4, starting transfers between devices, to_columns(): return [lax.ppermute(x, ('comp', 'col'), pairs) for pairs in ocean]  5.08 us
    ppermute x1, starting transfers between devices, shards(): lax.ppermute(own, 'comp', [(i, comp_size - 1 - i) for i in range(comp_siz...  3.03 us
  transfers between devices with their start and end apart: 17, of which 4 were waited for; matrix products, arithmetic and copies ran while one was open for 0% of the time, Pallas kernels for 50%

profile of v7, /device:TPU:0, one launch (start us, length us, event | category | flops | bytes accessed | tf_op | source)
XLA Modules:
  0.0 92.0 jit_solution(17436205467082784369)
XLA Ops:
  0.6 3.0 %collective-permute-start.7 = (f32[320,128]{1,0:T(8,128)}, f32[320,128]{1,0:T(8,128)}, u32[]{:S(2)}, u32[]{:S(2)}) collective-permute-start(f32[320,128]{1,0:T(8,128)} %bitcast.19), channel_id=1, source_target_pairs={{0,16},{16,0},{1,17},{17,1},{2,18},{18,2},{3,19},{19,3},{4,20},{20... | collective-permute-start | bytes 491528 | tf_op jit(solution)/shard_map/ppermute | solution.py:482
  3.7 4.6 %shard_map.86 = (bf16[4,320,128]{2,1,0:T(8,128)(2,1)}, bf16[4,320,128]{2,1,0:T(8,128)(2,1)}, bf16[4,320,128]{2,1,0:T(8,128)(2,1)}, bf16[4,320,128]{2,1,0:T(8,128...) custom-call(s32[1]{0:T(128)} %bitcast.place, s32[1,320]{1,0:T(1,128)} %bitcast.13, ...), custom_call_target="tpu_custom_call" | custom-call | flops 10000000 | bytes 5242880 | tf_op jit(solution)/shard_map/pallas_call | solution.py:487
  8.3 1.3 %collective-permute-start = (bf16[5,32,128]{2,1,0:T(8,128)(2,1)}, bf16[5,32,128]{2,1,0:T(8,128)(2,1)}, u32[]{:S(2)}, u32[]{:S(2)}) collective-permute-start(bf16[5,32,128]{2,1,0:T(8,128)(2,1)} %get-tuple-element.29.rest_0_), channel_id=1, source_target_pairs={{16,17},{17,16},{18,19},{19,18},{20,21},{21,20},{22,23},{23,22},{2... | collective-permute-start | bytes 122888 | tf_op jit(solution)/shard_map/ppermute | solution.py:543
  9.6 1.3 %collective-permute-start.1 = (bf16[5,32,128]{2,1,0:T(8,128)(2,1)}, bf16[5,32,128]{2,1,0:T(8,128)(2,1)}, u32[]{:S(2)}, u32[]{:S(2)}) collective-permute-start(bf16[5,32,128]{2,1,0:T(8,128)(2,1)} %get-tuple-element.29.rest_0_), channel_id=1, source_target_pairs={{17,18},{18,17},{21,22},{22,21},{25,26},{26,25},{29,30},{30,29}} | collective-permute-start | bytes 122888 | tf_op jit(solution)/shard_map/ppermute | solution.py:543
  10.8 4.0 %shard_map.87 = (bf16[4,320,128]{2,1,0:T(8,128)(2,1)}, bf16[4,320,128]{2,1,0:T(8,128)(2,1)}, bf16[4,320,128]{2,1,0:T(8,128)(2,1)}, bf16[4,320,128]{2,1,0:T(8,128)(2,1)}) custom-call(s32[1]{0:T(128)} %bitcast.place, s32[1,320]{1,0:T(1,128)} %bitcast.14, f32[10240,128]{1,0:T(8,128)} %bitcast.10, f32[320,2,16,128]{3,2,1,0:T(8,128)} %bitcast.11, f32[320]{0:T(512)} %gauss.3, ...), custom_call_target="tpu_custom_call" | custom-call | flops 10000000 | bytes 5242880 | tf_op jit(solution)/shard_map/pallas_call | solution.py:487
  14.9 1.6 %collective-permute-start.3 = (bf16[4,320,128]{2,1,0:T(8,128)(2,1)}, bf16[4,320,128]{2,1,0:T(8,128)(2,1)}, u32[]{:S(2)}, u32[]{:S(2)}) collective-permute-start(bf16[4,320,128]{2,1,0:T(8,128)(2,1)} %get-tuple-element.32), channel_id=1, source_target_pairs={{0,12},{4,8},{8,4},{12,0},{16,28},{20,24},{24,20},{28,16},{1,13},{... | collective-permute-start | bytes 983048 | tf_op jit(solution)/shard_map/ppermute | solution.py:536
  16.6 0.5 collective-permute-start.6
  17.1 4.4 %shard_map.89 = (f32[320,128]{1,0:T(8,128)}, f32[320,128]{1,0:T(8,128)}) custom-call(s32[1]{0:T(128)} %bitcast.place, s32[1,320]{1,0:T(1,128)} %bitcast.15, f32[320,128]{1,0:T(8,128)} %collective-permute-done.7.partner, f32[320,128]{1,0:T(8,128)} %bitcast.20, s32[320,128]{1,0:T(8,128)} %bitcast.22, bf16[5,32,128]{2,1,0:T(8,128)(2,1)} %get-tuple-element.29.rest_0_), custom_call_target="tpu_custom_call" | custom-call | flops 10000000000 | bytes 491520 | tf_op jit(solution)/shard_map/pallas_call | solution.py:487
  21.4 1.6 %collective-permute-start.12 = (bf16[4,320,128]{2,1,0:T(8,128)(2,1)}, bf16[4,320,128]{2,1,0:T(8,128)(2,1)}, u32[]{:S(2)}, u32[]{:S(2)}) collective-permute-start(bf16[4,320,128]{2,1,0:T(8,128)(2,1)} %get-tuple-element.47), channel_id=1, source_target_pairs={{0,8},{4,12},{8,0},{12,4},{16,20},{20,16},{24,28},{28,24},{1,9},{5... | collective-permute-start | bytes 983048 | tf_op jit(solution)/shard_map/ppermute | solution.py:536
  23.3 1.7 %collective-permute-done.3.rest_1_.rest_3_ = bf16[4,320,128]{2,1,0:T(8,128)(2,1)} collective-permute-done((bf16[4,320,128]{2,1,0:T(8,128)(2,1)}, bf16[4,320,128]{2,1,0:T(8,128)(2,1)}, u32[]{:S(2)}, u32[]{:S(2)}) %collective-permute-start.3) | collective-permute-done | bytes 327712 | tf_op jit(solution)/shard_map/ppermute | solution.py:536
  25.0 1.5 %shard_map.88 = (f32[10240,128]{1,0:T(8,128)}, bf16[5,32,128]{2,1,0:T(8,128)(2,1)}, bf16[2,32,128]{2,1,0:T(8,128)(2,1)}) custom-call(s32[1]{0:T(128)} %bitcast.place, s32[1,320]{1,0:T(1,128)} %bitcast.16, f32[10240,128]{1,0:T(8,128)} %get-tuple-element.28.field, bf16[5,32,128]{2,1,0:T(8,128)(2,1)} %collective-permute-done.near_in, ...), custom_call_target="tpu_custom_call" | custom-call | flops 10000000 | bytes 10485760 | tf_op jit(solution)/shard_map/pallas_call | solution.py:487
  26.4 6.5 %collective-permute-done.6.rest_2_ = bf16[4,320,128]{2,1,0:T(8,128)(2,1)} collective-permute-done((bf16[4,320,128]{2,1,0:T(8,128)(2,1)}, bf16[4,320,128]{2,1,0:T(8,128)(2,1)}, u32[]{:S(2)}, u32[]{:S(2)}) %collective-permute-start.6) | collective-permute-done | bytes 327712 | tf_op jit(solution)/shard_map/ppermute | solution.py:536
  33.0 10.6 %shard_map.90 = (bf16[4,320,128]{2,1,0:T(8,128)(2,1)}, bf16[4,320,128]{2,1,0:T(8,128)(2,1)}, bf16[4,320,128]{2,1,0:T(8,128)(2,1)}, bf16[4,320,128]{2,1,0:T(8,128)(2,1)}) custom-call(s32[1]{0:T(128)} %bitcast.place, bf16[8,1280,1280]{2,1,0:T(8,128)(2,1)} %legendre.3, bf16[4,320,128]{2,1,0:T(8,128)(2,1)} %get-tuple-element.35.rest_0_, ...), custom_call_target="tpu_custom_call" | custom-call | flops 3355443200 | bytes 13107200 | tf_op jit(solution)/shard_map/pallas_call | solution.py:487
  43.6 1.3 %collective-permute-start.4 = (bf16[5,32,128]{2,1,0:T(8,128)(2,1)}, bf16[5,32,128]{2,1,0:T(8,128)(2,1)}, u32[]{:S(2)}, u32[]{:S(2)}) collective-permute-start(bf16[5,32,128]{2,1,0:T(8,128)(2,1)} %get-tuple-element.34), channel_id=1, source_target_pairs={{16,17},{17,16},{18,19},{19,18},{20,21},{21,20},{22,23},{23,22},{2... | collective-permute-start | bytes 122888 | tf_op jit(solution)/shard_map/ppermute | solution.py:543
  44.9 1.3 %collective-permute-start.5 = (bf16[5,32,128]{2,1,0:T(8,128)(2,1)}, bf16[5,32,128]{2,1,0:T(8,128)(2,1)}, u32[]{:S(2)}, u32[]{:S(2)}) collective-permute-start(bf16[5,32,128]{2,1,0:T(8,128)(2,1)} %get-tuple-element.34), channel_id=1, source_target_pairs={{17,18},{18,17},{21,22},{22,21},{25,26},{26,25},{29,30},{30,29}} | collective-permute-start | bytes 122888 | tf_op jit(solution)/shard_map/ppermute | solution.py:543
  46.1 9.9 %shard_map.93 = (bf16[4,320,128]{2,1,0:T(8,128)(2,1)}, bf16[4,320,128]{2,1,0:T(8,128)(2,1)}, bf16[4,320,128]{2,1,0:T(8,128)(2,1)}, bf16[4,320,128]{2,1,0:T(8,128)(2,1)}) custom-call(s32[1]{0:T(128)} %bitcast.place, bf16[8,1280,1280]{2,1,0:T(8,128)(2,1)} %legendre.3, bf16[4,320,128]{2,1,0:T(8,128)(2,1)} %get-tuple-element.45.rest_0_, ...), custom_call_target="tpu_custom_call" | custom-call | flops 3355443200 | bytes 13107200 | tf_op jit(solution)/shard_map/pallas_call | solution.py:487
  56.1 0.6 collective-permute-start.14
  56.6 1.6 %collective-permute-start.15 = (bf16[4,320,128]{2,1,0:T(8,128)(2,1)}, bf16[4,320,128]{2,1,0:T(8,128)(2,1)}, u32[]{:S(2)}, u32[]{:S(2)}) collective-permute-start(bf16[4,320,128]{2,1,0:T(8,128)(2,1)} %get-tuple-element.51), channel_id=1, source_target_pairs={{0,8},{4,12},{8,0},{12,4},{16,20},{20,16},{24,28},{28,24},{1,9},{5... | collective-permute-start | bytes 983048 | tf_op jit(solution)/shard_map/ppermute | solution.py:536
  58.2 1.7 %collective-permute-start.9 = (bf16[4,320,128]{2,1,0:T(8,128)(2,1)}, bf16[4,320,128]{2,1,0:T(8,128)(2,1)}, u32[]{:S(2)}, u32[]{:S(2)}) collective-permute-start(bf16[4,320,128]{2,1,0:T(8,128)(2,1)} %get-tuple-element.40), channel_id=1, source_target_pairs={{0,12},{4,8},{8,4},{12,0},{16,28},{20,24},{24,20},{28,16},{1,13},{... | collective-permute-start | bytes 983048 | tf_op jit(solution)/shard_map/ppermute | solution.py:536
  60.4 10.0 %shard_map.91 = (f32[320,128]{1,0:T(8,128)}, f32[320,128]{1,0:T(8,128)}) custom-call(s32[1]{0:T(128)} %bitcast.place, s32[1,320]{1,0:T(1,128)} %bitcast.17, f32[320,128]{1,0:T(8,128)} %collective-permute-done.7.partner, f32[320,128]{1,0:T(8,128)} %bitcast.21, s32[320,128]{1,0:T(8,128)} %bitcast.23, ...), custom_call_target="tpu_custom_call", output_to_operand_aliasing={{0}: (5, {}), {1}: (6, {})} | custom-call | flops 10000000000 | bytes 491520 | tf_op jit(solution)/shard_map/pallas_call | solution.py:487
  70.4 10.3 %collective-permute-done.9.rest_1_.rest_3_ = bf16[4,320,128]{2,1,0:T(8,128)(2,1)} collective-permute-done((bf16[4,320,128]{2,1,0:T(8,128)(2,1)}, bf16[4,320,128]{2,1,0:T(8,128)(2,1)}, u32[]{:S(2)}, u32[]{:S(2)}) %collective-permute-start.9) | collective-permute-done | bytes 327712 | tf_op jit(solution)/shard_map/ppermute | solution.py:536
  80.7 1.0 %shard_map.92.sea = f32[10240,128]{1,0:T(8,128)} custom-call(s32[1]{0:T(128)} %bitcast.place, s32[1,320]{1,0:T(1,128)} %bitcast.18, f32[10240,128]{1,0:T(8,128)} %get-tuple-element.33.rest_2_.field, bf16[5,32,128]{2,1,0:T(8,128)(2,1)} %collective-permute-done.4.near_in, bf16[5,32,128]{2,1,0:T(8,128)(2,1)} %collective-permute-done.5.far_in, ...), custom_call_target="tpu_custom_call" | custom-call | flops 10000000 | bytes 10485760 | tf_op jit(solution)/shard_map/pallas_call | solution.py:487
  81.7 6.0 %collective-permute-done.10.rest_2_ = bf16[4,320,128]{2,1,0:T(8,128)(2,1)} collective-permute-done((bf16[4,320,128]{2,1,0:T(8,128)(2,1)}, bf16[4,320,128]{2,1,0:T(8,128)(2,1)}, u32[]{:S(2)}, u32[]{:S(2)}) %collective-permute-start.10) | collective-permute-done | bytes 327712 | tf_op jit(solution)/shard_map/ppermute | solution.py:536
  87.7 4.3 %shard_map.94 = f32[10240,128]{1,0:T(8,128)} custom-call(s32[1]{0:T(128)} %bitcast.place, f32[10240,128]{1,0:T(8,128)} %shard_map.92.sea, bf16[4,320,128]{2,1,0:T(8,128)(2,1)} %get-tuple-element.43.rest_0_, bf16[4,320,128]{2,1,0:T(8,128)(2,1)} %copy-done, bf16[4,320,128]{2,1,0:T(8,128)(2,1)} %collective-permute-done.10.rest_2_, ...), custom_call_target="tpu_custom_call", output_to_operand_aliasing={{}: (1, {})} | custom-call | flops 10000000 | bytes 10485760 | tf_op jit(solution)/shard_map/pallas_call | solution.py:487
  (23 shorter events, 0.9 us)
Async XLA Ops:
  0.6 15.9 %collective-permute-start.7 = (f32[320,128]{1,0:T(8,128)}, f32[320,128]{1,0:T(8,128)}, u32[]{:S(2)}, u32[]{:S(2)}) collective-permute-start(f32[320,128]{1,0:T(8,128)} %bitcast.19), channel_id=1, source_target_pairs={{0,16},{16,0},{1,17},{17,1},{2,18},{18,2},{3,19},{19,3},{4,20},{20... | collective-permute-start | bytes 491528 | tf_op jit(solution)/shard_map/ppermute | solution.py:482
  8.3 13.1 %collective-permute-start = (bf16[5,32,128]{2,1,0:T(8,128)(2,1)}, bf16[5,32,128]{2,1,0:T(8,128)(2,1)}, u32[]{:S(2)}, u32[]{:S(2)}) collective-permute-start(bf16[5,32,128]{2,1,0:T(8,128)(2,1)} %get-tuple-element.29.rest_0_), channel_id=1, source_target_pairs={{16,17},{17,16},{18,19},{19,18},{20,21},{21,20},{22,23},{23,22},{2... | collective-permute-start | bytes 122888 | tf_op jit(solution)/shard_map/ppermute | solution.py:543
  9.6 11.9 %collective-permute-start.1 = (bf16[5,32,128]{2,1,0:T(8,128)(2,1)}, bf16[5,32,128]{2,1,0:T(8,128)(2,1)}, u32[]{:S(2)}, u32[]{:S(2)}) collective-permute-start(bf16[5,32,128]{2,1,0:T(8,128)(2,1)} %get-tuple-element.29.rest_0_), channel_id=1, source_target_pairs={{17,18},{18,17},{21,22},{22,21},{25,26},{26,25},{29,30},{30,29}} | collective-permute-start | bytes 122888 | tf_op jit(solution)/shard_map/ppermute | solution.py:543
  14.9 8.2 %collective-permute-start.2 = (bf16[4,320,128]{2,1,0:T(8,128)(2,1)}, bf16[4,320,128]{2,1,0:T(8,128)(2,1)S(1)}, u32[]{:S(2)}, u32[]{:S(2)}) collective-permute-start(bf16[4,320,128]{2,1,0:T(8,128)(2,1)} %get-tuple-element.31), channel_id=1, source_target_pairs={{0,4},{4,0},{8,12},{12,8},{16,20},{20,16},{24,28},{28,24},{1,5},{5... | collective-permute-start | bytes 983048 | tf_op jit(solution)/shard_map/ppermute | solution.py:536
  14.9 10.0 %collective-permute-start.3 = (bf16[4,320,128]{2,1,0:T(8,128)(2,1)}, bf16[4,320,128]{2,1,0:T(8,128)(2,1)}, u32[]{:S(2)}, u32[]{:S(2)}) collective-permute-start(bf16[4,320,128]{2,1,0:T(8,128)(2,1)} %get-tuple-element.32), channel_id=1, source_target_pairs={{0,12},{4,8},{8,4},{12,0},{16,28},{20,24},{24,20},{28,16},{1,13},{... | collective-permute-start | bytes 983048 | tf_op jit(solution)/shard_map/ppermute | solution.py:536
  16.6 16.4 %collective-permute-start.6 = (bf16[4,320,128]{2,1,0:T(8,128)(2,1)}, bf16[4,320,128]{2,1,0:T(8,128)(2,1)}, u32[]{:S(2)}, u32[]{:S(2)}) collective-permute-start(bf16[4,320,128]{2,1,0:T(8,128)(2,1)} %get-tuple-element.36), channel_id=1, source_target_pairs={{0,8},{4,12},{8,0},{12,4},{16,20},{20,16},{24,28},{28,24},{1,9},{5... | collective-permute-start | bytes 983048 | tf_op jit(solution)/shard_map/ppermute | solution.py:536
  21.4 23.4 %collective-permute-start.11 = (bf16[4,320,128]{2,1,0:T(8,128)(2,1)}, bf16[4,320,128]{2,1,0:T(8,128)(2,1)}, u32[]{:S(2)}, u32[]{:S(2)}) collective-permute-start(bf16[4,320,128]{2,1,0:T(8,128)(2,1)} %get-tuple-element.46), channel_id=1, source_target_pairs={{0,4},{4,0},{8,12},{12,8},{16,20},{20,16},{24,28},{28,24},{1,5},{5... | collective-permute-start | bytes 983048 | tf_op jit(solution)/shard_map/ppermute | solution.py:536
  21.4 24.7 %collective-permute-start.12 = (bf16[4,320,128]{2,1,0:T(8,128)(2,1)}, bf16[4,320,128]{2,1,0:T(8,128)(2,1)}, u32[]{:S(2)}, u32[]{:S(2)}) collective-permute-start(bf16[4,320,128]{2,1,0:T(8,128)(2,1)} %get-tuple-element.47), channel_id=1, source_target_pairs={{0,8},{4,12},{8,0},{12,4},{16,20},{20,16},{24,28},{28,24},{1,9},{5... | collective-permute-start | bytes 983048 | tf_op jit(solution)/shard_map/ppermute | solution.py:536
  23.0 1.9 %copy-start.1 = (bf16[4,320,128]{2,1,0:T(8,128)(2,1)}, bf16[4,320,128]{2,1,0:T(8,128)(2,1)S(1)}, u32[]{:S(2)}) copy-start(bf16[4,320,128]{2,1,0:T(8,128)(2,1)S(1)} %collective-permute-done.2.rest_0_.rest_1_) | copy-start | bytes 983044
  23.0 23.1 %collective-permute-start.13 = (bf16[4,320,128]{2,1,0:T(8,128)(2,1)}, bf16[4,320,128]{2,1,0:T(8,128)(2,1)}, u32[]{:S(2)}, u32[]{:S(2)}) collective-permute-start(bf16[4,320,128]{2,1,0:T(8,128)(2,1)} %get-tuple-element.48), channel_id=1, source_target_pairs={{0,12},{4,8},{8,4},{12,0},{16,20},{20,16},{24,28},{28,24},{1,13},{... | collective-permute-start | bytes 983048 | tf_op jit(solution)/shard_map/ppermute | solution.py:536
  43.5 16.5 %collective-permute-start.8 = (bf16[4,320,128]{2,1,0:T(8,128)(2,1)}, bf16[4,320,128]{2,1,0:T(8,128)(2,1)S(1)}, u32[]{:S(2)}, u32[]{:S(2)}) collective-permute-start(bf16[4,320,128]{2,1,0:T(8,128)(2,1)} %get-tuple-element.39), channel_id=1, source_target_pairs={{0,4},{4,0},{8,12},{12,8},{16,20},{20,16},{24,28},{28,24},{1,5},{5... | collective-permute-start | bytes 983048 | tf_op jit(solution)/shard_map/ppermute | solution.py:536
  43.6 14.6 %collective-permute-start.4 = (bf16[5,32,128]{2,1,0:T(8,128)(2,1)}, bf16[5,32,128]{2,1,0:T(8,128)(2,1)}, u32[]{:S(2)}, u32[]{:S(2)}) collective-permute-start(bf16[5,32,128]{2,1,0:T(8,128)(2,1)} %get-tuple-element.34), channel_id=1, source_target_pairs={{16,17},{17,16},{18,19},{19,18},{20,21},{21,20},{22,23},{23,22},{2... | collective-permute-start | bytes 122888 | tf_op jit(solution)/shard_map/ppermute | solution.py:543
  44.9 13.4 %collective-permute-start.5 = (bf16[5,32,128]{2,1,0:T(8,128)(2,1)}, bf16[5,32,128]{2,1,0:T(8,128)(2,1)}, u32[]{:S(2)}, u32[]{:S(2)}) collective-permute-start(bf16[5,32,128]{2,1,0:T(8,128)(2,1)} %get-tuple-element.34), channel_id=1, source_target_pairs={{17,18},{18,17},{21,22},{22,21},{25,26},{26,25},{29,30},{30,29}} | collective-permute-start | bytes 122888 | tf_op jit(solution)/shard_map/ppermute | solution.py:543
  56.1 25.7 %collective-permute-start.14 = (bf16[4,320,128]{2,1,0:T(8,128)(2,1)}, bf16[4,320,128]{2,1,0:T(8,128)(2,1)}, u32[]{:S(2)}, u32[]{:S(2)}) collective-permute-start(bf16[4,320,128]{2,1,0:T(8,128)(2,1)} %get-tuple-element.50), channel_id=1, source_target_pairs={{0,4},{4,0},{8,12},{12,8},{16,20},{20,16},{24,28},{28,24},{1,5},{5... | collective-permute-start | bytes 983048 | tf_op jit(solution)/shard_map/ppermute | solution.py:536
  56.6 25.1 %collective-permute-start.15 = (bf16[4,320,128]{2,1,0:T(8,128)(2,1)}, bf16[4,320,128]{2,1,0:T(8,128)(2,1)}, u32[]{:S(2)}, u32[]{:S(2)}) collective-permute-start(bf16[4,320,128]{2,1,0:T(8,128)(2,1)} %get-tuple-element.51), channel_id=1, source_target_pairs={{0,8},{4,12},{8,0},{12,4},{16,20},{20,16},{24,28},{28,24},{1,9},{5... | collective-permute-start | bytes 983048 | tf_op jit(solution)/shard_map/ppermute | solution.py:536
  58.2 23.5 %collective-permute-start.16 = (bf16[4,320,128]{2,1,0:T(8,128)(2,1)}, bf16[4,320,128]{2,1,0:T(8,128)(2,1)}, u32[]{:S(2)}, u32[]{:S(2)}) collective-permute-start(bf16[4,320,128]{2,1,0:T(8,128)(2,1)} %get-tuple-element.52), channel_id=1, source_target_pairs={{0,12},{4,8},{8,4},{12,0},{16,20},{20,16},{24,28},{28,24},{1,13},{... | collective-permute-start | bytes 983048 | tf_op jit(solution)/shard_map/ppermute | solution.py:536
  58.2 22.4 %collective-permute-start.9 = (bf16[4,320,128]{2,1,0:T(8,128)(2,1)}, bf16[4,320,128]{2,1,0:T(8,128)(2,1)}, u32[]{:S(2)}, u32[]{:S(2)}) collective-permute-start(bf16[4,320,128]{2,1,0:T(8,128)(2,1)} %get-tuple-element.40), channel_id=1, source_target_pairs={{0,12},{4,8},{8,4},{12,0},{16,28},{20,24},{24,20},{28,16},{1,13},{... | collective-permute-start | bytes 983048 | tf_op jit(solution)/shard_map/ppermute | solution.py:536
  60.0 10.4 %copy-start = (bf16[4,320,128]{2,1,0:T(8,128)(2,1)}, bf16[4,320,128]{2,1,0:T(8,128)(2,1)S(1)}, u32[]{:S(2)}) copy-start(bf16[4,320,128]{2,1,0:T(8,128)(2,1)S(1)} %collective-permute-done.8.rest_0_.rest_1_) | copy-start | bytes 983044
  60.0 27.7 %collective-permute-start.10 = (bf16[4,320,128]{2,1,0:T(8,128)(2,1)}, bf16[4,320,128]{2,1,0:T(8,128)(2,1)}, u32[]{:S(2)}, u32[]{:S(2)}) collective-permute-start(bf16[4,320,128]{2,1,0:T(8,128)(2,1)} %get-tuple-element.44), channel_id=1, source_target_pairs={{0,8},{4,12},{8,0},{12,4},{16,20},{20,16},{24,28},{28,24},{1,9},{5... | collective-permute-start | bytes 983048 | tf_op jit(solution)/shard_map/ppermute | solution.py:536

commit v8 on v7

--- a/solution.py
+++ b/solution.py
@@ -230,7 +230,7 @@
     packed[slot] = kept
 
 
-def sweep_kernel(place, counts, field, near_in, far_in, *rest, block, n_row, n_col, near_parts, final):
+def sweep_kernel(place, counts, field, east_in, west_in, *rest, block, n_row, n_col, near_parts, final):
     halos, rest = rest[:len(near_parts)], rest[len(near_parts):]
     if final:
         gap, out, masked, sides = rest
@@ -263,10 +263,8 @@
             return found
 
         for slot in range(sides.shape[0]):
-            near, far = near_in[slot].astype(jnp.float32), far_in[slot].astype(jnp.float32)
-            east_is_near = (col & 1) == 0
-            west = jnp.where(col > 0, jnp.where(east_is_near, far, near), 0.0)
-            east = jnp.where(col < n_col - 1, jnp.where(east_is_near, near, far), 0.0)
+            west = jnp.where(col > 0, west_in[slot].astype(jnp.float32), 0.0)
+            east = jnp.where(col < n_col - 1, east_in[slot].astype(jnp.float32), 0.0)
             sides[slot] = jnp.where((lane & 1) == 0, pltpu.roll(east, lanes - 1, 1), pltpu.roll(west, 1, 1))
         if not final:
             packed[...] = jnp.zeros_like(packed)
@@ -422,45 +420,43 @@
     lax.fori_loop(0, source.shape[0] // 8, body, 0)
 
 
-def exit_kernel(place, sea, *rest, n_row, n_col, widths, block):
+def exit_kernel(place, state, *rest, n_row, n_col, widths, block, half):
     chunks = len(widths)
-    back, (out, table) = rest[:n_row * chunks], rest[n_row * chunks:]
+    wave_dev = sum(widths)
+    mine = parts_of_half(half, n_row, wave_dev)
+    back, (out, table) = rest[:len(mine) * chunks], rest[len(mine) * chunks:]
     comp, row, _ = where_am_i(place, n_row, n_col)
-    levels = sum(widths) * n_row
-    wave_dev = levels // n_row
     flip = row * wave_dev
-    tall = block * levels
 
     def turn(*refs):
         parts, out = refs[:-1], refs[-1]
 
-        def source(wave, lat, count):
-            part, local = divmod(wave, wave_dev)
+        def source(wave, lat, size):
+            part, local = divmod(16 * half + wave, wave_dev)
             chunk, slot = chunk_of(local, widths)
-            return parts[n_row * chunk + part][slot, lat:lat + count, :]
-
-        for lat in range(0, block - 15, 16):
-            halves = [
-                jnp.concatenate([source(half + wave, lat, 16) for wave in range(16)], axis=0)
-                for half in range(0, levels, 16)
-            ]
-            turned = product(table[...], jnp.concatenate(halves, axis=1))
-            for s in range(16):
-                for half in range(0, levels, 16):
-                    start = pl.multiple_of((lat + s) * levels + (half ^ (flip & ~15)), 16)
-                    part = lanes * (half // 16)
-                    out[pl.ds(start, 16), :] = turned[16 * s:16 * s + 16, part:part + lanes]
-        for lat in range(block - block % 16, block, 8):
-            for wave in range(levels):
-                out[pl.ds(lat * levels + (wave ^ flip), 8, stride=levels), :] = source(wave, lat, 8).astype(jnp.float32)
+            return parts[len(mine) * chunk + mine.index(part)][slot, lat:lat + size, :]
+
+        for lat in range(0, block, 16):
+            size = min(16, block - lat)
+            rows = [source(wave, lat, size) for wave in range(16)]
+            if size == 16:
+                swap, rows = table[...], jnp.concatenate(rows, axis=0)
+            else:
+                shape = (16 * size, 16 * size)
+                line, column = iota(shape, 0), iota(shape, 1)
+                swap = as_bf16(column == ((line & 15) ^ (flip & 15)) * size + (line >> 4))
+                rows = jnp.concatenate([r.astype(jnp.float32) for r in rows], axis=0).astype(jnp.bfloat16)
+            turned = product(swap, rows)
+            for s in range(size):
+                out[lat + s] = turned[16 * s:16 * s + 16, :]
 
     @pl.when(comp == 0)
     def _():
         table[...] = swap_matrix(0, flip & 15)
         pltpu.emit_pipeline(
-            turn, grid=(out.shape[0] // tall,),
-            in_specs=[pl.BlockSpec((w, block, lanes), lambda i: (0, i, 0)) for w in widths for _ in range(n_row)],
-            out_specs=[pl.BlockSpec((tall, lanes), lambda i: (i, 0))],
+            turn, grid=(out.shape[0] // block,),
+            in_specs=[pl.BlockSpec((w, block, lanes), lambda i: (0, i, 0)) for w in widths for _ in mine],
+            out_specs=[pl.BlockSpec((block, pl.Squeezed(), 16, lanes), lambda i: (i, half ^ (flip >> 4), 0, 0))],
         )(*back, out)
 
 
@@ -483,7 +479,7 @@
 
     slots = pl.cdiv(rows, 64)
 
-    def call(kernel, grid, in_specs, out_specs, out_shape, args, scratch=(), vmem_limit=66700000, flops=10**7, size=0, aliases={}):
+    def call(kernel, grid, in_specs, out_specs, out_shape, args, scratch=(), vmem_limit=66800000, flops=10**7, size=0, aliases={}):
         return pl.pallas_call(
             functools.partial(kernel, n_row=n_row, n_col=n_col),
             out_shape=out_shape,
@@ -536,11 +532,13 @@
             got.append(lax.ppermute(parts[k], ("comp", "row"), route))
         return got
 
+    chain = [n_col + i for i in range(n_col - 1)]
+
     def to_columns(x):
-        near = [(i, i ^ 1) for i in range(n_col) if i ^ 1 < n_col]
-        far = [(i, j) for i in range(n_col) for j in [((i + 1) ^ 1) - 1] if 0 <= j < n_col]
-        ocean = [[(n_col + a, n_col + b) for a, b in pairs] for pairs in (near, far)]
-        return [lax.ppermute(x, ("comp", "col"), pairs) for pairs in ocean]
+        return [
+            lax.ppermute(x, ("comp", "col"), [(i + 1, i) for i in chain]),
+            lax.ppermute(x, ("comp", "col"), [(i, i + 1) for i in chain]),
+        ]
 
     coeffs = [traded([send[c, k] for k in range(n_row)], f"there{c}") for c in range(chunks)]
     sides = to_columns(edge)
@@ -608,11 +606,15 @@
     new_surface, gap = surfaces[-1]
     (sea,) = sweep(first_step, returned[0], sides, True, (gap,))
 
-    state = call(
-        functools.partial(exit_kernel, widths=widths, block=block), (),
-        [anywhere] * (1 + n_row * chunks), anywhere, sds((rows * levels, lanes), f32),
-        (sea, *sum(returned, [])), scratch=[pltpu.VMEM((256, 256), bf16)], size=2 * state_bytes, aliases={1: 0},
-    )
+    state = sea.reshape(rows, levels // 16, 16, lanes)
+    for half in range(2):
+        mine = parts_of_half(half, n_row, wave_dev)
+        state = call(
+            functools.partial(exit_kernel, widths=widths, block=block, half=half), (),
+            [anywhere] * (1 + len(mine) * chunks), anywhere, sds(state.shape, f32),
+            (state, *(returned[c][k] for c in range(chunks) for k in mine)),
+            scratch=[pltpu.VMEM((256, 256), bf16)], size=state_bytes, aliases={1: 0},
+        )
     return state.reshape(model_state.shape), new_surface[None]
 
 

time: 92.5 us -> 90.1 us (0.974)
  starting transfers between devices: 16.6 us -> 13.9 us
  Pallas kernels: 50.2 us -> 52.3 us
  waiting for transfers between devices: 24.4 us -> 22.5 us
    ppermute x4, starting transfers between devices: 5.08 us -> 2.65 us  [the longest x2 1.33 us: to_columns(): lax.ppermute(x, ('comp', 'col'), [(i + 1, i) for i in chain])]
    pallas_call x9 -> x10, Pallas kernels: 50.2 us -> 52.3 us  [call(): pl.pallas_call(functools.partial(kernel, n_row=n_row, n_col=n_col), out_s...]
    ppermute x12, waiting for transfers between devices: 24.4 us -> 22.5 us  [traded(): got.append(lax.ppermute(parts[k], ('comp', 'row'), route))]
  transfers between devices with their start and end apart: 17 -> 17, of which waited for: 4 -> 5; matrix products, arithmetic and copies ran while one was open for 0% -> 0% of each run, Pallas kernels for 50% -> 55%
where the time goes in v8:
time: 90.1 us; the launch traced here: 89.6 us
  Pallas kernels  52.3 us (58%)
  waiting for transfers between devices  22.5 us (25%)
  starting transfers between devices  13.9 us (15%)
    pallas_call x10, Pallas kernels, call(): pl.pallas_call(functools.partial(kernel, n_row=n_row, n_col=n_col), out_s...  52.3 us
    ppermute x12, waiting for transfers between devices, traded(): got.append(lax.ppermute(parts[k], ('comp', 'row'), route))  22.5 us
    ppermute x12, starting transfers between devices, traded(): got.append(lax.ppermute(parts[k], ('comp', 'row'), route))  8.19 us
    ppermute x1, starting transfers between devices, shards(): lax.ppermute(own, 'comp', [(i, comp_size - 1 - i) for i in range(comp_siz...  3.03 us
  transfers between devices with their start and end apart: 17, of which 5 were waited for; matrix products, arithmetic and copies ran while one was open for 0% of the time, Pallas kernels for 55%

profile of v8, /device:TPU:0, one launch (start us, length us, event | category | flops | bytes accessed | tf_op | source)
XLA Modules:
  0.0 89.6 jit_solution(11827103074936075552)
XLA Ops:
  0.6 3.0 %collective-permute-start.7 = (f32[320,128]{1,0:T(8,128)}, f32[320,128]{1,0:T(8,128)}, u32[]{:S(2)}, u32[]{:S(2)}) collective-permute-start(f32[320,128]{1,0:T(8,128)} %bitcast.21), channel_id=1, source_target_pairs={{0,16},{16,0},{1,17},{17,1},{2,18},{18,2},{3,19},{19,3},{4,20},{20... | collective-permute-start | bytes 491528 | tf_op jit(solution)/shard_map/ppermute | solution.py:478
  3.7 4.6 %shard_map.86 = (bf16[4,320,128]{2,1,0:T(8,128)(2,1)}, bf16[4,320,128]{2,1,0:T(8,128)(2,1)}, bf16[4,320,128]{2,1,0:T(8,128)(2,1)}, bf16[4,320,128]{2,1,0:T(8,128...) custom-call(s32[1]{0:T(128)} %bitcast.place, s32[1,320]{1,0:T(1,128)} %bitcast.15, ...), custom_call_target="tpu_custom_call" | custom-call | flops 10000000 | bytes 5242880 | tf_op jit(solution)/shard_map/pallas_call | solution.py:483
  8.3 0.7 collective-permute-start
  8.9 0.7 collective-permute-start.1
  9.6 4.0 %shard_map.87 = (bf16[4,320,128]{2,1,0:T(8,128)(2,1)}, bf16[4,320,128]{2,1,0:T(8,128)(2,1)}, bf16[4,320,128]{2,1,0:T(8,128)(2,1)}, bf16[4,320,128]{2,1,0:T(8,128)(2,1)}) custom-call(s32[1]{0:T(128)} %bitcast.place, s32[1,320]{1,0:T(1,128)} %bitcast.16, f32[10240,128]{1,0:T(8,128)} %bitcast.11, f32[320,2,16,128]{3,2,1,0:T(8,128)} %bitcast.12, f32[320]{0:T(512)} %gauss.3, ...), custom_call_target="tpu_custom_call" | custom-call | flops 10000000 | bytes 5242880 | tf_op jit(solution)/shard_map/pallas_call | solution.py:483
  13.7 1.6 %collective-permute-start.3 = (bf16[4,320,128]{2,1,0:T(8,128)(2,1)}, bf16[4,320,128]{2,1,0:T(8,128)(2,1)}, u32[]{:S(2)}, u32[]{:S(2)}) collective-permute-start(bf16[4,320,128]{2,1,0:T(8,128)(2,1)} %get-tuple-element.32), channel_id=1, source_target_pairs={{0,12},{4,8},{8,4},{12,0},{16,28},{20,24},{24,20},{28,16},{1,13},{... | collective-permute-start | bytes 983048 | tf_op jit(solution)/shard_map/ppermute | solution.py:532
  15.8 4.4 %shard_map.89 = (f32[320,128]{1,0:T(8,128)}, f32[320,128]{1,0:T(8,128)}) custom-call(s32[1]{0:T(128)} %bitcast.place, s32[1,320]{1,0:T(1,128)} %bitcast.17, f32[320,128]{1,0:T(8,128)} %collective-permute-done.7.partner, f32[320,128]{1,0:T(8,128)} %bitcast.22, s32[320,128]{1,0:T(8,128)} %bitcast.24, bf16[5,32,128]{2,1,0:T(8,128)(2,1)} %get-tuple-element.29.rest_0_), custom_call_target="tpu_custom_call" | custom-call | flops 10000000000 | bytes 491520 | tf_op jit(solution)/shard_map/pallas_call | solution.py:483
  20.3 1.6 %collective-permute-start.11 = (bf16[4,320,128]{2,1,0:T(8,128)(2,1)}, bf16[4,320,128]{2,1,0:T(8,128)(2,1)}, u32[]{:S(2)}, u32[]{:S(2)}) collective-permute-start(bf16[4,320,128]{2,1,0:T(8,128)(2,1)} %get-tuple-element.46), channel_id=1, source_target_pairs={{0,8},{4,12},{8,0},{12,4},{16,20},{20,16},{24,28},{28,24},{1,9},{5... | collective-permute-start | bytes 983048 | tf_op jit(solution)/shard_map/ppermute | solution.py:532
  22.1 1.6 %collective-permute-done.3.rest_1_.rest_3_ = bf16[4,320,128]{2,1,0:T(8,128)(2,1)} collective-permute-done((bf16[4,320,128]{2,1,0:T(8,128)(2,1)}, bf16[4,320,128]{2,1,0:T(8,128)(2,1)}, u32[]{:S(2)}, u32[]{:S(2)}) %collective-permute-start.3) | collective-permute-done | bytes 327712 | tf_op jit(solution)/shard_map/ppermute | solution.py:532
  23.7 1.5 %shard_map.88 = (f32[10240,128]{1,0:T(8,128)}, bf16[5,32,128]{2,1,0:T(8,128)(2,1)}, bf16[2,32,128]{2,1,0:T(8,128)(2,1)}) custom-call(s32[1]{0:T(128)} %bitcast.place, s32[1,320]{1,0:T(1,128)} %bitcast.18, f32[10240,128]{1,0:T(8,128)} %get-tuple-element.28.field, bf16[5,32,128]{2,1,0:T(8,128)(2,1)} %copy-done.2, bf16[5,32,128]{2,1,0:T(8,128)(2,1)} %copy-done.3, ...), custom_call_target="tpu_custom_call" | custom-call | flops 10000000 | bytes 10485760 | tf_op jit(solution)/shard_map/pallas_call | solution.py:483
  25.2 6.5 %collective-permute-done.6.rest_2_ = bf16[4,320,128]{2,1,0:T(8,128)(2,1)} collective-permute-done((bf16[4,320,128]{2,1,0:T(8,128)(2,1)}, bf16[4,320,128]{2,1,0:T(8,128)(2,1)}, u32[]{:S(2)}, u32[]{:S(2)}) %collective-permute-start.6) | collective-permute-done | bytes 327712 | tf_op jit(solution)/shard_map/ppermute | solution.py:532
  31.7 10.6 %shard_map.90 = (bf16[4,320,128]{2,1,0:T(8,128)(2,1)}, bf16[4,320,128]{2,1,0:T(8,128)(2,1)}, bf16[4,320,128]{2,1,0:T(8,128)(2,1)}, bf16[4,320,128]{2,1,0:T(8,128)(2,1)}) custom-call(s32[1]{0:T(128)} %bitcast.place, bf16[8,1280,1280]{2,1,0:T(8,128)(2,1)} %legendre.3, bf16[4,320,128]{2,1,0:T(8,128)(2,1)} %get-tuple-element.35.rest_0_, ...), custom_call_target="tpu_custom_call" | custom-call | flops 3355443200 | bytes 13107200 | tf_op jit(solution)/shard_map/pallas_call | solution.py:483
  42.4 0.7 collective-permute-start.4
  43.0 0.7 collective-permute-start.5
  43.7 0.8 collective-permute-done.12.rest_3_
  44.5 9.9 %shard_map.93 = (bf16[4,320,128]{2,1,0:T(8,128)(2,1)}, bf16[4,320,128]{2,1,0:T(8,128)(2,1)}, bf16[4,320,128]{2,1,0:T(8,128)(2,1)}, bf16[4,320,128]{2,1,0:T(8,128)(2,1)}) custom-call(s32[1]{0:T(128)} %bitcast.place, bf16[8,1280,1280]{2,1,0:T(8,128)(2,1)} %legendre.3, bf16[4,320,128]{2,1,0:T(8,128)(2,1)} %get-tuple-element.44.rest_0_, ...), custom_call_target="tpu_custom_call" | custom-call | flops 3355443200 | bytes 13107200 | tf_op jit(solution)/shard_map/pallas_call | solution.py:483
  54.9 1.3 %collective-permute-start.9 = (bf16[4,320,128]{2,1,0:T(8,128)(2,1)}, bf16[4,320,128]{2,1,0:T(8,128)(2,1)}, u32[]{:S(2)}, u32[]{:S(2)}) collective-permute-start(bf16[4,320,128]{2,1,0:T(8,128)(2,1)} %get-tuple-element.40), channel_id=1, source_target_pairs={{0,12},{4,8},{8,4},{12,0},{16,28},{20,24},{24,20},{28,16},{1,13},{... | collective-permute-start | bytes 983048 | tf_op jit(solution)/shard_map/ppermute | solution.py:532
  56.6 1.4 %collective-permute-start.16 = (bf16[4,320,128]{2,1,0:T(8,128)(2,1)}, bf16[4,320,128]{2,1,0:T(8,128)(2,1)}, u32[]{:S(2)}, u32[]{:S(2)}) collective-permute-start(bf16[4,320,128]{2,1,0:T(8,128)(2,1)} %get-tuple-element.52), channel_id=1, source_target_pairs={{0,12},{4,8},{8,4},{12,0},{16,20},{20,16},{24,28},{28,24},{1,13},{... | collective-permute-start | bytes 983048 | tf_op jit(solution)/shard_map/ppermute | solution.py:532
  58.4 10.0 %shard_map.91 = (f32[320,128]{1,0:T(8,128)}, f32[320,128]{1,0:T(8,128)}) custom-call(s32[1]{0:T(128)} %bitcast.place, s32[1,320]{1,0:T(1,128)} %bitcast.19, f32[320,128]{1,0:T(8,128)} %collective-permute-done.7.partner, f32[320,128]{1,0:T(8,128)} %bitcast.23, s32[320,128]{1,0:T(8,128)} %bitcast.25, ...), custom_call_target="tpu_custom_call", output_to_operand_aliasing={{0}: (5, {}), {1}: (6, {})} | custom-call | flops 10000000000 | bytes 491520 | tf_op jit(solution)/shard_map/pallas_call | solution.py:483
  68.4 1.0 %shard_map.92 = f32[10240,128]{1,0:T(8,128)} custom-call(s32[1]{0:T(128)} %bitcast.place, s32[1,320]{1,0:T(1,128)} %bitcast.20, f32[10240,128]{1,0:T(8,128)} %get-tuple-element.33.rest_2_.field, bf16[5,32,128]{2,1,0:T(8,128)(2,1)} %copy-done, bf16[5,32,128]{2,1,0:T(8,128)(2,1)} %copy-done.1, bf16[4,320,128]{2,1,0:T(8,128)(2,1)} %collective-permute-done.8.rest_0_.rest_1_, ...), custom_call_target="tpu_custom_call" | custom-call | flops 10000000 | bytes 10485760 | tf_op jit(solution)/shard_map/pallas_call | solution.py:483
  69.5 3.3 %shard_map.94.state = f32[320,2,16,128]{3,2,1,0:T(8,128)} custom-call(s32[1]{0:T(128)} %bitcast.place, f32[320,2,16,128]{3,2,1,0:T(8,128)} %bitcast.13, bf16[4,320,128]{2,1,0:T(8,128)(2,1)} %get-tuple-element.43.rest_0_, bf16[4,320,128]{2,1,0:T(8,128)(2,1)} %collective-permute-done.8.rest_0_.rest_1_, ...), custom_call_target="tpu_custom_call", output_to_operand_aliasing={{}: (1, {})} | custom-call | flops 10000000 | bytes 5242880 | tf_op jit(solution)/shard_map/pallas_call | solution.py:483
  72.8 6.3 %collective-permute-done.16.rest_3_ = bf16[4,320,128]{2,1,0:T(8,128)(2,1)} collective-permute-done((bf16[4,320,128]{2,1,0:T(8,128)(2,1)}, bf16[4,320,128]{2,1,0:T(8,128)(2,1)}, u32[]{:S(2)}, u32[]{:S(2)}) %collective-permute-start.16) | collective-permute-done | bytes 327712 | tf_op jit(solution)/shard_map/ppermute | solution.py:532
  79.0 7.3 %collective-permute-done.14.rest_0_ = bf16[4,320,128]{2,1,0:T(8,128)(2,1)} collective-permute-done((bf16[4,320,128]{2,1,0:T(8,128)(2,1)}, bf16[4,320,128]{2,1,0:T(8,128)(2,1)}, u32[]{:S(2)}, u32[]{:S(2)}) %collective-permute-start.14) | collective-permute-done | bytes 327712 | tf_op jit(solution)/shard_map/ppermute | solution.py:532
  86.3 3.2 %shard_map.95 = f32[320,2,16,128]{3,2,1,0:T(8,128)} custom-call(s32[1]{0:T(128)} %bitcast.place, f32[320,2,16,128]{3,2,1,0:T(8,128)} %shard_map.94.state, bf16[4,320,128]{2,1,0:T(8,128)(2,1)} %collective-permute-done.14.rest_0_, bf16[4,320,128]{2,1,0:T(8,128)(2,1)} %collective-permute-done.9.rest_1_, ...), custom_call_target="tpu_custom_call", output_to_operand_aliasing={{}: (1, {})} | custom-call | flops 10000000 | bytes 5242880 | tf_op jit(solution)/shard_map/pallas_call | solution.py:483
  (30 shorter events, 2.4 us)
Async XLA Ops:
  0.6 14.7 %collective-permute-start.7 = (f32[320,128]{1,0:T(8,128)}, f32[320,128]{1,0:T(8,128)}, u32[]{:S(2)}, u32[]{:S(2)}) collective-permute-start(f32[320,128]{1,0:T(8,128)} %bitcast.21), channel_id=1, source_target_pairs={{0,16},{16,0},{1,17},{17,1},{2,18},{18,2},{3,19},{19,3},{4,20},{20... | collective-permute-start | bytes 491528 | tf_op jit(solution)/shard_map/ppermute | solution.py:478
  8.3 11.9 %collective-permute-start = (bf16[5,32,128]{2,1,0:T(8,128)(2,1)}, bf16[5,32,128]{2,1,0:T(8,128)(2,1)S(1)}, u32[]{:S(2)}, u32[]{:S(2)}) collective-permute-start(bf16[5,32,128]{2,1,0:T(8,128)(2,1)} %get-tuple-element.29.rest_0_), channel_id=1, source_target_pairs={{17,16},{18,17},{19,18},{21,20},{22,21},{23,22},{25,24},{26,25},{2... | collective-permute-start | bytes 122888 | tf_op jit(solution)/shard_map/ppermute | solution.py:539
  8.9 11.3 %collective-permute-start.1 = (bf16[5,32,128]{2,1,0:T(8,128)(2,1)}, bf16[5,32,128]{2,1,0:T(8,128)(2,1)S(1)}, u32[]{:S(2)}, u32[]{:S(2)}) collective-permute-start(bf16[5,32,128]{2,1,0:T(8,128)(2,1)} %get-tuple-element.29.rest_0_), channel_id=1, source_target_pairs={{16,17},{17,18},{18,19},{20,21},{21,22},{22,23},{24,25},{25,26},{2... | collective-permute-start | bytes 122888 | tf_op jit(solution)/shard_map/ppermute | solution.py:540
  13.6 8.3 %collective-permute-start.2 = (bf16[4,320,128]{2,1,0:T(8,128)(2,1)}, bf16[4,320,128]{2,1,0:T(8,128)(2,1)}, u32[]{:S(2)}, u32[]{:S(2)}) collective-permute-start(bf16[4,320,128]{2,1,0:T(8,128)(2,1)} %get-tuple-element.31), channel_id=1, source_target_pairs={{0,4},{4,0},{8,12},{12,8},{16,20},{20,16},{24,28},{28,24},{1,5},{5... | collective-permute-start | bytes 983048 | tf_op jit(solution)/shard_map/ppermute | solution.py:532
  13.7 10.0 %collective-permute-start.3 = (bf16[4,320,128]{2,1,0:T(8,128)(2,1)}, bf16[4,320,128]{2,1,0:T(8,128)(2,1)}, u32[]{:S(2)}, u32[]{:S(2)}) collective-permute-start(bf16[4,320,128]{2,1,0:T(8,128)(2,1)} %get-tuple-element.32), channel_id=1, source_target_pairs={{0,12},{4,8},{8,4},{12,0},{16,28},{20,24},{24,20},{28,16},{1,13},{... | collective-permute-start | bytes 983048 | tf_op jit(solution)/shard_map/ppermute | solution.py:532
  15.3 16.4 %collective-permute-start.6 = (bf16[4,320,128]{2,1,0:T(8,128)(2,1)}, bf16[4,320,128]{2,1,0:T(8,128)(2,1)}, u32[]{:S(2)}, u32[]{:S(2)}) collective-permute-start(bf16[4,320,128]{2,1,0:T(8,128)(2,1)} %get-tuple-element.36), channel_id=1, source_target_pairs={{0,8},{4,12},{8,0},{12,4},{16,20},{20,16},{24,28},{28,24},{1,9},{5... | collective-permute-start | bytes 983048 | tf_op jit(solution)/shard_map/ppermute | solution.py:532
  20.2 3.5 %copy-start.2 = (bf16[5,32,128]{2,1,0:T(8,128)(2,1)}, bf16[5,32,128]{2,1,0:T(8,128)(2,1)S(1)}, u32[]{:S(2)}) copy-start(bf16[5,32,128]{2,1,0:T(8,128)(2,1)S(1)} %collective-permute-done.east_in) | copy-start | bytes 122884
  20.2 22.9 %collective-permute-start.10 = (bf16[4,320,128]{2,1,0:T(8,128)(2,1)}, bf16[4,320,128]{2,1,0:T(8,128)(2,1)}, u32[]{:S(2)}, u32[]{:S(2)}) collective-permute-start(bf16[4,320,128]{2,1,0:T(8,128)(2,1)} %get-tuple-element.45), channel_id=1, source_target_pairs={{0,4},{4,0},{8,12},{12,8},{16,20},{20,16},{24,28},{28,24},{1,5},{5... | collective-permute-start | bytes 983048 | tf_op jit(solution)/shard_map/ppermute | solution.py:532
  20.3 3.5 %copy-start.3 = (bf16[5,32,128]{2,1,0:T(8,128)(2,1)}, bf16[5,32,128]{2,1,0:T(8,128)(2,1)S(1)}, u32[]{:S(2)}) copy-start(bf16[5,32,128]{2,1,0:T(8,128)(2,1)S(1)} %collective-permute-done.1.west_in) | copy-start | bytes 122884
  20.3 23.4 %collective-permute-start.11 = (bf16[4,320,128]{2,1,0:T(8,128)(2,1)}, bf16[4,320,128]{2,1,0:T(8,128)(2,1)}, u32[]{:S(2)}, u32[]{:S(2)}) collective-permute-start(bf16[4,320,128]{2,1,0:T(8,128)(2,1)} %get-tuple-element.46), channel_id=1, source_target_pairs={{0,8},{4,12},{8,0},{12,4},{16,20},{20,16},{24,28},{28,24},{1,9},{5... | collective-permute-start | bytes 983048 | tf_op jit(solution)/shard_map/ppermute | solution.py:532
  21.9 22.7 %collective-permute-start.12 = (bf16[4,320,128]{2,1,0:T(8,128)(2,1)}, bf16[4,320,128]{2,1,0:T(8,128)(2,1)}, u32[]{:S(2)}, u32[]{:S(2)}) collective-permute-start(bf16[4,320,128]{2,1,0:T(8,128)(2,1)} %get-tuple-element.47), channel_id=1, source_target_pairs={{0,12},{4,8},{8,4},{12,0},{16,20},{20,16},{24,28},{28,24},{1,13},{... | collective-permute-start | bytes 983048 | tf_op jit(solution)/shard_map/ppermute | solution.py:532
  31.7 10.6 %copy-start.4 = (bf16[5,32,128]{2,1,0:T(8,128)(2,1)S(1)}, bf16[5,32,128]{2,1,0:T(8,128)(2,1)}, u32[]{:S(2)}) copy-start(bf16[5,32,128]{2,1,0:T(8,128)(2,1)} %get-tuple-element.34) | copy-start | bytes 122884
  42.3 15.7 %collective-permute-start.8 = (bf16[4,320,128]{2,1,0:T(8,128)(2,1)}, bf16[4,320,128]{2,1,0:T(8,128)(2,1)}, u32[]{:S(2)}, u32[]{:S(2)}) collective-permute-start(bf16[4,320,128]{2,1,0:T(8,128)(2,1)} %get-tuple-element.39), channel_id=1, source_target_pairs={{0,4},{4,0},{8,12},{12,8},{16,20},{20,16},{24,28},{28,24},{1,5},{5... | collective-permute-start | bytes 983048 | tf_op jit(solution)/shard_map/ppermute | solution.py:532
  42.4 13.8 %collective-permute-start.4 = (bf16[5,32,128]{2,1,0:T(8,128)(2,1)S(1)}, bf16[5,32,128]{2,1,0:T(8,128)(2,1)S(1)}, u32[]{:S(2)}, u32[]{:S(2)}) collective-permute-start(bf16[5,32,128]{2,1,0:T(8,128)(2,1)S(1)} %copy-done.4), channel_id=1, source_target_pairs={{17,16},{18,17},{19,18},{21,20},{22,21},{23,22},{25,24},{26,25},{2... | collective-permute-start | bytes 122888 | tf_op jit(solution)/shard_map/ppermute | solution.py:539
  43.0 13.6 %collective-permute-start.5 = (bf16[5,32,128]{2,1,0:T(8,128)(2,1)S(1)}, bf16[5,32,128]{2,1,0:T(8,128)(2,1)S(1)}, u32[]{:S(2)}, u32[]{:S(2)}) collective-permute-start(bf16[5,32,128]{2,1,0:T(8,128)(2,1)S(1)} %copy-done.4), channel_id=1, source_target_pairs={{16,17},{17,18},{18,19},{20,21},{21,22},{22,23},{24,25},{25,26},{2... | collective-permute-start | bytes 122888 | tf_op jit(solution)/shard_map/ppermute | solution.py:540
  54.4 15.1 %collective-permute-start.13 = (bf16[4,320,128]{2,1,0:T(8,128)(2,1)}, bf16[4,320,128]{2,1,0:T(8,128)(2,1)}, u32[]{:S(2)}, u32[]{:S(2)}) collective-permute-start(bf16[4,320,128]{2,1,0:T(8,128)(2,1)} %get-tuple-element.49), channel_id=1, source_target_pairs={{0,4},{4,0},{8,12},{12,8},{16,20},{20,16},{24,28},{28,24},{1,5},{5... | collective-permute-start | bytes 983048 | tf_op jit(solution)/shard_map/ppermute | solution.py:532
  54.9 13.5 %collective-permute-start.9 = (bf16[4,320,128]{2,1,0:T(8,128)(2,1)}, bf16[4,320,128]{2,1,0:T(8,128)(2,1)}, u32[]{:S(2)}, u32[]{:S(2)}) collective-permute-start(bf16[4,320,128]{2,1,0:T(8,128)(2,1)} %get-tuple-element.40), channel_id=1, source_target_pairs={{0,12},{4,8},{8,4},{12,0},{16,28},{20,24},{24,20},{28,16},{1,13},{... | collective-permute-start | bytes 983048 | tf_op jit(solution)/shard_map/ppermute | solution.py:532
  56.2 12.2 %copy-start = (bf16[5,32,128]{2,1,0:T(8,128)(2,1)}, bf16[5,32,128]{2,1,0:T(8,128)(2,1)S(1)}, u32[]{:S(2)}) copy-start(bf16[5,32,128]{2,1,0:T(8,128)(2,1)S(1)} %collective-permute-done.4.east_in) | copy-start | bytes 122884
  56.2 16.5 %collective-permute-start.15 = (bf16[4,320,128]{2,1,0:T(8,128)(2,1)}, bf16[4,320,128]{2,1,0:T(8,128)(2,1)}, u32[]{:S(2)}, u32[]{:S(2)}) collective-permute-start(bf16[4,320,128]{2,1,0:T(8,128)(2,1)} %get-tuple-element.51), channel_id=1, source_target_pairs={{0,8},{4,12},{8,0},{12,4},{16,20},{20,16},{24,28},{28,24},{1,9},{5... | collective-permute-start | bytes 983048 | tf_op jit(solution)/shard_map/ppermute | solution.py:532
  56.6 11.8 %copy-start.1 = (bf16[5,32,128]{2,1,0:T(8,128)(2,1)}, bf16[5,32,128]{2,1,0:T(8,128)(2,1)S(1)}, u32[]{:S(2)}) copy-start(bf16[5,32,128]{2,1,0:T(8,128)(2,1)S(1)} %collective-permute-done.5.west_in) | copy-start | bytes 122884
  56.6 22.4 %collective-permute-start.16 = (bf16[4,320,128]{2,1,0:T(8,128)(2,1)}, bf16[4,320,128]{2,1,0:T(8,128)(2,1)}, u32[]{:S(2)}, u32[]{:S(2)}) collective-permute-start(bf16[4,320,128]{2,1,0:T(8,128)(2,1)} %get-tuple-element.52), channel_id=1, source_target_pairs={{0,12},{4,8},{8,4},{12,0},{16,20},{20,16},{24,28},{28,24},{1,13},{... | collective-permute-start | bytes 983048 | tf_op jit(solution)/shard_map/ppermute | solution.py:532
  58.0 28.3 %collective-permute-start.14 = (bf16[4,320,128]{2,1,0:T(8,128)(2,1)}, bf16[4,320,128]{2,1,0:T(8,128)(2,1)}, u32[]{:S(2)}, u32[]{:S(2)}) collective-permute-start(bf16[4,320,128]{2,1,0:T(8,128)(2,1)} %get-tuple-element.50), channel_id=1, source_target_pairs={{0,8},{4,12},{8,0},{12,4},{16,20},{20,16},{24,28},{28,24},{1,9},{5... | collective-permute-start | bytes 983048 | tf_op jit(solution)/shard_map/ppermute | solution.py:532
